TPU v7x, 32 devices: a whole 2x2x4 slice. The times are simulated.
32 devices in a mesh: dp: 8 (over z, x), mp: 4 (over y, core).
Axes of the slice: x: 2, y: 2, z: 4, core: 2. Of those that a mesh axis runs over, the one named last changes fastest.
Arguments:
- passage_embeds: bfloat16 [18432, 1024], P('dp'), may hold values from -24 to 24
- passage_lengths: int32 [8, 24], P('dp'), may hold values from 1 to 192, 2304 in all within a row
- slot_question: int32 [8, 24], P('dp'), may hold values from 0 to 7, as said below
- answer_states: bfloat16 [1024, 1024], P('dp'), may hold values from -24 to 24
- w_enc_attn: bfloat16 [4, 1024, 1024], P(None, 'dp', 'mp'), may hold values from -0.1875 to 0.1875
- w_enc_ff: bfloat16 [3, 1024, 2816], P(None, 'dp', 'mp'), may hold values from -0.1875 to 0.1875
- w_cross_kv: bfloat16 [2, 1024, 1024], P(None, 'dp', 'mp'), may hold values from -0.1875 to 0.1875
- w_dec_attn: bfloat16 [6, 1024, 1024], P(None, 'dp', 'mp'), may hold values from -0.1875 to 0.1875
- w_dec_ff: bfloat16 [3, 1024, 2816], P(None, 'dp', 'mp'), may hold values from -0.1875 to 0.1875
Outputs:
- decoded: bfloat16 [1024, 1024], P('dp', 'mp')
Inputs may be any that keep to these rules, and one draw needn't show every extreme that they name: `passage_lengths`: each row sums to 2304. `slot_question`: each question is named by exactly 24 slots; a row names one question at most 3 times, and every row names some question that many times.
All inputs are finite; a program needn't handle non-finite values.
Results may differ from a plain program's by a relative error of at most 0.025.
Values may be sent and summed in bfloat16 or wider, within the bound.
No kernel may reach another device: no remote copies, remote signals or barrier semaphores. Data moves between devices by JAX's collectives and lax.ppermute only.
A program may use at most 128 MiB of HBM per device.

v0:
```python
import functools
import math

import jax
import jax.numpy as jnp
from jax import lax
from jax.experimental import pallas as pl
from jax.experimental.pallas import tpu as pltpu
from jax.sharding import PartitionSpec as P


HEAD_DIM = 64
EPSILON = 1e-06
LANES = 128
HALO = 256
F32 = jnp.float32
BF16 = jnp.bfloat16
EXP2_FACTOR = 3.0 / math.sqrt(HEAD_DIM) * math.log2(math.e)


def rms_normed(values):
    values = values.astype(F32)
    factor = lax.rsqrt(jnp.mean(values * values, axis=-1, keepdims=True) + EPSILON)
    return (values * factor).astype(BF16)


def dot(left, right):
    return jnp.dot(left, right, preferred_element_type=F32)


def dot_t(left, right):
    return lax.dot_general(left, right, (((1,), (1,)), ((), ())), preferred_element_type=F32)


def swap_x(value):
    count = lax.axis_size("dp")
    return lax.ppermute(value, "dp", [(i, i ^ 1) for i in range(count)])


def swap_core(value):
    count = lax.axis_size("mp")
    return lax.ppermute(value, "mp", [(i, i ^ 1) for i in range(count)])


def z_groups():
    count = lax.axis_size("dp")
    return [[i + x for i in range(0, count, 2)] for x in range(2)]


def y_groups():
    count = lax.axis_size("mp")
    return [[i + c for i in range(0, count, 2)] for c in range(2)]


def gather_z(value, axis):
    return lax.all_gather(value, "dp", axis_index_groups=z_groups(), axis=axis, tiled=True)


def few_z():
    return lax.axis_size("dp") // 2 <= 4


def swap_z(value, step):
    count = lax.axis_size("dp")
    return lax.ppermute(value, "dp", [(i, i ^ (2 * step)) for i in range(count)])


def z_place(index):
    return index ^ (lax.axis_index("dp") // 2) if few_z() else index


def pieces_z(value, axis):
    if not few_z():
        return [gather_z(value, axis)]
    return [value] + [swap_z(value, step) for step in range(1, lax.axis_size("dp") // 2)]


def meet(*values):
    return lax.optimization_barrier(values)


def swap_y(value):
    return lax.ppermute(value, "mp", [(i, i ^ 2) for i in range(4)])


def gather_y(value):
    size_y = lax.axis_size("mp") // 2
    if size_y == 1:
        return [value]
    if size_y == 2:
        return [value, swap_y(value)]
    pieces = lax.all_gather(value, "mp", axis_index_groups=y_groups(), axis=0)
    return [pieces[i] for i in range(size_y)]


def scatter_y_sum(value):
    size_y = lax.axis_size("mp") // 2
    y = lax.axis_index("mp") // 2
    if size_y == 2:
        other = swap_y(lax.dynamic_index_in_dim(value, 1 - y, 0, keepdims=False))
        own = lax.dynamic_index_in_dim(value, y, 0, keepdims=False)
        return own.astype(F32) + other.astype(F32)
    summed = lax.psum_scatter(
        value, "mp", scatter_dimension=0, axis_index_groups=y_groups(), tiled=True
    )
    return summed[0].astype(F32)


def join_kernel(*refs, axis):
    *pieces, out, sems = refs
    begin, copies = 0, []
    for index, piece in enumerate(pieces):
        size = piece.shape[axis]
        where = (slice(None),) * axis + (pl.ds(begin, size),)
        copies.append(pltpu.make_async_copy(piece, out.at[where], sems.at[index]))
        copies[-1].start()
        begin += size
    for copy in copies:
        copy.wait()


def join(pieces, axis):
    if len(pieces) == 1:
        return pieces[0]
    shape = list(pieces[0].shape)
    shape[axis] = sum(piece.shape[axis] for piece in pieces)
    if axis == len(shape) - 1 and pieces[0].shape[axis] % LANES:
        return jnp.concatenate(pieces, axis=axis)
    return pl.pallas_call(
        functools.partial(join_kernel, axis=axis),
        out_shape=jax.ShapeDtypeStruct(tuple(shape), pieces[0].dtype),
        in_specs=[pl.BlockSpec(memory_space=pl.ANY)] * len(pieces),
        out_specs=pl.BlockSpec(memory_space=pltpu.VMEM),
        scratch_shapes=[pltpu.SemaphoreType.DMA((len(pieces),))],
        cost_estimate=pl.CostEstimate(
            flops=0, bytes_accessed=4 * math.prod(shape), transcendentals=0
        ),
        name="join",
    )(*pieces)


def pick(value, index, count, axis):
    width = value.shape[axis] // count
    return lax.dynamic_slice_in_dim(value, index * width, width, axis)


def in_order(first, own, other, axis):
    return jnp.concatenate(
        [jnp.where(first, own, other), jnp.where(first, other, own)], axis=axis
    )


def spread_near(block):
    return (swap_x(block), swap_y(block)) if lax.axis_size("mp") == 4 else (swap_x(block),)


def spread_far(near, axis):
    if len(near) == 1:
        return ()
    side, over = near
    cut = far_cut(side.shape[axis])
    first = lax.slice_in_dim(over, 0, cut, axis=axis)
    second = lax.slice_in_dim(side, cut, side.shape[axis], axis=axis)
    return (swap_x(first), swap_y(second))


def far_cut(size):
    return -(-(size // 2) // LANES) * LANES


def attn_pieces(block, near, far):
    own = [block, near[0]]
    if len(near) == 1:
        return [own] + [[piece] for piece in gather_y(join(own, 1))[1:]]
    return [own, [near[1], *far]]


def ff_piece(block, near, far):
    own = [(block, 0, block.shape[1]), (near[0], 0, block.shape[1])]
    if len(near) == 1:
        rest = [gather_y(half)[1:] for half in (block, near[0])]
        return [own] + [
            [(mine, 0, mine.shape[1]), (theirs, 0, theirs.shape[1])]
            for mine, theirs in zip(*rest)
        ]
    return [own, [(near[1], 0, near[1].shape[1]), (far[0], 0, near[1].shape[1])]]


def ff_kernel(*refs, chunks, done, last):
    refs, out_ref = refs[:-1], refs[-1]
    if chunks:
        half = refs[0].shape[1] // 2
        mine, theirs = refs[0][:, :half], refs[0][:, half:]

    def weight(place):
        index, lead, begin, count = place
        return refs[index][lead, begin : begin + count, :]

    sums = [None, None]

    def add(hidden, places):
        for k in range(2):
            term = dot(hidden, weight(places[k]))
            sums[k] = term if sums[k] is None else sums[k] + term

    for index, places in done:
        add(refs[index][...], places)
    for gate, up, *down in chunks:
        gated = dot_t(mine, weight(gate[0])) + dot_t(theirs, weight(gate[1]))
        linear = dot_t(mine, weight(up[0])) + dot_t(theirs, weight(up[1]))
        hidden = (jax.nn.gelu(gated, approximate=True) * linear).astype(BF16)
        if last:
            add(hidden, down[0])
        else:
            out_ref[...] = hidden
    if last:
        half = sums[0].shape[1]
        out_ref[:, :half] = sums[0].astype(BF16)
        out_ref[:, half:] = sums[1].astype(BF16)


def ff(h, chunks, done, last):
    rows = h.shape[0]
    block = math.gcd(rows, 384)
    operands, specs, seen = [], [], {}
    if chunks:
        operands.append(h)
        specs.append(pl.BlockSpec((block, h.shape[1]), lambda i: (i, 0)))

    def place(lead, entry):
        array, begin, count, *more = entry
        lead += sum(more)
        if id(array) not in seen:
            seen[id(array)] = len(operands)
            operands.append(array)
            specs.append(pl.BlockSpec(array.shape, lambda i: (0, 0, 0)))
        return seen[id(array)], lead, begin, count

    def places(lead, entries):
        return tuple(place(lead, entry) for entry in entries)

    before = []
    for hidden, (lead, entries) in done:
        operands.append(hidden)
        specs.append(pl.BlockSpec((block, hidden.shape[1]), lambda i: (i, 0)))
        index = len(operands) - 1
        before.append((index, places(lead, entries)))
    plan = [tuple(places(lead, entries) for lead, entries in chunk) for chunk in chunks]
    width = h.shape[1] if last else chunks[0][0][1][0][2]
    flops = 2 * rows * h.shape[1] * sum(
        [(3 if last else 2) * c[0][1][0][2] for c in chunks] + [d[0].shape[1] for d in done]
    )
    return pl.pallas_call(
        functools.partial(ff_kernel, chunks=plan, done=before, last=last),
        out_shape=jax.ShapeDtypeStruct((rows, width), BF16),
        grid=(rows // block,),
        in_specs=specs,
        out_specs=pl.BlockSpec((block, width), lambda i: (i, 0)),
        compiler_params=pltpu.CompilerParams(vmem_limit_bytes=48 * 2**20),
        cost_estimate=pl.CostEstimate(
            flops=flops, bytes_accessed=2 * rows * (h.shape[1] + width), transcendentals=0
        ),
        name="ff",
    )(*operands)


def row_block(rows, most):
    return max(n for n in range(16, most + 1, 16) if rows % n == 0)


def resident(array):
    return pl.BlockSpec(array.shape, lambda i: (0,) * array.ndim)


def out_kernel(*refs, plan, index):
    *refs, out_ref = refs
    cuts = {0, out_ref.shape[1]}
    for _, parts in plan:
        begin = 0
        for part in parts:
            begin += refs[part].shape[1]
            cuts.add(begin)
    cuts = sorted(cuts)
    for low, high in zip(cuts, cuts[1:]):
        total = None
        for mix, parts in plan:
            begin = 0
            for part in parts:
                size = refs[part].shape[1]
                if begin <= low < begin + size:
                    term = dot_t(refs[mix][...], refs[part][index, low - begin : high - begin, :])
                    total = term if total is None else total + term
                begin += size
        out_ref[:, low:high] = total.astype(BF16)


def out_project(mixes, pieces, index):
    rows = mixes[0].shape[0]
    features = sum(part.shape[1] for part in pieces[0])
    block = math.gcd(rows, 384)
    operands, specs, plan = [], [], []
    for mix, parts in zip(mixes, pieces):
        plan.append((len(operands), range(len(operands) + 1, len(operands) + 1 + len(parts))))
        operands += [mix, *parts]
        specs.append(pl.BlockSpec((block, mix.shape[1]), lambda i: (i, 0)))
        specs += [resident(part) for part in parts]
    return pl.pallas_call(
        functools.partial(out_kernel, plan=plan, index=index),
        out_shape=jax.ShapeDtypeStruct((rows, features), BF16),
        grid=(rows // block,),
        in_specs=specs,
        out_specs=pl.BlockSpec((block, features), lambda i: (i, 0)),
        compiler_params=pltpu.CompilerParams(vmem_limit_bytes=32 * 2**20),
        cost_estimate=pl.CostEstimate(
            flops=2 * rows * features * sum(m.shape[1] for m in mixes),
            bytes_accessed=4 * rows * features,
            transcendentals=0,
        ),
        name="out_project",
    )(*operands)


def prepare_kernel(begin_ref, order_ref, x_ref, o_ref, raw_ref, *, width):
    rows, features = o_ref.shape
    chunk = 32

    def step(r, carry):
        begin = pl.multiple_of(r * chunk, chunk)
        blocks, total = [], 0.0
        for p in range(features // width):
            source = pl.multiple_of(order_ref[p] * width, width)
            block = x_ref[pl.ds(begin, chunk), pl.ds(source, width)]
            raw_ref[pl.ds(begin, chunk), p * width : (p + 1) * width] = block
            block = block.astype(F32)
            blocks.append(block)
            total = total + block * block
        mean = jnp.sum(total, axis=1, keepdims=True) / features
        factor = lax.rsqrt(mean + EPSILON)
        for p, block in enumerate(blocks):
            o_ref[pl.ds(begin, chunk), p * width : (p + 1) * width] = (block * factor).astype(BF16)
        return carry

    lax.fori_loop(0, rows // chunk, step, 0, unroll=2)


def prepare(values, begin, rows, order, width):
    features = values.shape[1]
    block = LANES
    spec = pl.BlockSpec((block, features), lambda i, first, order: (i, 0))
    return pl.pallas_call(
        functools.partial(prepare_kernel, width=width),
        out_shape=[jax.ShapeDtypeStruct((rows, features), BF16)] * 2,
        grid_spec=pltpu.PrefetchScalarGridSpec(
            num_scalar_prefetch=2,
            grid=(rows // block,),
            in_specs=[
                pl.BlockSpec((block, features), lambda i, first, order: (first[0] + i, 0))
            ],
            out_specs=[spec, spec],
        ),
        cost_estimate=pl.CostEstimate(
            flops=4 * rows * features, bytes_accessed=6 * rows * features, transcendentals=0
        ),
        name="prepare",
    )((begin // block).reshape(1), order, values)


def own_first(values, x, width, place):
    size_z = values.shape[1] // (2 * width)
    blocks = [
        lax.dynamic_slice_in_dim(values, (2 * place(z) + index) * width, width, 1)
        for index in (x, 1 - x)
        for z in range(size_z)
    ]
    return jnp.concatenate(blocks, axis=1)


def two_heads(q, k, v, allowed, low_half):
    zero, one = jnp.zeros_like(v), jnp.ones_like(v)
    keys = jnp.concatenate([jnp.where(low_half, k, zero), jnp.where(low_half, zero, k)], axis=0)
    vals = jnp.concatenate(
        [
            jnp.concatenate([jnp.where(low_half, v, zero), jnp.where(low_half, one, zero)], axis=1),
            jnp.concatenate([jnp.where(low_half, zero, v), jnp.where(low_half, zero, one)], axis=1),
        ],
        axis=0,
    )
    weights = jnp.exp2(dot_t(q, keys) * EXP2_FACTOR)
    count = k.shape[0]
    if count % LANES == 0:
        weights = jnp.where(jnp.concatenate([allowed, allowed], axis=1), weights, 0.0)
        return dot(weights.astype(BF16), vals)
    first = jnp.where(allowed, weights[:, :count], 0.0).astype(BF16)
    second = jnp.where(allowed, weights[:, count:], 0.0).astype(BF16)
    return dot(first, vals[:count]) + dot(second, vals[count:])


def enc_attention_kernel(
    low_ref, high_ref, first_ref, seg_q_ref, seg_k_ref, q_ref, k_ref, v_ref, o_ref, acc, *, rows
):
    width = q_ref.shape[1]
    first_row = first_ref[0]
    key_rows = seg_k_ref.shape[2]
    last = seg_k_ref.shape[0] - 1
    low_half = lax.broadcasted_iota(jnp.int32, (1, LANES), 1) < HEAD_DIM

    def block(i, carry):
        begin = pl.multiple_of(i * rows, rows)
        query_begin = pl.multiple_of(first_row + i * rows, math.gcd(rows, LANES))
        low, high = low_ref[i], high_ref[i]
        acc[...] = jnp.zeros_like(acc)

        def step(j, inner):
            for p in range(width // LANES):
                columns = slice(p * LANES, (p + 1) * LANES)
                total = None
                for u in range(2):
                    index = low + 2 * j + u
                    clipped = jnp.minimum(index, last)
                    offset = pl.multiple_of(clipped * key_rows, key_rows)
                    seg_k = jnp.where(index < high, seg_k_ref[clipped], -1)
                    allowed = seg_q_ref[pl.ds(begin, rows), :key_rows] == seg_k
                    part = two_heads(
                        q_ref[pl.ds(query_begin, rows), columns],
                        k_ref[pl.ds(offset, key_rows), columns],
                        v_ref[pl.ds(offset, key_rows), columns],
                        allowed,
                        low_half,
                    )
                    total = part if total is None else total + part
                acc[p] += total
            return inner

        lax.fori_loop(0, (high - low + 1) // 2, step, 0)
        for p in range(width // LANES):
            sums = acc[p]
            o_ref[pl.ds(begin, rows), p * LANES : (p + 1) * LANES] = (
                sums[:, :LANES] / sums[:, LANES:]
            ).astype(BF16)
        return carry

    lax.fori_loop(0, low_ref.shape[0], block, 0)


def project_into(h_ref, weights, mats, outs):
    rows = h_ref.shape[0]
    begin = pl.multiple_of(pl.program_id(0) * rows, rows)
    for mat, out in zip(mats, outs):
        total, column = None, 0
        for weight in weights:
            size = weight.shape[1]
            term = dot(h_ref[:, column : column + size], weight[mat])
            total = term if total is None else total + term
            column += size
        out[pl.ds(begin, rows), :] = total.astype(BF16)


def enc_block_kernel(low_ref, high_ref, first_ref, seg_q_ref, seg_k_ref, h_ref, *refs, rows):
    *weights, o_ref, q, k, v, acc = refs
    project_into(h_ref, weights, (0, 1, 2), (q, k, v))

    @pl.when(pl.program_id(0) == pl.num_programs(0) - 1)
    def _():
        enc_attention_kernel(
            low_ref, high_ref, first_ref, seg_q_ref, seg_k_ref, q, k, v, o_ref, acc, rows=rows
        )


def enc_block(low, high, first_row, seg_q, seg_k, h, weights):
    rows, window, width = seg_q.shape[0], h.shape[0], weights[0].shape[2]
    query_rows = rows // low.shape[0]
    step = row_block(window, 400)
    smem = pl.BlockSpec(memory_space=pltpu.SMEM)
    return pl.pallas_call(
        functools.partial(enc_block_kernel, rows=query_rows),
        out_shape=jax.ShapeDtypeStruct((rows, width), BF16),
        grid=(window // step,),
        in_specs=[smem] * 3
        + [resident(seg_q), resident(seg_k)]
        + [pl.BlockSpec((step, h.shape[1]), lambda i: (i, 0))]
        + [resident(weight) for weight in weights],
        out_specs=pl.BlockSpec((rows, width), lambda i: (0, 0)),
        scratch_shapes=[pltpu.VMEM((window, width), BF16)] * 3
        + [pltpu.VMEM((width // LANES, query_rows, 2 * LANES), F32)],
        compiler_params=pltpu.CompilerParams(vmem_limit_bytes=32 * 2**20),
        cost_estimate=pl.CostEstimate(
            flops=window * width * (6 * h.shape[1] + 3072),
            bytes_accessed=2 * h.size,
            transcendentals=0,
        ),
        name="enc_block",
    )(low, high, first_row.reshape(1), seg_q, seg_k, h, *weights)


def cross_block_kernel(begin_ref, end_ref, question_ref, x_ref, *refs, key_rows, count):
    queries, (h_ref, *weights, o_ref, k, v, acc) = refs[:count], refs[count:]
    project_into(h_ref, weights, (0, 1), (k, v))

    @pl.when(pl.program_id(0) == pl.num_programs(0) - 1)
    def _():
        cross_kernel(
            begin_ref, end_ref, question_ref, x_ref, queries, k, v, o_ref, acc, key_rows=key_rows
        )


def cross_kernel(
    begin_ref, end_ref, question_ref, x_ref, queries, k_ref, v_ref, o_ref, acc, *, key_rows
):
    questions, length = queries[0].shape[:2]
    pairs = k_ref.shape[1] // LANES
    own_x = x_ref[0]

    def pair_of(question, p):
        if len(queries) == 1:
            return queries[0][question, :, p * LANES : (p + 1) * LANES]
        own, other = (ref[question] for ref in queries)
        return jnp.where(own_x == p, own, other)

    last = k_ref.shape[0] // key_rows - 1
    acc[...] = jnp.zeros_like(acc)
    low_half = lax.broadcasted_iota(jnp.int32, (1, LANES), 1) < HEAD_DIM

    def passage(s, carry):
        begin, end, question = begin_ref[s], end_ref[s], question_ref[s]
        first = begin // key_rows

        def step(j, inner):
            for p in range(pairs):
                columns = slice(p * LANES, (p + 1) * LANES)
                total = None
                query = pair_of(question, p)
                for u in range(2):
                    index = first + 2 * j + u
                    offset = pl.multiple_of(jnp.minimum(index, last) * key_rows, key_rows)
                    position = index * key_rows + lax.broadcasted_iota(
                        jnp.int32, (1, key_rows), 1
                    )
                    allowed = (position >= begin) & (position < end)
                    part = two_heads(
                        query,
                        k_ref[pl.ds(offset, key_rows), columns],
                        v_ref[pl.ds(offset, key_rows), columns],
                        allowed,
                        low_half,
                    )
                    total = part if total is None else total + part
                acc[question, p] += total
            return inner

        blocks = (end + key_rows - 1) // key_rows - first
        lax.fori_loop(0, jnp.where(end > begin, (blocks + 1) // 2, 0), step, 0)
        return carry

    lax.fori_loop(0, begin_ref.shape[0], passage, 0)
    eye = lax.broadcasted_iota(jnp.int32, (length, LANES), 0) == lax.broadcasted_iota(
        jnp.int32, (length, LANES), 1
    )
    extra = o_ref.shape[2] - 2 * length
    place = lax.broadcasted_iota(jnp.int32, (extra, LANES), 0)

    def finish(z, carry):
        for p in range(pairs):
            totals = jnp.zeros((extra, LANES), F32)
            for x in range(2):
                sums = acc[2 * z + x, p]
                o_ref[z, p, x * length : (x + 1) * length, :] = sums[:, :LANES].astype(BF16)
                total = sums[:, LANES:]
                turned = pltpu.roll(total, HEAD_DIM, 1)
                for h in range(2):
                    own = jnp.where(low_half, total, turned) if h == 0 else jnp.where(low_half, turned, total)
                    row = jnp.sum(jnp.where(eye, own, 0.0), axis=0, keepdims=True)
                    totals = jnp.where(place == 2 * x + h, row, totals)
            o_ref[z, p, 2 * length :, :] = totals.astype(BF16)
        return carry

    lax.fori_loop(0, questions // 2, finish, 0)


def cross_block(begin, end, question, x, queries, h, weights):
    questions, length = queries[0].shape[:2]
    rows, width = h.shape[0], weights[0].shape[2]
    key_rows = math.gcd(rows, LANES)
    pairs = width // LANES
    step = row_block(rows, 400)
    smem = pl.BlockSpec(memory_space=pltpu.SMEM)
    shape = (questions // 2, pairs, 2 * length + 16, LANES)
    return pl.pallas_call(
        functools.partial(cross_block_kernel, key_rows=key_rows, count=len(queries)),
        out_shape=jax.ShapeDtypeStruct(shape, BF16),
        grid=(rows // step,),
        in_specs=[smem] * 4
        + [resident(q) for q in queries]
        + [pl.BlockSpec((step, h.shape[1]), lambda i: (i, 0))]
        + [resident(weight) for weight in weights],
        out_specs=pl.BlockSpec(shape, lambda i: (0, 0, 0, 0)),
        scratch_shapes=[pltpu.VMEM((rows, width), BF16)] * 2
        + [pltpu.VMEM((questions, pairs, length, 2 * LANES), F32)],
        compiler_params=pltpu.CompilerParams(vmem_limit_bytes=40 * 2**20),
        cost_estimate=pl.CostEstimate(
            flops=rows * width * (4 * h.shape[1] + 2048), bytes_accessed=2 * h.size, transcendentals=0
        ),
        name="cross_block",
    )(begin, end, question, x.reshape(1), *queries, h, *weights)


def by_column_x(sums, length):
    size_z, pairs = sums.shape[:2]
    if pairs == 2:
        return sums
    num = sums[:, 0, : 2 * length].reshape(size_z, 2 * length, 2, HEAD_DIM).transpose(0, 2, 1, 3)
    tot = sums[:, 0, 2 * length : 2 * length + 4].reshape(size_z, 2, 2, length)
    tot = tot.transpose(0, 2, 1, 3).reshape(size_z, 2, -1, HEAD_DIM)
    return jnp.concatenate([num, tot], axis=2)


def self_kernel(x_ref, w_ref, o_ref, *, questions):
    rows, width = x_ref.shape[0], w_ref.shape[2]
    length = rows // questions
    q, k, v = (dot(x_ref[...], w_ref[i]).astype(BF16) for i in range(3))
    low_half = lax.broadcasted_iota(jnp.int32, (1, LANES), 1) < HEAD_DIM
    causal = lax.broadcasted_iota(jnp.int32, (length, length), 1) <= lax.broadcasted_iota(
        jnp.int32, (length, length), 0
    )
    for question in range(questions):
        own = slice(question * length, (question + 1) * length)
        total = None
        for p in range(width // LANES):
            columns = slice(p * LANES, (p + 1) * LANES)
            sums = two_heads(
                q[own, columns], k[own, columns], v[own, columns], causal, low_half
            )
            mixture = (sums[:, :LANES] / sums[:, LANES:]).astype(BF16)
            term = dot_t(mixture, w_ref[3, :, columns])
            total = term if total is None else total + term
        o_ref[own, :] = total.astype(BF16)


def self_block(x, weights, questions):
    if weights.shape[2] % LANES:
        q, k, v = (dot(x, weights[i]).astype(BF16) for i in range(3))
        return dot_t(self_attention(q, k, v, questions), weights[3]).astype(BF16)
    vmem = pl.BlockSpec(memory_space=pltpu.VMEM)
    return pl.pallas_call(
        functools.partial(self_kernel, questions=questions),
        out_shape=jax.ShapeDtypeStruct((x.shape[0], weights.shape[1]), BF16),
        in_specs=[vmem, vmem],
        out_specs=vmem,
        cost_estimate=pl.CostEstimate(
            flops=8 * x.size * weights.shape[2], bytes_accessed=2 * weights.size, transcendentals=0
        ),
        name="self_block",
    )(x, weights)


def self_attention(q, k, v, questions):
    rows, width = q.shape
    heads = width // HEAD_DIM
    length = rows // questions
    shape = (questions, length, heads, HEAD_DIM)
    q, k, v = q.reshape(shape), k.reshape(shape), v.reshape(shape)
    scores = jnp.einsum("oqhc,okhc->ohqk", q, k, preferred_element_type=F32)
    causal = jnp.arange(length)[None, :] <= jnp.arange(length)[:, None]
    weights = jnp.where(causal, jnp.exp(scores * (3.0 / math.sqrt(HEAD_DIM))), 0.0)
    totals = jnp.sum(weights, axis=3)
    mixture = jnp.einsum("ohqk,okhc->oqhc", weights.astype(BF16), v, preferred_element_type=F32)
    return (mixture / jnp.transpose(totals, (0, 2, 1))[..., None]).astype(BF16).reshape(rows, width)


def core_rows_sum(partial, core):
    other = swap_core(pick(partial, 1 - core, 2, 0).astype(BF16))
    return pick(partial, core, 2, 0).astype(F32) + other.astype(F32)


def flip(values):
    half = values.shape[1] // 2
    return jnp.concatenate([values[:, half:], values[:, :half]], axis=1)


def answer_start(partial, core, size_y):
    mine = core_rows_sum(partial, core).astype(BF16)
    if size_y != 2:
        return (mine, swap_x(mine))
    rows = mine.shape[0] // 2
    top, bottom = mine[:rows], mine[rows:]
    return top, bottom, swap_x(top), swap_y(bottom)


def answer_turn(values):
    if len(values) == 2:
        mine, other = values
        mine = mine.astype(F32) + flip(other).astype(F32)
        return (lax.psum(mine, "mp", axis_index_groups=y_groups()),)
    top, bottom, other_top, other_bottom = values
    top = (top.astype(F32) + flip(other_top).astype(F32)).astype(BF16)
    bottom = (bottom.astype(F32) + other_bottom.astype(F32)).astype(BF16)
    return top, bottom, swap_y(top), swap_x(bottom)


def answer_end(values):
    if len(values) == 1:
        return values[0]
    top, bottom, other_top, other_bottom = values
    top = top.astype(F32) + other_top.astype(F32)
    bottom = bottom.astype(F32) + flip(other_bottom).astype(F32)
    return jnp.concatenate([top, bottom], axis=0)


def both_cores(values, core):
    return in_order(core == 0, values, swap_core(values), 0)


def local(
    passage_embeds,
    passage_lengths,
    slot_question,
    answer_states,
    w_enc_attn,
    w_enc_ff,
    w_cross_kv,
    w_dec_attn,
    w_dec_ff,
):
    dp_count, mp_count = lax.axis_size("dp"), lax.axis_size("mp")
    size_z, size_y = dp_count // 2, mp_count // 2
    x = lax.axis_index("dp") % 2
    core = lax.axis_index("mp") % 2
    y = lax.axis_index("mp") // 2
    features = passage_embeds.shape[1]
    shard_width = features // dp_count

    length = answer_states.shape[0]
    enc_ff_t = w_enc_ff.transpose(0, 2, 1)
    dec_ff_t = w_dec_ff.transpose(0, 2, 1)
    attn_z = pieces_z(w_enc_attn, 1)
    dec_attn_pair = (pick(w_dec_attn, x, 2, 2), swap_x(pick(w_dec_attn, 1 - x, 2, 2)))
    dec_ff_pair = (pick(dec_ff_t, x, 2, 1), swap_x(pick(dec_ff_t, 1 - x, 2, 1)))
    other_answers = swap_x(answer_states)
    (
        attn_z,
        dec_attn_pair,
        dec_ff_pair,
        other_answers,
        enc_ff_t,
        passage_embeds,
        passage_lengths,
        answer_states,
    ) = meet(
        attn_z,
        dec_attn_pair,
        dec_ff_pair,
        other_answers,
        enc_ff_t,
        passage_embeds,
        passage_lengths,
        answer_states,
    )
    attn_block = join(attn_z, 1)
    attn_near = spread_near(attn_block)
    gate_z = pieces_z(enc_ff_t[0:1], 2)
    row_count = passage_embeds.shape[0]
    rows = row_count // size_y
    sides = min(size_y - 1, 2)
    window = min(row_count, rows + sides * HALO)
    row_begin = y * rows
    window_begin = jnp.clip(row_begin - HALO, 0, row_count - window)
    lengths = passage_lengths[0]
    ends = jnp.cumsum(lengths)
    starts = ends - lengths
    positions = window_begin + jnp.arange(window, dtype=jnp.int32)
    segment = jnp.sum((positions[:, None] >= ends[None, :]).astype(jnp.int32), axis=1)
    query_block = math.gcd(rows, 3 * LANES)
    key_block = math.gcd(window, LANES)
    block_first = row_begin + jnp.arange(rows // query_block, dtype=jnp.int32) * query_block
    block_last = block_first + query_block - 1
    inside_first = jnp.max(
        jnp.where(starts[None, :] <= block_first[:, None], starts[None, :], 0), axis=1
    )
    inside_last = jnp.min(
        jnp.where(ends[None, :] > block_last[:, None], ends[None, :], row_count), axis=1
    )
    low = (inside_first - window_begin) // key_block
    high = (inside_last - window_begin + key_block - 1) // key_block
    seg_k = segment.reshape(window // key_block, 1, key_block)
    seg_q = jnp.broadcast_to(
        lax.dynamic_slice_in_dim(segment, row_begin - window_begin, rows, 0)[:, None],
        (rows, LANES),
    )

    own_begin = row_begin - window_begin
    if shard_width % LANES == 0 and window % LANES == 0 and rows % LANES == 0:
        order = jnp.stack([2 * z_place(z) + i for i in (x, 1 - x) for z in range(size_z)])
        normed, embeds = prepare(passage_embeds, window_begin, window, order, shard_width)
    else:
        embeds = lax.dynamic_slice_in_dim(passage_embeds, window_begin, window, 0)
        embeds = own_first(embeds, x, shard_width, z_place)
        normed = rms_normed(embeds)
    answers = in_order(x == 0, answer_states, other_answers, 0)
    answers = own_first(answers, x, shard_width, z_place)
    answer_normed = rms_normed(answers)

    attn_near, gate_z, normed, enc_ff_t = meet(attn_near, gate_z, normed, enc_ff_t)
    attn_far = spread_far(attn_near, 1)
    gate_block = join(gate_z, 2)
    gate_near = spread_near(gate_block)
    rest_z = pieces_z(enc_ff_t[1:3], 2)

    def attend(parts):
        return enc_block(low, high, own_begin, seg_q, seg_k, normed, parts)

    if size_y == 2:
        mixes = [attend([attn_block, attn_near[0]])]
        attn_far, gate_near, rest_z, mixes, w_cross_kv, dec_attn_pair = meet(
            attn_far, gate_near, rest_z, mixes, w_cross_kv, dec_attn_pair
        )
    rest_block = join(rest_z, 2)
    rest_near = spread_near(rest_block)
    dec_attn_z = pieces_z(jnp.stack(dec_attn_pair, axis=1), 2)
    attn_weights = attn_pieces(attn_block, attn_near, attn_far)
    if size_y == 2:
        mixes.append(attend(attn_weights[1]))
    else:
        mixes = [attend(parts) for parts in attn_weights]
    partial = out_project(mixes, attn_weights, 3)
    own_embeds = lax.dynamic_slice_in_dim(embeds, own_begin + core * (rows // 2), rows // 2, 0)
    first_rows = (own_embeds.astype(F32) + core_rows_sum(partial, core)).astype(BF16)
    normed = both_cores(rms_normed(first_rows), core)

    rest_near, dec_attn_z, normed, w_cross_kv, dec_ff_pair = meet(
        rest_near, dec_attn_z, normed, w_cross_kv, dec_ff_pair
    )
    gate_far = (swap_x(gate_near[1]),) if size_y == 2 else ()
    rest_far = (swap_y(rest_near[0]),) if size_y == 2 else ()
    cross_z = pieces_z(w_cross_kv, 1)
    dec_ff_z = pieces_z(jnp.stack(dec_ff_pair, axis=1).reshape(-1, *dec_ff_pair[0].shape[1:]), 2)
    dec_attn = join(dec_attn_z, 2).reshape(w_dec_attn.shape[0], features, -1)
    self_partial = self_block(answer_normed, dec_attn, 2)
    exchange = answer_start(self_partial, core, size_y)
    gate_own = ff_piece(gate_block, gate_near, gate_near)[0]
    rest_own = ff_piece(rest_block, rest_near, rest_near)[0]
    hidden = [ff(normed, [((0, gate_own), (0, rest_own))], [], False)]

    gate_far, rest_far, hidden, exchange, cross_z = meet(
        gate_far, rest_far, hidden, exchange, cross_z
    )
    gate_ff = ff_piece(gate_block, gate_near, gate_far)
    exchange = answer_turn(exchange)
    cross_block_z = join(cross_z, 1)
    cross_near = spread_near(cross_block_z)
    rest_ff = ff_piece(rest_block, rest_near, rest_far)
    for gate, rest in zip(gate_ff[1:], rest_ff[1:]):
        hidden.append(ff(normed, [((0, gate), (0, rest))], [], False))

    hidden, exchange, cross_near = meet(hidden, exchange, cross_near)
    cross_far = spread_far(cross_near, 1)
    first_answer = (pick(answers, core, 2, 0).astype(F32) + answer_end(exchange)).astype(BF16)
    cross_q = dot(both_cores(rms_normed(first_answer), core), dec_attn[4]).astype(BF16)
    cross_q = pieces_z(cross_q, 0)
    partial = ff(normed, [], [(h, (1, rest)) for h, rest in zip(hidden, rest_ff)], True)

    cross_q, cross_far, partial = meet(cross_q, cross_far, partial)
    cross_q = join(cross_q, 0)
    shape = (dp_count, length, -1)
    if size_y == 2 and cross_q.shape[1] == LANES:
        side, over = swap_x(cross_q), swap_y(cross_q)
        half = cross_q.shape[0] // 2
        far = jnp.concatenate([swap_x(over[:half]), swap_y(side[half:])], axis=0)
        cross_q = [[q.reshape(shape) for q in pair] for pair in ((cross_q, side), (over, far))]
    else:
        cross_q = in_order(x == 0, cross_q, swap_x(cross_q), 1)
        cross_q = [[q] for q in gather_y(cross_q.reshape(shape))]
    second_rows = (first_rows.astype(F32) + core_rows_sum(partial, core)).astype(BF16)
    normed = both_cores(rms_normed(second_rows), core)
    cross_weights = attn_pieces(cross_block_z, cross_near, cross_far)

    begin = jnp.clip(starts - row_begin, 0, rows)
    end = jnp.clip(ends - row_begin, 0, rows)
    questions = slot_question[0]
    questions = z_place(questions // 2) * 2 + questions % 2
    cross_q, normed, dec_ff = meet(cross_q, normed, join(dec_ff_z, 2))

    def answer_part(index):
        sums = cross_block(
            begin, end, questions, x, cross_q[index], normed, cross_weights[index]
        )
        return by_column_x(sums, length)

    if size_y == 2:
        other = answer_part(1)
        other = swap_y(other)
        own = answer_part(0)
        summed = own.astype(F32) + other.astype(F32)
    else:
        packed = [answer_part(index) for index in range(size_y)]
        summed = packed[0].astype(F32) if size_y == 1 else scatter_y_sum(jnp.stack(packed))
    other = swap_x(lax.dynamic_index_in_dim(summed, 1 - x, 1, keepdims=False).astype(BF16))
    summed = lax.dynamic_index_in_dim(summed, x, 1, keepdims=False) + other.astype(F32)
    if few_z():
        own = summed[0]
        for step in range(1, size_z):
            own = own + swap_z(summed[step].astype(BF16), step).astype(F32)
        summed = own
    else:
        exchanged = lax.all_to_all(
            summed.astype(BF16), "dp", 0, 0, axis_index_groups=z_groups(), tiled=True
        )
        summed = jnp.sum(exchanged.astype(F32), axis=0)
    width = summed.shape[1]
    heads = width // HEAD_DIM
    num = summed[: 2 * length].reshape(2, length, heads, HEAD_DIM)
    tot = summed[2 * length : 2 * length + 2 * heads * length // width]
    tot = tot.reshape(2, heads, length).transpose(0, 2, 1)
    cross_mix = (num / tot[..., None]).astype(BF16).reshape(2 * length, width)
    exchange = answer_start(dot_t(cross_mix, dec_attn[5]).astype(BF16), core, size_y)
    second_sum = answer_end(answer_turn(exchange))
    second_answer = (first_answer.astype(F32) + second_sum).astype(BF16)
    answer_normed = both_cores(rms_normed(second_answer), core)
    halves = [(dec_ff, 0, dec_ff.shape[1], half) for half in range(2)]
    partial = ff(answer_normed, [((0, halves), (2, halves), (4, halves))], [], True)
    per_column = size_z // mp_count
    columns = per_column * shard_width

    def columns_of(values, indices):
        values = values.reshape(values.shape[0], 2, size_z, shard_width)
        blocks = [
            lax.dynamic_index_in_dim(values, z_place(index * per_column + i), 2, keepdims=False)
            for index in indices
            for i in range(per_column)
        ]
        return jnp.stack(blocks, axis=2).reshape(values.shape[0], 2, len(indices), columns)

    other = swap_core(columns_of(partial, [2 * i + 1 - core for i in range(size_y)]))
    mine = columns_of(partial, [2 * i + core for i in range(size_y)])
    mine = mine.astype(F32) + other.astype(F32)
    other = swap_x(pick(mine, 1 - x, 2, 0).astype(BF16)).astype(F32)
    mine = pick(mine, x, 2, 0) + jnp.stack([other[:, 1], other[:, 0]], axis=1)
    summed = scatter_y_sum(mine.astype(BF16).transpose(2, 0, 1, 3))
    residual = pick(both_cores(second_answer, core), x, 2, 0)
    residual = columns_of(residual, [lax.axis_index("mp")])[:, :, 0]
    result = (residual.astype(F32) + summed).astype(BF16)
    result = result.reshape(length, 2, per_column, 1, shard_width)
    return in_order(x == 0, result[:, 0], result[:, 1], 2).reshape(length, 2 * columns)


def solution(mesh):
    in_specs = (
        P("dp", None),
        P("dp", None),
        P("dp", None),
        P("dp", None),
        P(None, "dp", "mp"),
        P(None, "dp", "mp"),
        P(None, "dp", "mp"),
        P(None, "dp", "mp"),
        P(None, "dp", "mp"),
    )
    out_specs = P("dp", "mp")

    return jax.shard_map(local, mesh=mesh, in_specs=in_specs, out_specs=out_specs, check_vma=False)
```

profile of v0, /device:TPU:0, one launch (start us, length us, event | category | flops | bytes accessed | tf_op | source)
XLA Modules:
  0.0 385.6 jit_solution(17335059695906907563)
XLA Ops:
  1.8 3.0 collective-permute-start.3
  8.6 2.6 collective-permute-start.1
  14.8 6.3 %collective-permute-done.5 = bf16[128,1024]{1,0:T(8,128)(2,1)S(1)} collective-permute-done((bf16[128,1024]{1,0:T(8,128)(2,1)S(1)}, bf16[128,1024]{1,0:T(8,128)(2,1)S(1)}, u32[]{:S(2)}, u32[]{:S(2)}) %collective-permute-start.5) | collective-permute-done | bytes 262176 | tf_op jit(solution)/shard_map/ppermute | solution.py:37
  21.1 4.4 %collective-permute-done.1.refs_2_ = bf16[4,128,256]{2,1,0:T(8,128)(2,1)S(1)} collective-permute-done((bf16[4,128,256]{2,1,0:T(8,128)(2,1)S(1)}, bf16[4,128,256]{2,1,0:T(8,128)(2,1)S(1)}, u32[]{:S(2)}, u32[]{:S(2)}) %collective-permute-start.1) | collective-permute-done | bytes 262176 | tf_op jit(solution)/shard_map/ppermute | solution.py:65
  25.4 3.7 collective-permute-done.2.refs_3_
  29.9 2.3 join.7.refs_0_.refs_1_
  35.0 2.5 collective-permute-start.10
  37.6 4.7 %collective-permute-start.9 = (bf16[1,704,128]{2,1,0:T(8,128)(2,1)S(1)}, bf16[1,704,128]{2,1,0:T(8,128)(2,1)S(1)}, u32[]{:S(2)}, u32[]{:S(2)}) collective-permute-start(bf16[1,704,128]{2,1,0:T(8,128)(2,1)S(1)} %slice.101.refs_0_), channel_id=1, source_target_pairs={{0,16},{4,20},{8,24},{12,28},{16,0},{20,4},{24,8},{28,12},{1,17},{... | collective-permute-start | bytes 540680 | tf_op jit(solution)/shard_map/ppermute | solution.py:65
  43.0 9.9 %prepare.1 = (bf16[1408,1024]{1,0:T(8,128)(2,1)}, bf16[1408,1024]{1,0:T(8,128)(2,1)}) custom-call(s32[1]{0:T(128)} %bitcast.3.begin_ref, s32[8]{0:T(128)} %stack.66.order_ref, bf16[2304,1024]{1,0:T(8,128)(2,1)} %x_ref), custom_call_target="tpu_custom_call" | custom-call | flops 5767168 | bytes 8650752 | tf_op jit(solution)/shard_map/prepare/pallas_call | solution.py:350
  57.7 2.5 collective-permute-start.17
  60.2 6.5 %collective-permute-start.16 = (bf16[2,704,128]{2,1,0:T(8,128)(2,1)}, bf16[2,704,128]{2,1,0:T(8,128)(2,1)}, u32[]{:S(2)}, u32[]{:S(2)}) collective-permute-start(bf16[2,704,128]{2,1,0:T(8,128)(2,1)} %slice.104.refs_0_), channel_id=1, source_target_pairs={{0,16},{4,20},{8,24},{12,28},{16,0},{20,4},{24,8},{28,12},{1,17},{... | collective-permute-start | bytes 1081352 | tf_op jit(solution)/shard_map/ppermute | solution.py:65
  66.9 2.1 join.8.refs_1_
  75.0 15.4 %collective-permute-done.16.refs_2_ = bf16[2,704,128]{2,1,0:T(8,128)(2,1)} collective-permute-done((bf16[2,704,128]{2,1,0:T(8,128)(2,1)}, bf16[2,704,128]{2,1,0:T(8,128)(2,1)}, u32[]{:S(2)}, u32[]{:S(2)}) %collective-permute-start.16) | collective-permute-done | bytes 360480 | tf_op jit(solution)/shard_map/ppermute | solution.py:65
  92.7 10.2 %enc_block.2.refs_0_ = bf16[1152,256]{1,0:T(8,128)(2,1)S(1)} custom-call(s32[3]{0:T(128)S(1)} %get-tuple-element.215.low_ref, s32[3]{0:T(128)S(1)} %get-tuple-element.214.high_ref, s32[1]{0:T(128)} %bitcast.14.first_ref, s32[1152,128]{1,0:T(8,128)S(1)} %broadcast_in_dim.20.seg_q_ref, s32[11,1,128]{2,1,0:T(1,128)S(1)} %reshape.179.seg_k_ref, ...), custom_call_target="tpu_custom_call" | custom-call | flops 3321888768 | bytes 2883584 | tf_op jit(solution)/shard_map/enc_block/pallas_call | solution.py:474
  103.0 10.9 %enc_block.3.refs_3_ = bf16[1152,256]{1,0:T(8,128)(2,1)S(1)} custom-call(s32[3]{0:T(128)S(1)} %get-tuple-element.215.low_ref, s32[3]{0:T(128)S(1)} %get-tuple-element.214.high_ref, s32[1]{0:T(128)} %bitcast.14.first_ref, s32[1152,128]{1,0:T(8,128)S(1)} %broadcast_in_dim.20.seg_q_ref, s32[11,1,128]{2,1,0:T(1,128)S(1)} %reshape.179.seg_k_ref, ...), custom_call_target="tpu_custom_call" | custom-call | flops 3321888768 | bytes 2883584 | tf_op jit(solution)/shard_map/enc_block/pallas_call | solution.py:474
  115.1 3.1 out_project.1
  118.5 2.9 collective-permute-done.24
  121.3 2.4 fusion.2
  125.4 2.5 join.9.refs_3_.refs_1_
  127.9 2.3 collective-permute-start.20
  140.0 6.1 %collective-permute-done.23.refs_3_ = bf16[6,2,128,128]{3,2,1,0:T(8,128)(2,1)S(1)} collective-permute-done((bf16[6,2,128,128]{3,2,1,0:T(8,128)(2,1)S(1)}, bf16[6,2,128,128]{3,2,1,0:T(8,128)(2,1)S(1)}, u32[]{:S(2)}, u32[]{:S(2)}) %collective-permute-start.23) | collective-permute-done | bytes 393248 | tf_op jit(solution)/shard_map/ppermute | solution.py:65
  146.1 23.7 %collective-permute-done.22.refs_2_ = bf16[6,2,128,128]{3,2,1,0:T(8,128)(2,1)S(1)} collective-permute-done((bf16[6,2,128,128]{3,2,1,0:T(8,128)(2,1)S(1)}, bf16[6,2,128,128]{3,2,1,0:T(8,128)(2,1)S(1)}, u32[]{:S(2)}, u32[]{:S(2)}) %collective-permute-start.22) | collective-permute-done | bytes 393248 | tf_op jit(solution)/shard_map/ppermute | solution.py:65
  172.8 2.6 join.10
  175.4 3.7 self_block.1
  183.6 2.3 collective-permute-start.30
  186.9 12.1 %collective-permute-done.18.refs_2_ = bf16[1,704,512]{2,1,0:T(8,128)(2,1)S(1)} collective-permute-done((bf16[1,704,512]{2,1,0:T(8,128)(2,1)}, bf16[1,704,512]{2,1,0:T(8,128)(2,1)S(1)}, u32[]{:S(2)}, u32[]{:S(2)}) %collective-permute-start.18) | collective-permute-done | bytes 720928 | tf_op jit(solution)/shard_map/ppermute | solution.py:37
  202.1 6.1 %ff.4.refs_0_ = bf16[1152,704]{1,0:T(8,128)(2,1)S(1)} custom-call(bf16[1152,1024]{1,0:T(8,128)(2,1)} %pad_maximum_fusion.refs_0_, bf16[1,704,512]{2,1,0:T(8,128)(2,1)S(1)} %copy-done.7, bf16[1,704,512]{2,1,0:T(8,128)(2,1)} %collective-permute-done.13.refs_2_, bf16[2,704,512]{2,1,0:T(8,128)(2,1)S(1)} %copy-done.6, ...), custom_call_target="tpu_custom_call" | custom-call | flops 3321888768 | bytes 3981312 | tf_op jit(solution)/shard_map/ff/pallas_call | solution.py:253
  217.6 6.2 %ff.5.refs_3_ = bf16[1152,704]{1,0:T(8,128)(2,1)S(1)} custom-call(bf16[1152,1024]{1,0:T(8,128)(2,1)} %pad_maximum_fusion.refs_0_, bf16[1,704,512]{2,1,0:T(8,128)(2,1)} %collective-permute-done.14.refs_1_, bf16[1,704,512]{2,1,0:T(8,128)(2,1)S(1)} %copy-done.21, bf16[2,704,512]{2,1,0:T(8,128)(2,1)S(1)} %copy-done.19, ...), custom_call_target="tpu_custom_call" | custom-call | flops 3321888768 | bytes 3981312 | tf_op jit(solution)/shard_map/ff/pallas_call | solution.py:253
  223.8 4.4 %collective-permute-done.33 = bf16[64,1024]{1,0:T(8,128)(2,1)S(1)} collective-permute-done((bf16[64,1024]{1,0:T(8,128)(2,1)S(1)}, bf16[64,1024]{1,0:T(8,128)(2,1)S(1)}, u32[]{:S(2)}, u32[]{:S(2)}) %collective-permute-start.33) | collective-permute-done | bytes 131104 | tf_op jit(solution)/shard_map/ppermute | solution.py:83
  235.9 3.1 collective-permute-start.38
  239.0 7.4 %ff.6 = bf16[1152,1024]{1,0:T(8,128)(2,1)} custom-call(bf16[1152,704]{1,0:T(8,128)(2,1)} %copy-done.26, bf16[2,704,512]{2,1,0:T(8,128)(2,1)S(1)} %copy-done.6, bf16[2,704,512]{2,1,0:T(8,128)(2,1)} %collective-permute-done.19.refs_4_.refs_2_, bf16[1152,704]{1,0:T(8,128)(2,1)} %copy-done.27, bf16[2,704,512]{2,1,0:T(8,128)(2,1)S(1)} %copy-done.19, ...), custom_call_target="tpu_custom_call" | custom-call | flops 3321888768 | bytes 4718592 | tf_op jit(solution)/shard_map/ff/pallas_call | solution.py:253
  248.2 2.8 collective-permute-done.47
  259.3 2.3 collective-permute-start.49
  261.6 4.6 %collective-permute-done.44 = bf16[1024,128]{1,0:T(8,128)(2,1)S(1)} collective-permute-done((bf16[1024,128]{1,0:T(8,128)(2,1)}, bf16[1024,128]{1,0:T(8,128)(2,1)S(1)}, u32[]{:S(2)}, u32[]{:S(2)}) %collective-permute-start.44) | collective-permute-done | bytes 262176 | tf_op jit(solution)/shard_map/ppermute | solution.py:83
  267.7 6.2 %collective-permute-done.43 = bf16[1024,128]{1,0:T(8,128)(2,1)S(1)} collective-permute-done((bf16[1024,128]{1,0:T(8,128)(2,1)}, bf16[1024,128]{1,0:T(8,128)(2,1)S(1)}, u32[]{:S(2)}, u32[]{:S(2)}) %collective-permute-start.43) | collective-permute-done | bytes 262176 | tf_op jit(solution)/shard_map/ppermute | solution.py:37
  276.8 26.7 %collective-permute-done.50.refs_2_ = bf16[6,352,128]{2,1,0:T(8,128)(2,1)S(1)} collective-permute-done((bf16[6,352,128]{2,1,0:T(8,128)(2,1)S(1)}, bf16[6,352,128]{2,1,0:T(8,128)(2,1)S(1)}, u32[]{:S(2)}, u32[]{:S(2)}) %collective-permute-start.50) | collective-permute-done | bytes 540704 | tf_op jit(solution)/shard_map/ppermute | solution.py:65
  304.3 2.9 join.13.refs_1_
  310.3 10.3 %cross_block.3 = bf16[4,2,272,128]{3,2,1,0:T(8,128)(2,1)} custom-call(s32[24]{0:T(128)S(1)} %get-tuple-element.213.begin_ref, s32[24]{0:T(128)S(1)} %get-tuple-element.212.end_ref, s32[24]{0:T(128)S(1)} %fusion.43.question_ref, s32[1]{0:T(128)} %bitcast.20.x_ref, bf16[8,128,128]{2,1,0:T(8,128)(2,1)S(1)} %bitcast.104, bf16[8,128,128]{2,1,0:T(8,128)(2,1)S(1)} %bitcast.102, ...), custom_call_target="tpu_custom_call" | custom-call | flops 1811939328 | bytes 2359296 | tf_op jit(solution)/shard_map/cross_block/pallas_call | solution.py:587
  322.9 9.5 %cross_block.2 = bf16[4,2,272,128]{3,2,1,0:T(8,128)(2,1)S(1)} custom-call(s32[24]{0:T(128)S(1)} %get-tuple-element.213.begin_ref, s32[24]{0:T(128)S(1)} %get-tuple-element.212.end_ref, s32[24]{0:T(128)S(1)} %fusion.43.question_ref, s32[1]{0:T(128)} %bitcast.20.x_ref, bf16[8,128,128]{2,1,0:T(8,128)(2,1)S(1)} %bitcast.101, bf16[8,128,128]{2,1,0:T(8,128)(2,1)S(1)} %bitcast.103, ...), custom_call_target="tpu_custom_call" | custom-call | flops 1811939328 | bytes 2359296 | tf_op jit(solution)/shard_map/cross_block/pallas_call | solution.py:587
  332.5 2.6 collective-permute-done.52
  337.4 6.1 %collective-permute-done.53 = bf16[4,272,128]{2,1,0:T(8,128)(2,1)S(1)} collective-permute-done((bf16[4,272,128]{2,1,0:T(8,128)(2,1)S(1)}, bf16[4,272,128]{2,1,0:T(8,128)(2,1)S(1)}, u32[]{:S(2)}, u32[]{:S(2)}) %collective-permute-start.53) | collective-permute-done | bytes 278560 | tf_op jit(solution)/shard_map/ppermute | solution.py:37
  343.7 2.4 collective-permute-start.56
  349.9 2.1 collective-permute-done.55
  356.9 3.0 collective-permute-done.58
  363.3 2.5 collective-permute-done.61
  369.0 2.3 ff.7
  376.0 4.4 %collective-permute-done.65 = bf16[128,2,2,128]{0,3,1,2:T(8,128)(2,1)S(1)} collective-permute-done((bf16[128,2,2,128]{0,3,1,2:T(8,128)(2,1)S(1)}, bf16[128,2,2,128]{0,3,1,2:T(8,128)(2,1)S(1)}, u32[]{:S(2)}, u32[]{:S(2)}) %collective-permute-start.65) | collective-permute-done | bytes 131104 | tf_op jit(solution)/shard_map/ppermute | solution.py:37
  382.3 2.5 collective-permute-done.66
  (355 shorter events, 113.2 us)
Async XLA Ops:
  1.8 11.0 %collective-permute-start.3 = (bf16[6,128,128]{2,1,0:T(8,128)(2,1)S(1)}, bf16[6,128,128]{2,1,0:T(8,128)(2,1)}, u32[]{:S(2)}, u32[]{:S(2)}) collective-permute-start(bf16[6,128,128]{2,1,0:T(8,128)(2,1)S(1)} %get-tuple-element.189), channel_id=1, source_target_pairs={{0,4},{4,0},{8,12},{12,8},{16,20},{20,16},{24,28},{28,24},{1,5},{5... | collective-permute-start | bytes 589832 | tf_op jit(solution)/shard_map/ppermute | solution.py:37
  6.6 22.5 %collective-permute-start.4 = (bf16[3,352,128]{2,1,0:T(8,128)(2,1)S(1)}, bf16[3,352,128]{2,1,0:T(8,128)(2,1)S(1)}, u32[]{:S(2)}, u32[]{:S(2)}) collective-permute-start(bf16[3,352,128]{2,1,0:T(8,128)(2,1)S(1)} %get-tuple-element.175), channel_id=1, source_target_pairs={{0,4},{4,0},{8,12},{12,8},{16,20},{20,16},{24,28},{28,24},{1,5},{5... | collective-permute-start | bytes 811016 | tf_op jit(solution)/shard_map/ppermute | solution.py:37
  6.6 14.5 %collective-permute-start.5 = (bf16[128,1024]{1,0:T(8,128)(2,1)S(1)}, bf16[128,1024]{1,0:T(8,128)(2,1)S(1)}, u32[]{:S(2)}, u32[]{:S(2)}) collective-permute-start(bf16[128,1024]{1,0:T(8,128)(2,1)S(1)} %copy-done.48), channel_id=1, source_target_pairs={{0,4},{4,0},{8,12},{12,8},{16,20},{20,16},{24,28},{28,24},{1,5},{5... | collective-permute-start | bytes 786440 | tf_op jit(solution)/shard_map/ppermute | solution.py:37
  8.6 16.8 %collective-permute-start.1 = (bf16[4,128,256]{2,1,0:T(8,128)(2,1)S(1)}, bf16[4,128,256]{2,1,0:T(8,128)(2,1)S(1)}, u32[]{:S(2)}, u32[]{:S(2)}) collective-permute-start(bf16[4,128,256]{2,1,0:T(8,128)(2,1)S(1)} %copy-done.52), channel_id=1, source_target_pairs={{0,16},{4,20},{8,24},{12,28},{16,0},{20,4},{24,8},{28,12},{1,17},{... | collective-permute-start | bytes 786440 | tf_op jit(solution)/shard_map/ppermute | solution.py:65
  11.2 14.2 %collective-permute-start = (bf16[4,128,256]{2,1,0:T(8,128)(2,1)S(1)}, bf16[4,128,256]{2,1,0:T(8,128)(2,1)S(1)}, u32[]{:S(2)}, u32[]{:S(2)}) collective-permute-start(bf16[4,128,256]{2,1,0:T(8,128)(2,1)S(1)} %copy-done.52), channel_id=1, source_target_pairs={{0,8},{4,12},{8,0},{12,4},{16,24},{20,28},{24,16},{28,20},{1,9},{5... | collective-permute-start | bytes 786440 | tf_op jit(solution)/shard_map/ppermute | solution.py:65
  12.8 16.3 %collective-permute-start.2 = (bf16[4,128,256]{2,1,0:T(8,128)(2,1)S(1)}, bf16[4,128,256]{2,1,0:T(8,128)(2,1)S(1)}, u32[]{:S(2)}, u32[]{:S(2)}) collective-permute-start(bf16[4,128,256]{2,1,0:T(8,128)(2,1)S(1)} %copy-done.52), channel_id=1, source_target_pairs={{0,24},{4,28},{8,16},{12,20},{16,8},{20,12},{24,0},{28,4},{1,25},{... | collective-permute-start | bytes 786440 | tf_op jit(solution)/shard_map/ppermute | solution.py:65
  32.2 23.5 %collective-permute-start.7 = (bf16[4,512,256]{2,1,0:T(8,128)(2,1)}, bf16[4,512,256]{2,1,0:T(8,128)(2,1)S(1)}, u32[]{:S(2)}, u32[]{:S(2)}) collective-permute-start(bf16[4,512,256]{2,1,0:T(8,128)(2,1)} %join.7.refs_0_.refs_1_), channel_id=1, source_target_pairs={{0,2},{1,3},{2,0},{3,1},{4,6},{5,7},{6,4},{7,5},{8,10},{9,11},{10,... | collective-permute-start | bytes 3145736 | tf_op jit(solution)/shard_map/ppermute | solution.py:83
  33.8 23.1 %collective-permute-start.6 = (bf16[4,512,256]{2,1,0:T(8,128)(2,1)}, bf16[4,512,256]{2,1,0:T(8,128)(2,1)S(1)}, u32[]{:S(2)}, u32[]{:S(2)}) collective-permute-start(bf16[4,512,256]{2,1,0:T(8,128)(2,1)} %join.7.refs_0_.refs_1_), channel_id=1, source_target_pairs={{0,4},{4,0},{8,12},{12,8},{16,20},{20,16},{24,28},{28,24},{1,5},{5... | collective-permute-start | bytes 3145736 | tf_op jit(solution)/shard_map/ppermute | solution.py:37
  35.0 17.9 %collective-permute-start.10 = (bf16[1,704,128]{2,1,0:T(8,128)(2,1)S(1)}, bf16[1,704,128]{2,1,0:T(8,128)(2,1)S(1)}, u32[]{:S(2)}, u32[]{:S(2)}) collective-permute-start(bf16[1,704,128]{2,1,0:T(8,128)(2,1)S(1)} %slice.101.refs_0_), channel_id=1, source_target_pairs={{0,24},{4,28},{8,16},{12,20},{16,8},{20,12},{24,0},{28,4},{1,25},{... | collective-permute-start | bytes 540680 | tf_op jit(solution)/shard_map/ppermute | solution.py:65
  37.6 16.5 %collective-permute-start.9 = (bf16[1,704,128]{2,1,0:T(8,128)(2,1)S(1)}, bf16[1,704,128]{2,1,0:T(8,128)(2,1)S(1)}, u32[]{:S(2)}, u32[]{:S(2)}) collective-permute-start(bf16[1,704,128]{2,1,0:T(8,128)(2,1)S(1)} %slice.101.refs_0_), channel_id=1, source_target_pairs={{0,16},{4,20},{8,24},{12,28},{16,0},{20,4},{24,8},{28,12},{1,17},{... | collective-permute-start | bytes 540680 | tf_op jit(solution)/shard_map/ppermute | solution.py:65
  42.2 11.8 %collective-permute-start.8 = (bf16[1,704,128]{2,1,0:T(8,128)(2,1)S(1)}, bf16[1,704,128]{2,1,0:T(8,128)(2,1)S(1)}, u32[]{:S(2)}, u32[]{:S(2)}) collective-permute-start(bf16[1,704,128]{2,1,0:T(8,128)(2,1)S(1)} %slice.101.refs_0_), channel_id=1, source_target_pairs={{0,8},{4,12},{8,0},{12,4},{16,24},{20,28},{24,16},{28,20},{1,9},{5... | collective-permute-start | bytes 540680 | tf_op jit(solution)/shard_map/ppermute | solution.py:65
  57.7 15.8 %collective-permute-start.17 = (bf16[2,704,128]{2,1,0:T(8,128)(2,1)}, bf16[2,704,128]{2,1,0:T(8,128)(2,1)}, u32[]{:S(2)}, u32[]{:S(2)}) collective-permute-start(bf16[2,704,128]{2,1,0:T(8,128)(2,1)} %slice.104.refs_0_), channel_id=1, source_target_pairs={{0,24},{4,28},{8,16},{12,20},{16,8},{20,12},{24,0},{28,4},{1,25},{... | collective-permute-start | bytes 1081352 | tf_op jit(solution)/shard_map/ppermute | solution.py:65
  60.2 30.2 %collective-permute-start.16 = (bf16[2,704,128]{2,1,0:T(8,128)(2,1)}, bf16[2,704,128]{2,1,0:T(8,128)(2,1)}, u32[]{:S(2)}, u32[]{:S(2)}) collective-permute-start(bf16[2,704,128]{2,1,0:T(8,128)(2,1)} %slice.104.refs_0_), channel_id=1, source_target_pairs={{0,16},{4,20},{8,24},{12,28},{16,0},{20,4},{24,8},{28,12},{1,17},{... | collective-permute-start | bytes 1081352 | tf_op jit(solution)/shard_map/ppermute | solution.py:65
  69.0 33.9 %collective-permute-start.14 = (bf16[1,704,512]{2,1,0:T(8,128)(2,1)}, bf16[1,704,512]{2,1,0:T(8,128)(2,1)}, u32[]{:S(2)}, u32[]{:S(2)}) collective-permute-start(bf16[1,704,512]{2,1,0:T(8,128)(2,1)} %join.8.refs_1_), channel_id=1, source_target_pairs={{0,2},{1,3},{2,0},{3,1},{4,6},{5,7},{6,4},{7,5},{8,10},{9,11},{10,... | collective-permute-start | bytes 2162696 | tf_op jit(solution)/shard_map/ppermute | solution.py:83
  69.8 33.2 %collective-permute-start.13 = (bf16[1,704,512]{2,1,0:T(8,128)(2,1)}, bf16[1,704,512]{2,1,0:T(8,128)(2,1)}, u32[]{:S(2)}, u32[]{:S(2)}) collective-permute-start(bf16[1,704,512]{2,1,0:T(8,128)(2,1)} %join.8.refs_1_), channel_id=1, source_target_pairs={{0,4},{4,0},{8,12},{12,8},{16,20},{20,16},{24,28},{28,24},{1,5},{5... | collective-permute-start | bytes 2162696 | tf_op jit(solution)/shard_map/ppermute | solution.py:37
  72.2 30.7 %collective-permute-start.12 = (bf16[4,256,256]{2,1,0:T(8,128)(2,1)}, bf16[4,256,256]{2,1,0:T(8,128)(2,1)}, u32[]{:S(2)}, u32[]{:S(2)}) collective-permute-start(bf16[4,256,256]{2,1,0:T(8,128)(2,1)} %slice.103), channel_id=1, source_target_pairs={{0,2},{1,3},{2,0},{3,1},{4,6},{5,7},{6,4},{7,5},{8,10},{9,11},{10,... | collective-permute-start | bytes 1572872 | tf_op jit(solution)/shard_map/ppermute | solution.py:83
  73.5 29.4 %collective-permute-start.11 = (bf16[4,256,256]{2,1,0:T(8,128)(2,1)}, bf16[4,256,256]{2,1,0:T(8,128)(2,1)}, u32[]{:S(2)}, u32[]{:S(2)}) collective-permute-start(bf16[4,256,256]{2,1,0:T(8,128)(2,1)} %slice.102), channel_id=1, source_target_pairs={{0,4},{4,0},{8,12},{12,8},{16,20},{20,16},{24,28},{28,24},{1,5},{5... | collective-permute-start | bytes 1572872 | tf_op jit(solution)/shard_map/ppermute | solution.py:37
  90.5 12.4 %collective-permute-start.15 = (bf16[2,704,128]{2,1,0:T(8,128)(2,1)}, bf16[2,704,128]{2,1,0:T(8,128)(2,1)}, u32[]{:S(2)}, u32[]{:S(2)}) collective-permute-start(bf16[2,704,128]{2,1,0:T(8,128)(2,1)} %slice.104.refs_0_), channel_id=1, source_target_pairs={{0,8},{4,12},{8,0},{12,4},{16,24},{20,28},{24,16},{28,20},{1,9},{5... | collective-permute-start | bytes 1081352 | tf_op jit(solution)/shard_map/ppermute | solution.py:65
  124.1 11.5 %collective-permute-start.25 = (bf16[576,1024]{1,0:T(8,128)(2,1)S(1)}, bf16[576,1024]{1,0:T(8,128)(2,1)}, u32[]{:S(2)}, u32[]{:S(2)}) collective-permute-start(bf16[576,1024]{1,0:T(8,128)(2,1)S(1)} %fusion.3), channel_id=1, source_target_pairs={{0,1},{1,0},{2,3},{3,2},{4,5},{5,4},{6,7},{7,6},{8,9},{9,8},{10,11... | collective-permute-start | bytes 3538952 | tf_op jit(solution)/shard_map/ppermute | solution.py:42
  127.9 41.9 %collective-permute-start.20 = (bf16[2,704,512]{2,1,0:T(8,128)(2,1)}, bf16[2,704,512]{2,1,0:T(8,128)(2,1)S(1)}, u32[]{:S(2)}, u32[]{:S(2)}) collective-permute-start(bf16[2,704,512]{2,1,0:T(8,128)(2,1)} %join.9.refs_3_.refs_1_), channel_id=1, source_target_pairs={{0,2},{1,3},{2,0},{3,1},{4,6},{5,7},{6,4},{7,5},{8,10},{9,11},{10,... | collective-permute-start | bytes 4325384 | tf_op jit(solution)/shard_map/ppermute | solution.py:83
  130.2 40.8 %collective-permute-start.19 = (bf16[2,704,512]{2,1,0:T(8,128)(2,1)}, bf16[2,704,512]{2,1,0:T(8,128)(2,1)}, u32[]{:S(2)}, u32[]{:S(2)}) collective-permute-start(bf16[2,704,512]{2,1,0:T(8,128)(2,1)} %join.9.refs_3_.refs_1_), channel_id=1, source_target_pairs={{0,4},{4,0},{8,12},{12,8},{16,20},{20,16},{24,28},{28,24},{1,5},{5... | collective-permute-start | bytes 4325384 | tf_op jit(solution)/shard_map/ppermute | solution.py:37
  132.1 13.9 %collective-permute-start.23 = (bf16[6,2,128,128]{3,2,1,0:T(8,128)(2,1)S(1)}, bf16[6,2,128,128]{3,2,1,0:T(8,128)(2,1)S(1)}, u32[]{:S(2)}, u32[]{:S(2)}) collective-permute-start(bf16[6,2,128,128]{3,2,1,0:T(8,128)(2,1)S(1)} %pad_maximum_fusion.4.refs_0_), channel_id=1, source_target_pairs={{0,24},{4,28},{8,16},{12,20},{16,8},{20,12},{24,0},{28,4},{1,25},{... | collective-permute-start | bytes 1179656 | tf_op jit(solution)/shard_map/ppermute | solution.py:65
  133.7 36.1 %collective-permute-start.22 = (bf16[6,2,128,128]{3,2,1,0:T(8,128)(2,1)S(1)}, bf16[6,2,128,128]{3,2,1,0:T(8,128)(2,1)S(1)}, u32[]{:S(2)}, u32[]{:S(2)}) collective-permute-start(bf16[6,2,128,128]{3,2,1,0:T(8,128)(2,1)S(1)} %pad_maximum_fusion.4.refs_0_), channel_id=1, source_target_pairs={{0,16},{4,20},{8,24},{12,28},{16,0},{20,4},{24,8},{28,12},{1,17},{... | collective-permute-start | bytes 1179656 | tf_op jit(solution)/shard_map/ppermute | solution.py:65
  135.6 34.1 %collective-permute-start.21 = (bf16[6,2,128,128]{3,2,1,0:T(8,128)(2,1)S(1)}, bf16[6,2,128,128]{3,2,1,0:T(8,128)(2,1)S(1)}, u32[]{:S(2)}, u32[]{:S(2)}) collective-permute-start(bf16[6,2,128,128]{3,2,1,0:T(8,128)(2,1)S(1)} %pad_maximum_fusion.4.refs_0_), channel_id=1, source_target_pairs={{0,8},{4,12},{8,0},{12,4},{16,24},{20,28},{24,16},{28,20},{1,9},{5... | collective-permute-start | bytes 1179656 | tf_op jit(solution)/shard_map/ppermute | solution.py:65
  171.0 39.2 %collective-permute-start.26 = (bf16[2,704,512]{2,1,0:T(8,128)(2,1)}, bf16[2,704,512]{2,1,0:T(8,128)(2,1)}, u32[]{:S(2)}, u32[]{:S(2)}) collective-permute-start(bf16[2,704,512]{2,1,0:T(8,128)(2,1)} %collective-permute-done.19.refs_4_.refs_2_), channel_id=1, source_target_pairs={{0,2},{1,3},{2,0},{3,1},{4,6},{5,7},{6,4},{7,5},{8,10},{9,11},{10,... | collective-permute-start | bytes 4325384 | tf_op jit(solution)/shard_map/ppermute | solution.py:83
  180.3 18.7 %collective-permute-start.18 = (bf16[1,704,512]{2,1,0:T(8,128)(2,1)}, bf16[1,704,512]{2,1,0:T(8,128)(2,1)S(1)}, u32[]{:S(2)}, u32[]{:S(2)}) collective-permute-start(bf16[1,704,512]{2,1,0:T(8,128)(2,1)} %collective-permute-done.14.refs_1_), channel_id=1, source_target_pairs={{0,4},{4,0},{8,12},{12,8},{16,20},{20,16},{24,28},{28,24},{1,5},{5... | collective-permute-start | bytes 2162696 | tf_op jit(solution)/shard_map/ppermute | solution.py:37
  181.5 19.6 %collective-permute-start.32 = (bf16[2,128,256]{2,1,0:T(8,128)(2,1)S(1)}, bf16[2,128,256]{2,1,0:T(8,128)(2,1)S(1)}, u32[]{:S(2)}, u32[]{:S(2)}) collective-permute-start(bf16[2,128,256]{2,1,0:T(8,128)(2,1)S(1)} %copy-done.59), channel_id=1, source_target_pairs={{0,24},{4,28},{8,16},{12,20},{16,8},{20,12},{24,0},{28,4},{1,25},{... | collective-permute-start | bytes 393224 | tf_op jit(solution)/shard_map/ppermute | solution.py:65
  183.6 25.9 %collective-permute-start.31 = (bf16[2,128,256]{2,1,0:T(8,128)(2,1)S(1)}, bf16[2,128,256]{2,1,0:T(8,128)(2,1)S(1)}, u32[]{:S(2)}, u32[]{:S(2)}) collective-permute-start(bf16[2,128,256]{2,1,0:T(8,128)(2,1)S(1)} %copy-done.59), channel_id=1, source_target_pairs={{0,16},{4,20},{8,24},{12,28},{16,0},{20,4},{24,8},{28,12},{1,17},{... | collective-permute-start | bytes 393224 | tf_op jit(solution)/shard_map/ppermute | solution.py:65
  183.6 25.9 %collective-permute-start.30 = (bf16[2,128,256]{2,1,0:T(8,128)(2,1)S(1)}, bf16[2,128,256]{2,1,0:T(8,128)(2,1)S(1)}, u32[]{:S(2)}, u32[]{:S(2)}) collective-permute-start(bf16[2,128,256]{2,1,0:T(8,128)(2,1)S(1)} %copy-done.59), channel_id=1, source_target_pairs={{0,8},{4,12},{8,0},{12,4},{16,24},{20,28},{24,16},{28,20},{1,9},{5... | collective-permute-start | bytes 393224 | tf_op jit(solution)/shard_map/ppermute | solution.py:65
  199.9 9.6 %collective-permute-start.29 = (bf16[64,1024]{1,0:T(8,128)(2,1)S(1)}, bf16[64,1024]{1,0:T(8,128)(2,1)S(1)}, u32[]{:S(2)}, u32[]{:S(2)}) collective-permute-start(bf16[64,1024]{1,0:T(8,128)(2,1)S(1)} %get-tuple-element.130), channel_id=1, source_target_pairs={{0,2},{1,3},{2,0},{3,1},{4,6},{5,7},{6,4},{7,5},{8,10},{9,11},{10,... | collective-permute-start | bytes 393224 | tf_op jit(solution)/shard_map/ppermute | solution.py:83
  201.8 7.7 %collective-permute-start.28 = (bf16[64,1024]{1,0:T(8,128)(2,1)S(1)}, bf16[64,1024]{1,0:T(8,128)(2,1)S(1)}, u32[]{:S(2)}, u32[]{:S(2)}) collective-permute-start(bf16[64,1024]{1,0:T(8,128)(2,1)S(1)} %get-tuple-element.128), channel_id=1, source_target_pairs={{0,4},{4,0},{8,12},{12,8},{16,20},{20,16},{24,28},{28,24},{1,5},{5... | collective-permute-start | bytes 393224 | tf_op jit(solution)/shard_map/ppermute | solution.py:37
  212.1 17.4 %collective-permute-start.36 = (bf16[2,512,256]{2,1,0:T(8,128)(2,1)}, bf16[2,512,256]{2,1,0:T(8,128)(2,1)S(1)}, u32[]{:S(2)}, u32[]{:S(2)}) collective-permute-start(bf16[2,512,256]{2,1,0:T(8,128)(2,1)} %join.11.refs_3_), channel_id=1, source_target_pairs={{0,2},{1,3},{2,0},{3,1},{4,6},{5,7},{6,4},{7,5},{8,10},{9,11},{10,... | collective-permute-start | bytes 1572872 | tf_op jit(solution)/shard_map/ppermute | solution.py:83
  213.8 15.7 %collective-permute-start.35 = (bf16[2,512,256]{2,1,0:T(8,128)(2,1)}, bf16[2,512,256]{2,1,0:T(8,128)(2,1)S(1)}, u32[]{:S(2)}, u32[]{:S(2)}) collective-permute-start(bf16[2,512,256]{2,1,0:T(8,128)(2,1)} %join.11.refs_3_), channel_id=1, source_target_pairs={{0,4},{4,0},{8,12},{12,8},{16,20},{20,16},{24,28},{28,24},{1,5},{5... | collective-permute-start | bytes 1572872 | tf_op jit(solution)/shard_map/ppermute | solution.py:37
  214.8 13.4 %collective-permute-start.33 = (bf16[64,1024]{1,0:T(8,128)(2,1)S(1)}, bf16[64,1024]{1,0:T(8,128)(2,1)S(1)}, u32[]{:S(2)}, u32[]{:S(2)}) collective-permute-start(bf16[64,1024]{1,0:T(8,128)(2,1)S(1)} %add_convert_fusion.6), channel_id=1, source_target_pairs={{0,2},{1,3},{2,0},{3,1},{4,6},{5,7},{6,4},{7,5},{8,10},{9,11},{10,... | collective-permute-start | bytes 393224 | tf_op jit(solution)/shard_map/ppermute | solution.py:83
  216.1 13.4 %collective-permute-start.34 = (bf16[64,1024]{1,0:T(8,128)(2,1)S(1)}, bf16[64,1024]{1,0:T(8,128)(2,1)S(1)}, u32[]{:S(2)}, u32[]{:S(2)}) collective-permute-start(bf16[64,1024]{1,0:T(8,128)(2,1)S(1)} %add_convert_fusion.5), channel_id=1, source_target_pairs={{0,4},{4,0},{8,12},{12,8},{16,20},{20,16},{24,28},{28,24},{1,5},{5... | collective-permute-start | bytes 393224 | tf_op jit(solution)/shard_map/ppermute | solution.py:37
  231.9 14.5 %collective-permute-start.42 = (bf16[2,256,256]{2,1,0:T(8,128)(2,1)S(1)}, bf16[2,256,256]{2,1,0:T(8,128)(2,1)S(1)}, u32[]{:S(2)}, u32[]{:S(2)}) collective-permute-start(bf16[2,256,256]{2,1,0:T(8,128)(2,1)S(1)} %slice.113), channel_id=1, source_target_pairs={{0,2},{1,3},{2,0},{3,1},{4,6},{5,7},{6,4},{7,5},{8,10},{9,11},{10,... | collective-permute-start | bytes 786440 | tf_op jit(solution)/shard_map/ppermute | solution.py:83
  232.3 14.1 %collective-permute-start.41 = (bf16[2,256,256]{2,1,0:T(8,128)(2,1)S(1)}, bf16[2,256,256]{2,1,0:T(8,128)(2,1)S(1)}, u32[]{:S(2)}, u32[]{:S(2)}) collective-permute-start(bf16[2,256,256]{2,1,0:T(8,128)(2,1)S(1)} %slice.112), channel_id=1, source_target_pairs={{0,4},{4,0},{8,12},{12,8},{16,20},{20,16},{24,28},{28,24},{1,5},{5... | collective-permute-start | bytes 786440 | tf_op jit(solution)/shard_map/ppermute | solution.py:37
  234.5 11.9 %collective-permute-start.40 = (bf16[256,128]{1,0:T(8,128)(2,1)S(1)}, bf16[256,128]{1,0:T(8,128)(2,1)S(1)}, u32[]{:S(2)}, u32[]{:S(2)}) collective-permute-start(bf16[256,128]{1,0:T(8,128)(2,1)S(1)} %convolution_convert_fusion.1.refs_0_), channel_id=1, source_target_pairs={{0,24},{4,28},{8,16},{12,20},{16,8},{20,12},{24,0},{28,4},{1,25},{... | collective-permute-start | bytes 196616 | tf_op jit(solution)/shard_map/ppermute | solution.py:65
  235.9 10.5 %collective-permute-start.39 = (bf16[256,128]{1,0:T(8,128)(2,1)S(1)}, bf16[256,128]{1,0:T(8,128)(2,1)S(1)}, u32[]{:S(2)}, u32[]{:S(2)}) collective-permute-start(bf16[256,128]{1,0:T(8,128)(2,1)S(1)} %convolution_convert_fusion.1.refs_0_), channel_id=1, source_target_pairs={{0,16},{4,20},{8,24},{12,28},{16,0},{20,4},{24,8},{28,12},{1,17},{... | collective-permute-start | bytes 196616 | tf_op jit(solution)/shard_map/ppermute | solution.py:65
  235.9 10.6 %collective-permute-start.38 = (bf16[256,128]{1,0:T(8,128)(2,1)S(1)}, bf16[256,128]{1,0:T(8,128)(2,1)S(1)}, u32[]{:S(2)}, u32[]{:S(2)}) collective-permute-start(bf16[256,128]{1,0:T(8,128)(2,1)S(1)} %convolution_convert_fusion.1.refs_0_), channel_id=1, source_target_pairs={{0,8},{4,12},{8,0},{12,4},{16,24},{20,28},{24,16},{28,20},{1,9},{5... | collective-permute-start | bytes 196616 | tf_op jit(solution)/shard_map/ppermute | solution.py:65
  254.4 52.9 %collective-permute-start.48 = (bf16[576,1024]{1,0:T(8,128)(2,1)}, bf16[576,1024]{1,0:T(8,128)(2,1)}, u32[]{:S(2)}, u32[]{:S(2)}) collective-permute-start(bf16[576,1024]{1,0:T(8,128)(2,1)} %fusion.1), channel_id=1, source_target_pairs={{0,1},{1,0},{2,3},{3,2},{4,5},{5,4},{6,7},{7,6},{8,9},{9,8},{10,11... | collective-permute-start | bytes 3538952 | tf_op jit(solution)/shard_map/ppermute | solution.py:42
  254.6 20.7 %collective-permute-start.51 = (bf16[6,352,128]{2,1,0:T(8,128)(2,1)S(1)}, bf16[6,352,128]{2,1,0:T(8,128)(2,1)S(1)}, u32[]{:S(2)}, u32[]{:S(2)}) collective-permute-start(bf16[6,352,128]{2,1,0:T(8,128)(2,1)S(1)} %bitcast.106), channel_id=1, source_target_pairs={{0,24},{4,28},{8,16},{12,20},{16,8},{20,12},{24,0},{28,4},{1,25},{... | collective-permute-start | bytes 1622024 | tf_op jit(solution)/shard_map/ppermute | solution.py:65
  257.6 8.6 %collective-permute-start.44 = (bf16[1024,128]{1,0:T(8,128)(2,1)}, bf16[1024,128]{1,0:T(8,128)(2,1)S(1)}, u32[]{:S(2)}, u32[]{:S(2)}) collective-permute-start(bf16[1024,128]{1,0:T(8,128)(2,1)} %join.12), channel_id=1, source_target_pairs={{0,2},{1,3},{2,0},{3,1},{4,6},{5,7},{6,4},{7,5},{8,10},{9,11},{10,... | collective-permute-start | bytes 786440 | tf_op jit(solution)/shard_map/ppermute | solution.py:83
  259.3 44.1 %collective-permute-start.50 = (bf16[6,352,128]{2,1,0:T(8,128)(2,1)S(1)}, bf16[6,352,128]{2,1,0:T(8,128)(2,1)S(1)}, u32[]{:S(2)}, u32[]{:S(2)}) collective-permute-start(bf16[6,352,128]{2,1,0:T(8,128)(2,1)S(1)} %bitcast.107), channel_id=1, source_target_pairs={{0,16},{4,20},{8,24},{12,28},{16,0},{20,4},{24,8},{28,12},{1,17},{... | collective-permute-start | bytes 1622024 | tf_op jit(solution)/shard_map/ppermute | solution.py:65
  259.3 44.9 %collective-permute-start.49 = (bf16[6,352,128]{2,1,0:T(8,128)(2,1)S(1)}, bf16[6,352,128]{2,1,0:T(8,128)(2,1)}, u32[]{:S(2)}, u32[]{:S(2)}) collective-permute-start(bf16[6,352,128]{2,1,0:T(8,128)(2,1)S(1)} %bitcast.108), channel_id=1, source_target_pairs={{0,8},{4,12},{8,0},{12,4},{16,24},{20,28},{24,16},{28,20},{1,9},{5... | collective-permute-start | bytes 1622024 | tf_op jit(solution)/shard_map/ppermute | solution.py:65
  273.9 33.3 %collective-permute-start.45 = (bf16[512,128]{1,0:T(8,128)(2,1)S(1)}, bf16[512,128]{1,0:T(8,128)(2,1)S(1)}, u32[]{:S(2)}, u32[]{:S(2)}) collective-permute-start(bf16[512,128]{1,0:T(8,128)(2,1)S(1)} %slice.136), channel_id=1, source_target_pairs={{0,4},{4,0},{8,12},{12,8},{16,20},{20,16},{24,28},{28,24},{1,5},{5... | collective-permute-start | bytes 393224 | tf_op jit(solution)/shard_map/ppermute | solution.py:37
  275.3 31.9 %collective-permute-start.46 = (bf16[512,128]{1,0:T(8,128)(2,1)S(1)}, bf16[512,128]{1,0:T(8,128)(2,1)S(1)}, u32[]{:S(2)}, u32[]{:S(2)}) collective-permute-start(bf16[512,128]{1,0:T(8,128)(2,1)S(1)} %slice.137), channel_id=1, source_target_pairs={{0,2},{1,3},{2,0},{3,1},{4,6},{5,7},{6,4},{7,5},{8,10},{9,11},{10,... | collective-permute-start | bytes 393224 | tf_op jit(solution)/shard_map/ppermute | solution.py:83
  320.7 14.4 %collective-permute-start.52 = (bf16[4,2,272,128]{3,2,1,0:T(8,128)(2,1)}, bf16[4,2,272,128]{3,2,1,0:T(8,128)(2,1)}, u32[]{:S(2)}, u32[]{:S(2)}) collective-permute-start(bf16[4,2,272,128]{3,2,1,0:T(8,128)(2,1)} %cross_block.3), channel_id=1, source_target_pairs={{0,2},{1,3},{2,0},{3,1},{4,6},{5,7},{6,4},{7,5},{8,10},{9,11},{10,... | collective-permute-start | bytes 1671176 | tf_op jit(solution)/shard_map/ppermute | solution.py:83
  (88 other events, 803.9 us)
where the time goes:
time: 387 us; the launch traced here: 386 us
  waiting for transfers between devices  156 us (40%)
  Pallas kernels  95.7 us (25%)
  starting transfers between devices  84.1 us (22%)
  local copies, waits for them, and re-layouts  29.2 us (8%)
  other arithmetic  18.5 us (5%)
    ppermute x24, waiting for transfers between devices, swap_z(): return lax.ppermute(value, 'dp', [(i, i ^ 2 * step) for i in range(count)])  85.8 us
    ppermute x18, waiting for transfers between devices, swap_x(): return lax.ppermute(value, 'dp', [(i, i ^ 1) for i in range(count)])  43.3 us
    ppermute x24, starting transfers between devices, swap_z(): return lax.ppermute(value, 'dp', [(i, i ^ 2 * step) for i in range(count)])  43.2 us
    pallas_call x4, Pallas kernels, ff(): pl.pallas_call(functools.partial(ff_kernel, chunks=plan, done=before, las...  22 us
    pallas_call x2, Pallas kernels, enc_block(): pl.pallas_call(functools.partial(enc_block_kernel, rows=query_rows), out_...  21.1 us
    ppermute x15, starting transfers between devices, swap_y(): return lax.ppermute(value, 'mp', [(i, i ^ 2) for i in range(4)])  20.3 us
    pallas_call x2, Pallas kernels, cross_block(): pl.pallas_call(functools.partial(cross_block_kernel, key_rows=key_rows, c...  19.9 us
    ppermute x18, starting transfers between devices, swap_x(): return lax.ppermute(value, 'dp', [(i, i ^ 1) for i in range(count)])  19.3 us
  transfers between devices with their start and end apart: 67, of which 31 were waited for; matrix products, arithmetic and copies ran while one was open for 4% of the time, Pallas kernels for 17%

commit v1 on v0

--- a/solution.py
+++ b/solution.py
@@ -492,19 +492,31 @@
     )(low, high, first_row.reshape(1), seg_q, seg_k, h, *weights)
 
 
-def cross_block_kernel(begin_ref, end_ref, question_ref, x_ref, *refs, key_rows, count):
+def cross_block_kernel(
+    active_ref, begin_ref, end_ref, question_ref, x_ref, *refs, key_rows, count
+):
     queries, (h_ref, *weights, o_ref, k, v, acc) = refs[:count], refs[count:]
     project_into(h_ref, weights, (0, 1), (k, v))
 
     @pl.when(pl.program_id(0) == pl.num_programs(0) - 1)
     def _():
         cross_kernel(
-            begin_ref, end_ref, question_ref, x_ref, queries, k, v, o_ref, acc, key_rows=key_rows
+            active_ref,
+            begin_ref,
+            end_ref,
+            question_ref,
+            x_ref,
+            queries,
+            k,
+            v,
+            o_ref,
+            acc,
+            key_rows=key_rows,
         )
 
 
 def cross_kernel(
-    begin_ref, end_ref, question_ref, x_ref, queries, k_ref, v_ref, o_ref, acc, *, key_rows
+    active_ref, begin_ref, end_ref, question_ref, x_ref, queries, k_ref, v_ref, o_ref, acc, *, key_rows
 ):
     questions, length = queries[0].shape[:2]
     pairs = k_ref.shape[1] // LANES
@@ -516,42 +528,57 @@
         own, other = (ref[question] for ref in queries)
         return jnp.where(own_x == p, own, other)
 
-    last = k_ref.shape[0] // key_rows - 1
     acc[...] = jnp.zeros_like(acc)
     low_half = lax.broadcasted_iota(jnp.int32, (1, LANES), 1) < HEAD_DIM
-
-    def passage(s, carry):
-        begin, end, question = begin_ref[s], end_ref[s], question_ref[s]
-        first = begin // key_rows
-
-        def step(j, inner):
-            for p in range(pairs):
-                columns = slice(p * LANES, (p + 1) * LANES)
-                total = None
-                query = pair_of(question, p)
-                for u in range(2):
-                    index = first + 2 * j + u
-                    offset = pl.multiple_of(jnp.minimum(index, last) * key_rows, key_rows)
-                    position = index * key_rows + lax.broadcasted_iota(
-                        jnp.int32, (1, key_rows), 1
-                    )
-                    allowed = (position >= begin) & (position < end)
-                    part = two_heads(
-                        query,
-                        k_ref[pl.ds(offset, key_rows), columns],
-                        v_ref[pl.ds(offset, key_rows), columns],
-                        allowed,
-                        low_half,
-                    )
-                    total = part if total is None else total + part
-                acc[question, p] += total
-            return inner
-
-        blocks = (end + key_rows - 1) // key_rows - first
-        lax.fori_loop(0, jnp.where(end > begin, (blocks + 1) // 2, 0), step, 0)
+    rows = k_ref.shape[0]
+
+    def bounds(s):
+        begin = begin_ref[s]
+        end = jnp.where(s < active_ref[1], end_ref[s], begin)
+        return begin, end, question_ref[s], begin // 16 * 16
+
+    def sums_of(place, j):
+        begin, end, question, tile = place
+        low = tile + j * key_rows
+        offset = pl.multiple_of(jnp.minimum(low, rows - key_rows), 16)
+        position = offset + lax.broadcasted_iota(jnp.int32, (1, key_rows), 1)
+        allowed = (position >= jnp.maximum(begin, low)) & (position < end)
+        return [
+            two_heads(
+                pair_of(question, p),
+                k_ref[pl.ds(offset, key_rows), p * LANES : (p + 1) * LANES],
+                v_ref[pl.ds(offset, key_rows), p * LANES : (p + 1) * LANES],
+                allowed,
+                low_half,
+            )
+            for p in range(pairs)
+        ]
+
+    def add(place, sums):
+        for p in range(pairs):
+            acc[place[2], p] += sums[p]
+
+    def two_passages(i, carry):
+        first = active_ref[0] + 2 * i
+        places = [bounds(first), bounds(jnp.minimum(first + 1, begin_ref.shape[0] - 1))]
+        places[1] = (
+            places[1][0],
+            jnp.where(first + 1 < active_ref[1], places[1][1], places[1][0]),
+            *places[1][2:],
+        )
+        both = [sums_of(place, 0) for place in places]
+        for place, sums in zip(places, both):
+            add(place, sums)
+        for place in places:
+
+            def more(j, inner, place=place):
+                add(place, sums_of(place, j))
+                return inner
+
+            lax.fori_loop(1, (place[1] - place[3] + key_rows - 1) // key_rows, more, 0)
         return carry
 
-    lax.fori_loop(0, begin_ref.shape[0], passage, 0)
+    lax.fori_loop(0, (active_ref[1] - active_ref[0] + 1) // 2, two_passages, 0)
     eye = lax.broadcasted_iota(jnp.int32, (length, LANES), 0) == lax.broadcasted_iota(
         jnp.int32, (length, LANES), 1
     )
@@ -579,16 +606,24 @@
 def cross_block(begin, end, question, x, queries, h, weights):
     questions, length = queries[0].shape[:2]
     rows, width = h.shape[0], weights[0].shape[2]
-    key_rows = math.gcd(rows, LANES)
+    key_rows = min(rows, LANES)
     pairs = width // LANES
     step = row_block(rows, 400)
+    place = jnp.arange(begin.shape[0], dtype=jnp.int32)
+    here = end > begin
+    active = jnp.stack(
+        [
+            jnp.min(jnp.where(here, place, begin.shape[0])),
+            jnp.max(jnp.where(here, place + 1, 0)),
+        ]
+    )
     smem = pl.BlockSpec(memory_space=pltpu.SMEM)
     shape = (questions // 2, pairs, 2 * length + 16, LANES)
     return pl.pallas_call(
         functools.partial(cross_block_kernel, key_rows=key_rows, count=len(queries)),
         out_shape=jax.ShapeDtypeStruct(shape, BF16),
         grid=(rows // step,),
-        in_specs=[smem] * 4
+        in_specs=[smem] * 5
         + [resident(q) for q in queries]
         + [pl.BlockSpec((step, h.shape[1]), lambda i: (i, 0))]
         + [resident(weight) for weight in weights],
@@ -600,7 +635,7 @@
             flops=rows * width * (4 * h.shape[1] + 2048), bytes_accessed=2 * h.size, transcendentals=0
         ),
         name="cross_block",
-    )(begin, end, question, x.reshape(1), *queries, h, *weights)
+    )(active, begin, end, question, x.reshape(1), *queries, h, *weights)
 
 
 def by_column_x(sums, length):
@@ -798,11 +833,13 @@
     answers = own_first(answers, x, shard_width, z_place)
     answer_normed = rms_normed(answers)
 
-    attn_near, gate_z, normed, enc_ff_t = meet(attn_near, gate_z, normed, enc_ff_t)
+    gate_z, rest_shard = meet(gate_z, enc_ff_t[1:3])
+    rest_z = pieces_z(rest_shard, 2)
+
+    attn_near, gate_z, normed = meet(attn_near, gate_z, normed)
     attn_far = spread_far(attn_near, 1)
     gate_block = join(gate_z, 2)
     gate_near = spread_near(gate_block)
-    rest_z = pieces_z(enc_ff_t[1:3], 2)
 
     def attend(parts):
         return enc_block(low, high, own_begin, seg_q, seg_k, normed, parts)

time: 387 us -> 380 us (0.982)
  starting transfers between devices: 84.1 us -> 72 us
  waiting for transfers between devices: 156 us -> 164 us
  Pallas kernels: 95.7 us -> 91.4 us
    ppermute x24, waiting for transfers between devices: 85.8 us -> 95.8 us  [swap_z(): return lax.ppermute(value, 'dp', [(i, i ^ 2 * step) for i in range(count)])]
    ppermute x24, starting transfers between devices: 43.2 us -> 35.1 us  [swap_z(): return lax.ppermute(value, 'dp', [(i, i ^ 2 * step) for i in range(count)])]
    ppermute x18, waiting for transfers between devices: 43.3 us -> 37.8 us  [swap_x(): return lax.ppermute(value, 'dp', [(i, i ^ 1) for i in range(count)])]
    pallas_call x2, Pallas kernels: 19.9 us -> 14.9 us  [cross_block(): pl.pallas_call(functools.partial(cross_block_kernel, key_rows=key_rows, c...]
  transfers between devices with their start and end apart: 67 -> 67, of which waited for: 31 -> 30; matrix products, arithmetic and copies ran while one was open for 4% -> 5% of each run, Pallas kernels for 17% -> 17%
where the time goes in v1:
time: 380 us; the launch traced here: 379 us
  waiting for transfers between devices  164 us (43%)
  Pallas kernels  91.4 us (24%)
  starting transfers between devices  72 us (19%)
  local copies, waits for them, and re-layouts  29.3 us (8%)
  other arithmetic  20.5 us (5%)
    ppermute x24, waiting for transfers between devices, swap_z(): return lax.ppermute(value, 'dp', [(i, i ^ 2 * step) for i in range(count)])  95.8 us
    ppermute x18, waiting for transfers between devices, swap_x(): return lax.ppermute(value, 'dp', [(i, i ^ 1) for i in range(count)])  37.8 us
    ppermute x24, starting transfers between devices, swap_z(): return lax.ppermute(value, 'dp', [(i, i ^ 2 * step) for i in range(count)])  35.1 us
    pallas_call x4, Pallas kernels, ff(): pl.pallas_call(functools.partial(ff_kernel, chunks=plan, done=before, las...  22 us
    pallas_call x2, Pallas kernels, enc_block(): pl.pallas_call(functools.partial(enc_block_kernel, rows=query_rows), out_...  21.1 us
    ppermute x15, waiting for transfers between devices, swap_y(): return lax.ppermute(value, 'mp', [(i, i ^ 2) for i in range(4)])  20.8 us
    ppermute x18, starting transfers between devices, swap_x(): return lax.ppermute(value, 'dp', [(i, i ^ 1) for i in range(count)])  17.8 us
    ppermute x15, starting transfers between devices, swap_y(): return lax.ppermute(value, 'mp', [(i, i ^ 2) for i in range(4)])  17.7 us
  transfers between devices with their start and end apart: 67, of which 30 were waited for; matrix products, arithmetic and copies ran while one was open for 5% of the time, Pallas kernels for 17%

profile of v1, /device:TPU:0, one launch (start us, length us, event | category | flops | bytes accessed | tf_op | source)
XLA Modules:
  0.0 379.1 jit_solution(8052099217005735940)
XLA Ops:
  1.8 3.0 collective-permute-start.3
  6.6 2.0 collective-permute-start.5
  8.6 2.6 collective-permute-start.1
  12.8 1.9 collective-permute-start.2
  14.7 6.3 %collective-permute-done.5 = bf16[128,1024]{1,0:T(8,128)(2,1)S(1)} collective-permute-done((bf16[128,1024]{1,0:T(8,128)(2,1)S(1)}, bf16[128,1024]{1,0:T(8,128)(2,1)S(1)}, u32[]{:S(2)}, u32[]{:S(2)}) %collective-permute-start.5) | collective-permute-done | bytes 262176 | tf_op jit(solution)/shard_map/ppermute | solution.py:37
  21.1 4.4 %collective-permute-done.1.refs_2_ = bf16[4,128,256]{2,1,0:T(8,128)(2,1)S(1)} collective-permute-done((bf16[4,128,256]{2,1,0:T(8,128)(2,1)S(1)}, bf16[4,128,256]{2,1,0:T(8,128)(2,1)S(1)}, u32[]{:S(2)}, u32[]{:S(2)}) %collective-permute-start.1) | collective-permute-done | bytes 262176 | tf_op jit(solution)/shard_map/ppermute | solution.py:65
  25.4 3.7 collective-permute-done.2.refs_3_
  30.0 2.3 join.7.refs_0_.refs_1_
  35.0 2.5 collective-permute-start.10
  37.6 4.7 %collective-permute-start.9 = (bf16[1,704,128]{2,1,0:T(8,128)(2,1)S(1)}, bf16[1,704,128]{2,1,0:T(8,128)(2,1)S(1)}, u32[]{:S(2)}, u32[]{:S(2)}) collective-permute-start(bf16[1,704,128]{2,1,0:T(8,128)(2,1)S(1)} %slice.101.refs_0_), channel_id=1, source_target_pairs={{0,16},{4,20},{8,24},{12,28},{16,0},{20,4},{24,8},{28,12},{1,17},{... | collective-permute-start | bytes 540680 | tf_op jit(solution)/shard_map/ppermute | solution.py:65
  43.8 10.3 %collective-permute-done.9.refs_2_ = bf16[1,704,128]{2,1,0:T(8,128)(2,1)S(1)} collective-permute-done((bf16[1,704,128]{2,1,0:T(8,128)(2,1)S(1)}, bf16[1,704,128]{2,1,0:T(8,128)(2,1)S(1)}, u32[]{:S(2)}, u32[]{:S(2)}) %collective-permute-start.9) | collective-permute-done | bytes 180256 | tf_op jit(solution)/shard_map/ppermute | solution.py:65
  54.0 3.0 collective-permute-start.17
  57.3 9.9 %prepare.1 = (bf16[1408,1024]{1,0:T(8,128)(2,1)}, bf16[1408,1024]{1,0:T(8,128)(2,1)}) custom-call(s32[1]{0:T(128)} %bitcast.3.begin_ref, s32[8]{0:T(128)} %stack.78.order_ref, bf16[2304,1024]{1,0:T(8,128)(2,1)} %x_ref), custom_call_target="tpu_custom_call" | custom-call | flops 5767168 | bytes 8650752 | tf_op jit(solution)/shard_map/prepare/pallas_call | solution.py:350
  67.3 2.8 join.8.refs_1_
  76.1 10.0 %collective-permute-done.16.refs_2_ = bf16[2,704,128]{2,1,0:T(8,128)(2,1)} collective-permute-done((bf16[2,704,128]{2,1,0:T(8,128)(2,1)}, bf16[2,704,128]{2,1,0:T(8,128)(2,1)}, u32[]{:S(2)}, u32[]{:S(2)}) %collective-permute-start.16) | collective-permute-done | bytes 360480 | tf_op jit(solution)/shard_map/ppermute | solution.py:65
  88.4 10.2 %enc_block.2.refs_0_ = bf16[1152,256]{1,0:T(8,128)(2,1)S(1)} custom-call(s32[3]{0:T(128)S(1)} %get-tuple-element.225.low_ref, s32[3]{0:T(128)S(1)} %get-tuple-element.224.high_ref, s32[1]{0:T(128)} %bitcast.14.first_ref, s32[1152,128]{1,0:T(8,128)S(1)} %broadcast_in_dim.27.seg_q_ref, s32[11,1,128]{2,1,0:T(1,128)S(1)} %reshape.179.seg_k_ref, ...), custom_call_target="tpu_custom_call" | custom-call | flops 3321888768 | bytes 2883584 | tf_op jit(solution)/shard_map/enc_block/pallas_call | solution.py:474
  98.6 10.9 %enc_block.3.refs_3_ = bf16[1152,256]{1,0:T(8,128)(2,1)S(1)} custom-call(s32[3]{0:T(128)S(1)} %get-tuple-element.225.low_ref, s32[3]{0:T(128)S(1)} %get-tuple-element.224.high_ref, s32[1]{0:T(128)} %bitcast.14.first_ref, s32[1152,128]{1,0:T(8,128)S(1)} %broadcast_in_dim.27.seg_q_ref, s32[11,1,128]{2,1,0:T(1,128)S(1)} %reshape.179.seg_k_ref, ...), custom_call_target="tpu_custom_call" | custom-call | flops 3321888768 | bytes 2883584 | tf_op jit(solution)/shard_map/enc_block/pallas_call | solution.py:474
  110.8 3.0 out_project.1
  114.2 2.9 collective-permute-done.24
  117.0 2.4 fusion.2
  121.0 2.5 join.9.refs_3_.refs_1_
  123.5 2.1 collective-permute-start.20
  129.3 2.9 collective-permute-start.22
  136.2 6.1 %collective-permute-done.23.refs_3_ = bf16[6,2,128,128]{3,2,1,0:T(8,128)(2,1)S(1)} collective-permute-done((bf16[6,2,128,128]{3,2,1,0:T(8,128)(2,1)S(1)}, bf16[6,2,128,128]{3,2,1,0:T(8,128)(2,1)S(1)}, u32[]{:S(2)}, u32[]{:S(2)}) %collective-permute-start.23) | collective-permute-done | bytes 393248 | tf_op jit(solution)/shard_map/ppermute | solution.py:65
  142.2 23.7 %collective-permute-done.22.refs_2_ = bf16[6,2,128,128]{3,2,1,0:T(8,128)(2,1)S(1)} collective-permute-done((bf16[6,2,128,128]{3,2,1,0:T(8,128)(2,1)S(1)}, bf16[6,2,128,128]{3,2,1,0:T(8,128)(2,1)S(1)}, u32[]{:S(2)}, u32[]{:S(2)}) %collective-permute-start.22) | collective-permute-done | bytes 393248 | tf_op jit(solution)/shard_map/ppermute | solution.py:65
  169.0 2.6 join.10
  171.6 3.7 self_block.1
  178.6 3.3 collective-permute-start.30
  182.9 12.3 %collective-permute-done.18.refs_2_ = bf16[1,704,512]{2,1,0:T(8,128)(2,1)S(1)} collective-permute-done((bf16[1,704,512]{2,1,0:T(8,128)(2,1)}, bf16[1,704,512]{2,1,0:T(8,128)(2,1)S(1)}, u32[]{:S(2)}, u32[]{:S(2)}) %collective-permute-start.18) | collective-permute-done | bytes 720928 | tf_op jit(solution)/shard_map/ppermute | solution.py:37
  198.7 6.1 %ff.4.refs_0_ = bf16[1152,704]{1,0:T(8,128)(2,1)S(1)} custom-call(bf16[1152,1024]{1,0:T(8,128)(2,1)} %pad_maximum_fusion.refs_0_, bf16[1,704,512]{2,1,0:T(8,128)(2,1)S(1)} %copy-done.7, bf16[1,704,512]{2,1,0:T(8,128)(2,1)} %collective-permute-done.13.refs_2_, bf16[2,704,512]{2,1,0:T(8,128)(2,1)S(1)} %copy-done.6, ...), custom_call_target="tpu_custom_call" | custom-call | flops 3321888768 | bytes 3981312 | tf_op jit(solution)/shard_map/ff/pallas_call | solution.py:253
  214.2 6.2 %ff.5.refs_3_ = bf16[1152,704]{1,0:T(8,128)(2,1)S(1)} custom-call(bf16[1152,1024]{1,0:T(8,128)(2,1)} %pad_maximum_fusion.refs_0_, bf16[1,704,512]{2,1,0:T(8,128)(2,1)} %collective-permute-done.14.refs_1_, bf16[1,704,512]{2,1,0:T(8,128)(2,1)S(1)} %copy-done.21, bf16[2,704,512]{2,1,0:T(8,128)(2,1)S(1)} %copy-done.19, ...), custom_call_target="tpu_custom_call" | custom-call | flops 3321888768 | bytes 3981312 | tf_op jit(solution)/shard_map/ff/pallas_call | solution.py:253
  220.4 4.4 %collective-permute-done.33 = bf16[64,1024]{1,0:T(8,128)(2,1)S(1)} collective-permute-done((bf16[64,1024]{1,0:T(8,128)(2,1)S(1)}, bf16[64,1024]{1,0:T(8,128)(2,1)S(1)}, u32[]{:S(2)}, u32[]{:S(2)}) %collective-permute-start.33) | collective-permute-done | bytes 131104 | tf_op jit(solution)/shard_map/ppermute | solution.py:83
  231.9 3.4 collective-permute-start.38
  235.2 7.4 %ff.6 = bf16[1152,1024]{1,0:T(8,128)(2,1)} custom-call(bf16[1152,704]{1,0:T(8,128)(2,1)} %copy-done.26, bf16[2,704,512]{2,1,0:T(8,128)(2,1)S(1)} %copy-done.6, bf16[2,704,512]{2,1,0:T(8,128)(2,1)} %collective-permute-done.19.refs_4_.refs_2_, bf16[1152,704]{1,0:T(8,128)(2,1)} %copy-done.27, bf16[2,704,512]{2,1,0:T(8,128)(2,1)S(1)} %copy-done.19, ...), custom_call_target="tpu_custom_call" | custom-call | flops 3321888768 | bytes 4718592 | tf_op jit(solution)/shard_map/ff/pallas_call | solution.py:253
  244.5 2.8 collective-permute-done.47
  255.9 6.3 %collective-permute-done.44 = bf16[1024,128]{1,0:T(8,128)(2,1)S(1)} collective-permute-done((bf16[1024,128]{1,0:T(8,128)(2,1)}, bf16[1024,128]{1,0:T(8,128)(2,1)S(1)}, u32[]{:S(2)}, u32[]{:S(2)}) %collective-permute-start.44) | collective-permute-done | bytes 262176 | tf_op jit(solution)/shard_map/ppermute | solution.py:83
  263.8 4.2 %collective-permute-done.51.refs_3_ = bf16[6,352,128]{2,1,0:T(8,128)(2,1)S(1)} collective-permute-done((bf16[6,352,128]{2,1,0:T(8,128)(2,1)S(1)}, bf16[6,352,128]{2,1,0:T(8,128)(2,1)S(1)}, u32[]{:S(2)}, u32[]{:S(2)}) %collective-permute-start.51) | collective-permute-done | bytes 540704 | tf_op jit(solution)/shard_map/ppermute | solution.py:65
  270.8 28.8 %collective-permute-done.50.refs_2_ = bf16[6,352,128]{2,1,0:T(8,128)(2,1)S(1)} collective-permute-done((bf16[6,352,128]{2,1,0:T(8,128)(2,1)S(1)}, bf16[6,352,128]{2,1,0:T(8,128)(2,1)S(1)}, u32[]{:S(2)}, u32[]{:S(2)}) %collective-permute-start.50) | collective-permute-done | bytes 540704 | tf_op jit(solution)/shard_map/ppermute | solution.py:65
  300.5 2.9 join.13.refs_1_
  306.6 7.9 %cross_block.3 = bf16[4,2,272,128]{3,2,1,0:T(8,128)(2,1)} custom-call(s32[2]{0:T(128)S(1)} %pad_add_fusion.active_ref, s32[24]{0:T(128)S(1)} %get-tuple-element.177.begin_ref, s32[24]{0:T(128)S(1)} %get-tuple-element.178.end_ref, s32[24]{0:T(128)S(1)} %fusion.43.question_ref, s32[1]{0:T(128)} %bitcast.22.x_ref, bf16[8,128,128]{2,1,0:T(8,128)(2,1)S(1)} %bitcast.107, ...), custom_call_target="tpu_custom_call" | custom-call | flops 1811939328 | bytes 2359296 | tf_op jit(solution)/shard_map/cross_block/pallas_call | solution.py:622
  316.4 7.1 %cross_block.2 = bf16[4,2,272,128]{3,2,1,0:T(8,128)(2,1)S(1)} custom-call(s32[2]{0:T(128)S(1)} %pad_add_fusion.active_ref, s32[24]{0:T(128)S(1)} %get-tuple-element.177.begin_ref, s32[24]{0:T(128)S(1)} %get-tuple-element.178.end_ref, s32[24]{0:T(128)S(1)} %fusion.43.question_ref, s32[1]{0:T(128)} %bitcast.22.x_ref, bf16[8,128,128]{2,1,0:T(8,128)(2,1)S(1)} %bitcast.104, ...), custom_call_target="tpu_custom_call" | custom-call | flops 1811939328 | bytes 2359296 | tf_op jit(solution)/shard_map/cross_block/pallas_call | solution.py:622
  323.5 5.4 %collective-permute-done.52 = bf16[4,2,272,128]{3,2,1,0:T(8,128)(2,1)} collective-permute-done((bf16[4,2,272,128]{3,2,1,0:T(8,128)(2,1)}, bf16[4,2,272,128]{3,2,1,0:T(8,128)(2,1)}, u32[]{:S(2)}, u32[]{:S(2)}) %collective-permute-start.52) | collective-permute-done | bytes 557088 | tf_op jit(solution)/shard_map/ppermute | solution.py:83
  330.8 6.5 %collective-permute-done.53 = bf16[4,272,128]{2,1,0:T(8,128)(2,1)S(1)} collective-permute-done((bf16[4,272,128]{2,1,0:T(8,128)(2,1)S(1)}, bf16[4,272,128]{2,1,0:T(8,128)(2,1)S(1)}, u32[]{:S(2)}, u32[]{:S(2)}) %collective-permute-start.53) | collective-permute-done | bytes 278560 | tf_op jit(solution)/shard_map/ppermute | solution.py:37
  350.1 3.3 collective-permute-done.58
  356.2 2.7 collective-permute-done.61
  362.4 2.3 ff.7
  369.1 4.8 %collective-permute-done.65 = bf16[128,2,2,128]{0,3,1,2:T(8,128)(2,1)S(1)} collective-permute-done((bf16[128,2,2,128]{0,3,1,2:T(8,128)(2,1)S(1)}, bf16[128,2,2,128]{0,3,1,2:T(8,128)(2,1)S(1)}, u32[]{:S(2)}, u32[]{:S(2)}) %collective-permute-start.65) | collective-permute-done | bytes 131104 | tf_op jit(solution)/shard_map/ppermute | solution.py:37
  375.2 3.0 collective-permute-done.66
  (356 shorter events, 103.9 us)
Async XLA Ops:
  1.8 11.0 %collective-permute-start.3 = (bf16[6,128,128]{2,1,0:T(8,128)(2,1)S(1)}, bf16[6,128,128]{2,1,0:T(8,128)(2,1)}, u32[]{:S(2)}, u32[]{:S(2)}) collective-permute-start(bf16[6,128,128]{2,1,0:T(8,128)(2,1)S(1)} %get-tuple-element.201), channel_id=1, source_target_pairs={{0,4},{4,0},{8,12},{12,8},{16,20},{20,16},{24,28},{28,24},{1,5},{5... | collective-permute-start | bytes 589832 | tf_op jit(solution)/shard_map/ppermute | solution.py:37
  6.6 22.5 %collective-permute-start.4 = (bf16[3,352,128]{2,1,0:T(8,128)(2,1)S(1)}, bf16[3,352,128]{2,1,0:T(8,128)(2,1)S(1)}, u32[]{:S(2)}, u32[]{:S(2)}) collective-permute-start(bf16[3,352,128]{2,1,0:T(8,128)(2,1)S(1)} %get-tuple-element.187), channel_id=1, source_target_pairs={{0,4},{4,0},{8,12},{12,8},{16,20},{20,16},{24,28},{28,24},{1,5},{5... | collective-permute-start | bytes 811016 | tf_op jit(solution)/shard_map/ppermute | solution.py:37
  6.6 14.5 %collective-permute-start.5 = (bf16[128,1024]{1,0:T(8,128)(2,1)S(1)}, bf16[128,1024]{1,0:T(8,128)(2,1)S(1)}, u32[]{:S(2)}, u32[]{:S(2)}) collective-permute-start(bf16[128,1024]{1,0:T(8,128)(2,1)S(1)} %copy-done.48), channel_id=1, source_target_pairs={{0,4},{4,0},{8,12},{12,8},{16,20},{20,16},{24,28},{28,24},{1,5},{5... | collective-permute-start | bytes 786440 | tf_op jit(solution)/shard_map/ppermute | solution.py:37
  8.6 16.8 %collective-permute-start.1 = (bf16[4,128,256]{2,1,0:T(8,128)(2,1)S(1)}, bf16[4,128,256]{2,1,0:T(8,128)(2,1)S(1)}, u32[]{:S(2)}, u32[]{:S(2)}) collective-permute-start(bf16[4,128,256]{2,1,0:T(8,128)(2,1)S(1)} %copy-done.52), channel_id=1, source_target_pairs={{0,16},{4,20},{8,24},{12,28},{16,0},{20,4},{24,8},{28,12},{1,17},{... | collective-permute-start | bytes 786440 | tf_op jit(solution)/shard_map/ppermute | solution.py:65
  11.2 14.2 %collective-permute-start = (bf16[4,128,256]{2,1,0:T(8,128)(2,1)S(1)}, bf16[4,128,256]{2,1,0:T(8,128)(2,1)S(1)}, u32[]{:S(2)}, u32[]{:S(2)}) collective-permute-start(bf16[4,128,256]{2,1,0:T(8,128)(2,1)S(1)} %copy-done.52), channel_id=1, source_target_pairs={{0,8},{4,12},{8,0},{12,4},{16,24},{20,28},{24,16},{28,20},{1,9},{5... | collective-permute-start | bytes 786440 | tf_op jit(solution)/shard_map/ppermute | solution.py:65
  12.8 16.3 %collective-permute-start.2 = (bf16[4,128,256]{2,1,0:T(8,128)(2,1)S(1)}, bf16[4,128,256]{2,1,0:T(8,128)(2,1)S(1)}, u32[]{:S(2)}, u32[]{:S(2)}) collective-permute-start(bf16[4,128,256]{2,1,0:T(8,128)(2,1)S(1)} %copy-done.52), channel_id=1, source_target_pairs={{0,24},{4,28},{8,16},{12,20},{16,8},{20,12},{24,0},{28,4},{1,25},{... | collective-permute-start | bytes 786440 | tf_op jit(solution)/shard_map/ppermute | solution.py:65
  32.3 35.0 %collective-permute-start.7 = (bf16[4,512,256]{2,1,0:T(8,128)(2,1)}, bf16[4,512,256]{2,1,0:T(8,128)(2,1)S(1)}, u32[]{:S(2)}, u32[]{:S(2)}) collective-permute-start(bf16[4,512,256]{2,1,0:T(8,128)(2,1)} %join.7.refs_0_.refs_1_), channel_id=1, source_target_pairs={{0,2},{1,3},{2,0},{3,1},{4,6},{5,7},{6,4},{7,5},{8,10},{9,11},{10,... | collective-permute-start | bytes 3145736 | tf_op jit(solution)/shard_map/ppermute | solution.py:83
  33.9 33.4 %collective-permute-start.6 = (bf16[4,512,256]{2,1,0:T(8,128)(2,1)}, bf16[4,512,256]{2,1,0:T(8,128)(2,1)S(1)}, u32[]{:S(2)}, u32[]{:S(2)}) collective-permute-start(bf16[4,512,256]{2,1,0:T(8,128)(2,1)} %join.7.refs_0_.refs_1_), channel_id=1, source_target_pairs={{0,4},{4,0},{8,12},{12,8},{16,20},{20,16},{24,28},{28,24},{1,5},{5... | collective-permute-start | bytes 3145736 | tf_op jit(solution)/shard_map/ppermute | solution.py:37
  35.0 8.7 %collective-permute-start.10 = (bf16[1,704,128]{2,1,0:T(8,128)(2,1)S(1)}, bf16[1,704,128]{2,1,0:T(8,128)(2,1)S(1)}, u32[]{:S(2)}, u32[]{:S(2)}) collective-permute-start(bf16[1,704,128]{2,1,0:T(8,128)(2,1)S(1)} %slice.101.refs_0_), channel_id=1, source_target_pairs={{0,24},{4,28},{8,16},{12,20},{16,8},{20,12},{24,0},{28,4},{1,25},{... | collective-permute-start | bytes 540680 | tf_op jit(solution)/shard_map/ppermute | solution.py:65
  37.6 16.5 %collective-permute-start.9 = (bf16[1,704,128]{2,1,0:T(8,128)(2,1)S(1)}, bf16[1,704,128]{2,1,0:T(8,128)(2,1)S(1)}, u32[]{:S(2)}, u32[]{:S(2)}) collective-permute-start(bf16[1,704,128]{2,1,0:T(8,128)(2,1)S(1)} %slice.101.refs_0_), channel_id=1, source_target_pairs={{0,16},{4,20},{8,24},{12,28},{16,0},{20,4},{24,8},{28,12},{1,17},{... | collective-permute-start | bytes 540680 | tf_op jit(solution)/shard_map/ppermute | solution.py:65
  42.2 11.8 %collective-permute-start.8 = (bf16[1,704,128]{2,1,0:T(8,128)(2,1)S(1)}, bf16[1,704,128]{2,1,0:T(8,128)(2,1)S(1)}, u32[]{:S(2)}, u32[]{:S(2)}) collective-permute-start(bf16[1,704,128]{2,1,0:T(8,128)(2,1)S(1)} %slice.101.refs_0_), channel_id=1, source_target_pairs={{0,8},{4,12},{8,0},{12,4},{16,24},{20,28},{24,16},{28,20},{1,9},{5... | collective-permute-start | bytes 540680 | tf_op jit(solution)/shard_map/ppermute | solution.py:65
  54.0 21.6 %collective-permute-start.17 = (bf16[2,704,128]{2,1,0:T(8,128)(2,1)}, bf16[2,704,128]{2,1,0:T(8,128)(2,1)}, u32[]{:S(2)}, u32[]{:S(2)}) collective-permute-start(bf16[2,704,128]{2,1,0:T(8,128)(2,1)} %slice.102.refs_0_), channel_id=1, source_target_pairs={{0,24},{4,28},{8,16},{12,20},{16,8},{20,12},{24,0},{28,4},{1,25},{... | collective-permute-start | bytes 1081352 | tf_op jit(solution)/shard_map/ppermute | solution.py:65
  57.1 29.1 %collective-permute-start.16 = (bf16[2,704,128]{2,1,0:T(8,128)(2,1)}, bf16[2,704,128]{2,1,0:T(8,128)(2,1)}, u32[]{:S(2)}, u32[]{:S(2)}) collective-permute-start(bf16[2,704,128]{2,1,0:T(8,128)(2,1)} %slice.102.refs_0_), channel_id=1, source_target_pairs={{0,16},{4,20},{8,24},{12,28},{16,0},{20,4},{24,8},{28,12},{1,17},{... | collective-permute-start | bytes 1081352 | tf_op jit(solution)/shard_map/ppermute | solution.py:65
  70.1 28.5 %collective-permute-start.14 = (bf16[1,704,512]{2,1,0:T(8,128)(2,1)}, bf16[1,704,512]{2,1,0:T(8,128)(2,1)}, u32[]{:S(2)}, u32[]{:S(2)}) collective-permute-start(bf16[1,704,512]{2,1,0:T(8,128)(2,1)} %join.8.refs_1_), channel_id=1, source_target_pairs={{0,2},{1,3},{2,0},{3,1},{4,6},{5,7},{6,4},{7,5},{8,10},{9,11},{10,... | collective-permute-start | bytes 2162696 | tf_op jit(solution)/shard_map/ppermute | solution.py:83
  70.7 27.9 %collective-permute-start.13 = (bf16[1,704,512]{2,1,0:T(8,128)(2,1)}, bf16[1,704,512]{2,1,0:T(8,128)(2,1)}, u32[]{:S(2)}, u32[]{:S(2)}) collective-permute-start(bf16[1,704,512]{2,1,0:T(8,128)(2,1)} %join.8.refs_1_), channel_id=1, source_target_pairs={{0,4},{4,0},{8,12},{12,8},{16,20},{20,16},{24,28},{28,24},{1,5},{5... | collective-permute-start | bytes 2162696 | tf_op jit(solution)/shard_map/ppermute | solution.py:37
  74.1 24.5 %collective-permute-start.12 = (bf16[4,256,256]{2,1,0:T(8,128)(2,1)}, bf16[4,256,256]{2,1,0:T(8,128)(2,1)}, u32[]{:S(2)}, u32[]{:S(2)}) collective-permute-start(bf16[4,256,256]{2,1,0:T(8,128)(2,1)} %slice.104), channel_id=1, source_target_pairs={{0,2},{1,3},{2,0},{3,1},{4,6},{5,7},{6,4},{7,5},{8,10},{9,11},{10,... | collective-permute-start | bytes 1572872 | tf_op jit(solution)/shard_map/ppermute | solution.py:83
  75.6 23.0 %collective-permute-start.11 = (bf16[4,256,256]{2,1,0:T(8,128)(2,1)}, bf16[4,256,256]{2,1,0:T(8,128)(2,1)}, u32[]{:S(2)}, u32[]{:S(2)}) collective-permute-start(bf16[4,256,256]{2,1,0:T(8,128)(2,1)} %slice.103), channel_id=1, source_target_pairs={{0,4},{4,0},{8,12},{12,8},{16,20},{20,16},{24,28},{28,24},{1,5},{5... | collective-permute-start | bytes 1572872 | tf_op jit(solution)/shard_map/ppermute | solution.py:37
  86.1 12.4 %collective-permute-start.15 = (bf16[2,704,128]{2,1,0:T(8,128)(2,1)}, bf16[2,704,128]{2,1,0:T(8,128)(2,1)}, u32[]{:S(2)}, u32[]{:S(2)}) collective-permute-start(bf16[2,704,128]{2,1,0:T(8,128)(2,1)} %slice.102.refs_0_), channel_id=1, source_target_pairs={{0,8},{4,12},{8,0},{12,4},{16,24},{20,28},{24,16},{28,20},{1,9},{5... | collective-permute-start | bytes 1081352 | tf_op jit(solution)/shard_map/ppermute | solution.py:65
  119.8 12.5 %collective-permute-start.25 = (bf16[576,1024]{1,0:T(8,128)(2,1)S(1)}, bf16[576,1024]{1,0:T(8,128)(2,1)}, u32[]{:S(2)}, u32[]{:S(2)}) collective-permute-start(bf16[576,1024]{1,0:T(8,128)(2,1)S(1)} %fusion.3), channel_id=1, source_target_pairs={{0,1},{1,0},{2,3},{3,2},{4,5},{5,4},{6,7},{7,6},{8,9},{9,8},{10,11... | collective-permute-start | bytes 3538952 | tf_op jit(solution)/shard_map/ppermute | solution.py:42
  123.5 42.5 %collective-permute-start.20 = (bf16[2,704,512]{2,1,0:T(8,128)(2,1)}, bf16[2,704,512]{2,1,0:T(8,128)(2,1)S(1)}, u32[]{:S(2)}, u32[]{:S(2)}) collective-permute-start(bf16[2,704,512]{2,1,0:T(8,128)(2,1)} %join.9.refs_3_.refs_1_), channel_id=1, source_target_pairs={{0,2},{1,3},{2,0},{3,1},{4,6},{5,7},{6,4},{7,5},{8,10},{9,11},{10,... | collective-permute-start | bytes 4325384 | tf_op jit(solution)/shard_map/ppermute | solution.py:83
  125.7 41.5 %collective-permute-start.19 = (bf16[2,704,512]{2,1,0:T(8,128)(2,1)}, bf16[2,704,512]{2,1,0:T(8,128)(2,1)}, u32[]{:S(2)}, u32[]{:S(2)}) collective-permute-start(bf16[2,704,512]{2,1,0:T(8,128)(2,1)} %join.9.refs_3_.refs_1_), channel_id=1, source_target_pairs={{0,4},{4,0},{8,12},{12,8},{16,20},{20,16},{24,28},{28,24},{1,5},{5... | collective-permute-start | bytes 4325384 | tf_op jit(solution)/shard_map/ppermute | solution.py:37
  128.2 14.0 %collective-permute-start.23 = (bf16[6,2,128,128]{3,2,1,0:T(8,128)(2,1)S(1)}, bf16[6,2,128,128]{3,2,1,0:T(8,128)(2,1)S(1)}, u32[]{:S(2)}, u32[]{:S(2)}) collective-permute-start(bf16[6,2,128,128]{3,2,1,0:T(8,128)(2,1)S(1)} %pad_maximum_fusion.4.refs_0_), channel_id=1, source_target_pairs={{0,24},{4,28},{8,16},{12,20},{16,8},{20,12},{24,0},{28,4},{1,25},{... | collective-permute-start | bytes 1179656 | tf_op jit(solution)/shard_map/ppermute | solution.py:65
  129.3 36.6 %collective-permute-start.22 = (bf16[6,2,128,128]{3,2,1,0:T(8,128)(2,1)S(1)}, bf16[6,2,128,128]{3,2,1,0:T(8,128)(2,1)S(1)}, u32[]{:S(2)}, u32[]{:S(2)}) collective-permute-start(bf16[6,2,128,128]{3,2,1,0:T(8,128)(2,1)S(1)} %pad_maximum_fusion.4.refs_0_), channel_id=1, source_target_pairs={{0,16},{4,20},{8,24},{12,28},{16,0},{20,4},{24,8},{28,12},{1,17},{... | collective-permute-start | bytes 1179656 | tf_op jit(solution)/shard_map/ppermute | solution.py:65
  132.2 33.8 %collective-permute-start.21 = (bf16[6,2,128,128]{3,2,1,0:T(8,128)(2,1)S(1)}, bf16[6,2,128,128]{3,2,1,0:T(8,128)(2,1)S(1)}, u32[]{:S(2)}, u32[]{:S(2)}) collective-permute-start(bf16[6,2,128,128]{3,2,1,0:T(8,128)(2,1)S(1)} %pad_maximum_fusion.4.refs_0_), channel_id=1, source_target_pairs={{0,8},{4,12},{8,0},{12,4},{16,24},{20,28},{24,16},{28,20},{1,9},{5... | collective-permute-start | bytes 1179656 | tf_op jit(solution)/shard_map/ppermute | solution.py:65
  167.2 39.6 %collective-permute-start.26 = (bf16[2,704,512]{2,1,0:T(8,128)(2,1)}, bf16[2,704,512]{2,1,0:T(8,128)(2,1)}, u32[]{:S(2)}, u32[]{:S(2)}) collective-permute-start(bf16[2,704,512]{2,1,0:T(8,128)(2,1)} %collective-permute-done.19.refs_4_.refs_2_), channel_id=1, source_target_pairs={{0,2},{1,3},{2,0},{3,1},{4,6},{5,7},{6,4},{7,5},{8,10},{9,11},{10,... | collective-permute-start | bytes 4325384 | tf_op jit(solution)/shard_map/ppermute | solution.py:83
  176.5 18.7 %collective-permute-start.18 = (bf16[1,704,512]{2,1,0:T(8,128)(2,1)}, bf16[1,704,512]{2,1,0:T(8,128)(2,1)S(1)}, u32[]{:S(2)}, u32[]{:S(2)}) collective-permute-start(bf16[1,704,512]{2,1,0:T(8,128)(2,1)} %collective-permute-done.14.refs_1_), channel_id=1, source_target_pairs={{0,4},{4,0},{8,12},{12,8},{16,20},{20,16},{24,28},{28,24},{1,5},{5... | collective-permute-start | bytes 2162696 | tf_op jit(solution)/shard_map/ppermute | solution.py:37
  177.5 19.8 %collective-permute-start.32 = (bf16[2,128,256]{2,1,0:T(8,128)(2,1)S(1)}, bf16[2,128,256]{2,1,0:T(8,128)(2,1)S(1)}, u32[]{:S(2)}, u32[]{:S(2)}) collective-permute-start(bf16[2,128,256]{2,1,0:T(8,128)(2,1)S(1)} %copy-done.59), channel_id=1, source_target_pairs={{0,24},{4,28},{8,16},{12,20},{16,8},{20,12},{24,0},{28,4},{1,25},{... | collective-permute-start | bytes 393224 | tf_op jit(solution)/shard_map/ppermute | solution.py:65
  178.6 27.4 %collective-permute-start.31 = (bf16[2,128,256]{2,1,0:T(8,128)(2,1)S(1)}, bf16[2,128,256]{2,1,0:T(8,128)(2,1)S(1)}, u32[]{:S(2)}, u32[]{:S(2)}) collective-permute-start(bf16[2,128,256]{2,1,0:T(8,128)(2,1)S(1)} %copy-done.59), channel_id=1, source_target_pairs={{0,16},{4,20},{8,24},{12,28},{16,0},{20,4},{24,8},{28,12},{1,17},{... | collective-permute-start | bytes 393224 | tf_op jit(solution)/shard_map/ppermute | solution.py:65
  178.6 27.4 %collective-permute-start.30 = (bf16[2,128,256]{2,1,0:T(8,128)(2,1)S(1)}, bf16[2,128,256]{2,1,0:T(8,128)(2,1)S(1)}, u32[]{:S(2)}, u32[]{:S(2)}) collective-permute-start(bf16[2,128,256]{2,1,0:T(8,128)(2,1)S(1)} %copy-done.59), channel_id=1, source_target_pairs={{0,8},{4,12},{8,0},{12,4},{16,24},{20,28},{24,16},{28,20},{1,9},{5... | collective-permute-start | bytes 393224 | tf_op jit(solution)/shard_map/ppermute | solution.py:65
  196.1 10.0 %collective-permute-start.29 = (bf16[64,1024]{1,0:T(8,128)(2,1)S(1)}, bf16[64,1024]{1,0:T(8,128)(2,1)S(1)}, u32[]{:S(2)}, u32[]{:S(2)}) collective-permute-start(bf16[64,1024]{1,0:T(8,128)(2,1)S(1)} %get-tuple-element.138), channel_id=1, source_target_pairs={{0,2},{1,3},{2,0},{3,1},{4,6},{5,7},{6,4},{7,5},{8,10},{9,11},{10,... | collective-permute-start | bytes 393224 | tf_op jit(solution)/shard_map/ppermute | solution.py:83
  208.7 16.8 %collective-permute-start.36 = (bf16[2,512,256]{2,1,0:T(8,128)(2,1)}, bf16[2,512,256]{2,1,0:T(8,128)(2,1)S(1)}, u32[]{:S(2)}, u32[]{:S(2)}) collective-permute-start(bf16[2,512,256]{2,1,0:T(8,128)(2,1)} %join.11.refs_3_), channel_id=1, source_target_pairs={{0,2},{1,3},{2,0},{3,1},{4,6},{5,7},{6,4},{7,5},{8,10},{9,11},{10,... | collective-permute-start | bytes 1572872 | tf_op jit(solution)/shard_map/ppermute | solution.py:83
  209.9 15.7 %collective-permute-start.35 = (bf16[2,512,256]{2,1,0:T(8,128)(2,1)}, bf16[2,512,256]{2,1,0:T(8,128)(2,1)S(1)}, u32[]{:S(2)}, u32[]{:S(2)}) collective-permute-start(bf16[2,512,256]{2,1,0:T(8,128)(2,1)} %join.11.refs_3_), channel_id=1, source_target_pairs={{0,4},{4,0},{8,12},{12,8},{16,20},{20,16},{24,28},{28,24},{1,5},{5... | collective-permute-start | bytes 1572872 | tf_op jit(solution)/shard_map/ppermute | solution.py:37
  211.0 13.8 %collective-permute-start.33 = (bf16[64,1024]{1,0:T(8,128)(2,1)S(1)}, bf16[64,1024]{1,0:T(8,128)(2,1)S(1)}, u32[]{:S(2)}, u32[]{:S(2)}) collective-permute-start(bf16[64,1024]{1,0:T(8,128)(2,1)S(1)} %add_convert_fusion.6), channel_id=1, source_target_pairs={{0,2},{1,3},{2,0},{3,1},{4,6},{5,7},{6,4},{7,5},{8,10},{9,11},{10,... | collective-permute-start | bytes 393224 | tf_op jit(solution)/shard_map/ppermute | solution.py:83
  212.3 13.2 %collective-permute-start.34 = (bf16[64,1024]{1,0:T(8,128)(2,1)S(1)}, bf16[64,1024]{1,0:T(8,128)(2,1)S(1)}, u32[]{:S(2)}, u32[]{:S(2)}) collective-permute-start(bf16[64,1024]{1,0:T(8,128)(2,1)S(1)} %add_convert_fusion.5), channel_id=1, source_target_pairs={{0,4},{4,0},{8,12},{12,8},{16,20},{20,16},{24,28},{28,24},{1,5},{5... | collective-permute-start | bytes 393224 | tf_op jit(solution)/shard_map/ppermute | solution.py:37
  227.9 14.7 %collective-permute-start.42 = (bf16[2,256,256]{2,1,0:T(8,128)(2,1)S(1)}, bf16[2,256,256]{2,1,0:T(8,128)(2,1)S(1)}, u32[]{:S(2)}, u32[]{:S(2)}) collective-permute-start(bf16[2,256,256]{2,1,0:T(8,128)(2,1)S(1)} %slice.113), channel_id=1, source_target_pairs={{0,2},{1,3},{2,0},{3,1},{4,6},{5,7},{6,4},{7,5},{8,10},{9,11},{10,... | collective-permute-start | bytes 786440 | tf_op jit(solution)/shard_map/ppermute | solution.py:83
  228.9 13.7 %collective-permute-start.41 = (bf16[2,256,256]{2,1,0:T(8,128)(2,1)S(1)}, bf16[2,256,256]{2,1,0:T(8,128)(2,1)S(1)}, u32[]{:S(2)}, u32[]{:S(2)}) collective-permute-start(bf16[2,256,256]{2,1,0:T(8,128)(2,1)S(1)} %slice.112), channel_id=1, source_target_pairs={{0,4},{4,0},{8,12},{12,8},{16,20},{20,16},{24,28},{28,24},{1,5},{5... | collective-permute-start | bytes 786440 | tf_op jit(solution)/shard_map/ppermute | solution.py:37
  230.8 11.9 %collective-permute-start.40 = (bf16[256,128]{1,0:T(8,128)(2,1)S(1)}, bf16[256,128]{1,0:T(8,128)(2,1)S(1)}, u32[]{:S(2)}, u32[]{:S(2)}) collective-permute-start(bf16[256,128]{1,0:T(8,128)(2,1)S(1)} %convolution_convert_fusion.1.refs_0_), channel_id=1, source_target_pairs={{0,24},{4,28},{8,16},{12,20},{16,8},{20,12},{24,0},{28,4},{1,25},{... | collective-permute-start | bytes 196616 | tf_op jit(solution)/shard_map/ppermute | solution.py:65
  231.9 10.8 %collective-permute-start.39 = (bf16[256,128]{1,0:T(8,128)(2,1)S(1)}, bf16[256,128]{1,0:T(8,128)(2,1)S(1)}, u32[]{:S(2)}, u32[]{:S(2)}) collective-permute-start(bf16[256,128]{1,0:T(8,128)(2,1)S(1)} %convolution_convert_fusion.1.refs_0_), channel_id=1, source_target_pairs={{0,16},{4,20},{8,24},{12,28},{16,0},{20,4},{24,8},{28,12},{1,17},{... | collective-permute-start | bytes 196616 | tf_op jit(solution)/shard_map/ppermute | solution.py:65
  231.9 10.8 %collective-permute-start.38 = (bf16[256,128]{1,0:T(8,128)(2,1)S(1)}, bf16[256,128]{1,0:T(8,128)(2,1)S(1)}, u32[]{:S(2)}, u32[]{:S(2)}) collective-permute-start(bf16[256,128]{1,0:T(8,128)(2,1)S(1)} %convolution_convert_fusion.1.refs_0_), channel_id=1, source_target_pairs={{0,8},{4,12},{8,0},{12,4},{16,24},{20,28},{24,16},{28,20},{1,9},{5... | collective-permute-start | bytes 196616 | tf_op jit(solution)/shard_map/ppermute | solution.py:65
  250.6 52.9 %collective-permute-start.48 = (bf16[576,1024]{1,0:T(8,128)(2,1)}, bf16[576,1024]{1,0:T(8,128)(2,1)}, u32[]{:S(2)}, u32[]{:S(2)}) collective-permute-start(bf16[576,1024]{1,0:T(8,128)(2,1)} %fusion.1), channel_id=1, source_target_pairs={{0,1},{1,0},{2,3},{3,2},{4,5},{5,4},{6,7},{7,6},{8,9},{9,8},{10,11... | collective-permute-start | bytes 3538952 | tf_op jit(solution)/shard_map/ppermute | solution.py:42
  250.8 17.2 %collective-permute-start.51 = (bf16[6,352,128]{2,1,0:T(8,128)(2,1)S(1)}, bf16[6,352,128]{2,1,0:T(8,128)(2,1)S(1)}, u32[]{:S(2)}, u32[]{:S(2)}) collective-permute-start(bf16[6,352,128]{2,1,0:T(8,128)(2,1)S(1)} %bitcast.109), channel_id=1, source_target_pairs={{0,24},{4,28},{8,16},{12,20},{16,8},{20,12},{24,0},{28,4},{1,25},{... | collective-permute-start | bytes 1622024 | tf_op jit(solution)/shard_map/ppermute | solution.py:65
  253.6 8.6 %collective-permute-start.44 = (bf16[1024,128]{1,0:T(8,128)(2,1)}, bf16[1024,128]{1,0:T(8,128)(2,1)S(1)}, u32[]{:S(2)}, u32[]{:S(2)}) collective-permute-start(bf16[1024,128]{1,0:T(8,128)(2,1)} %join.12), channel_id=1, source_target_pairs={{0,2},{1,3},{2,0},{3,1},{4,6},{5,7},{6,4},{7,5},{8,10},{9,11},{10,... | collective-permute-start | bytes 786440 | tf_op jit(solution)/shard_map/ppermute | solution.py:83
  255.0 8.2 %collective-permute-start.43 = (bf16[1024,128]{1,0:T(8,128)(2,1)}, bf16[1024,128]{1,0:T(8,128)(2,1)S(1)}, u32[]{:S(2)}, u32[]{:S(2)}) collective-permute-start(bf16[1024,128]{1,0:T(8,128)(2,1)} %join.12), channel_id=1, source_target_pairs={{0,4},{4,0},{8,12},{12,8},{16,20},{20,16},{24,28},{28,24},{1,5},{5... | collective-permute-start | bytes 786440 | tf_op jit(solution)/shard_map/ppermute | solution.py:37
  255.5 44.1 %collective-permute-start.50 = (bf16[6,352,128]{2,1,0:T(8,128)(2,1)S(1)}, bf16[6,352,128]{2,1,0:T(8,128)(2,1)S(1)}, u32[]{:S(2)}, u32[]{:S(2)}) collective-permute-start(bf16[6,352,128]{2,1,0:T(8,128)(2,1)S(1)} %bitcast.110), channel_id=1, source_target_pairs={{0,16},{4,20},{8,24},{12,28},{16,0},{20,4},{24,8},{28,12},{1,17},{... | collective-permute-start | bytes 1622024 | tf_op jit(solution)/shard_map/ppermute | solution.py:65
  262.2 38.3 %collective-permute-start.49 = (bf16[6,352,128]{2,1,0:T(8,128)(2,1)S(1)}, bf16[6,352,128]{2,1,0:T(8,128)(2,1)}, u32[]{:S(2)}, u32[]{:S(2)}) collective-permute-start(bf16[6,352,128]{2,1,0:T(8,128)(2,1)S(1)} %bitcast.111), channel_id=1, source_target_pairs={{0,8},{4,12},{8,0},{12,4},{16,24},{20,28},{24,16},{28,20},{1,9},{5... | collective-permute-start | bytes 1622024 | tf_op jit(solution)/shard_map/ppermute | solution.py:65
  263.2 40.2 %collective-permute-start.45 = (bf16[512,128]{1,0:T(8,128)(2,1)S(1)}, bf16[512,128]{1,0:T(8,128)(2,1)S(1)}, u32[]{:S(2)}, u32[]{:S(2)}) collective-permute-start(bf16[512,128]{1,0:T(8,128)(2,1)S(1)} %slice.136), channel_id=1, source_target_pairs={{0,4},{4,0},{8,12},{12,8},{16,20},{20,16},{24,28},{28,24},{1,5},{5... | collective-permute-start | bytes 393224 | tf_op jit(solution)/shard_map/ppermute | solution.py:37
  268.0 35.4 %collective-permute-start.46 = (bf16[512,128]{1,0:T(8,128)(2,1)S(1)}, bf16[512,128]{1,0:T(8,128)(2,1)S(1)}, u32[]{:S(2)}, u32[]{:S(2)}) collective-permute-start(bf16[512,128]{1,0:T(8,128)(2,1)S(1)} %slice.137), channel_id=1, source_target_pairs={{0,2},{1,3},{2,0},{3,1},{4,6},{5,7},{6,4},{7,5},{8,10},{9,11},{10,... | collective-permute-start | bytes 393224 | tf_op jit(solution)/shard_map/ppermute | solution.py:83
  314.5 14.4 %collective-permute-start.52 = (bf16[4,2,272,128]{3,2,1,0:T(8,128)(2,1)}, bf16[4,2,272,128]{3,2,1,0:T(8,128)(2,1)}, u32[]{:S(2)}, u32[]{:S(2)}) collective-permute-start(bf16[4,2,272,128]{3,2,1,0:T(8,128)(2,1)} %cross_block.3), channel_id=1, source_target_pairs={{0,2},{1,3},{2,0},{3,1},{4,6},{5,7},{6,4},{7,5},{8,10},{9,11},{10,... | collective-permute-start | bytes 1671176 | tf_op jit(solution)/shard_map/ppermute | solution.py:83
  (88 other events, 766.1 us)

commit v2 on v1

--- a/solution.py
+++ b/solution.py
@@ -900,20 +900,23 @@
     if size_y == 2 and cross_q.shape[1] == LANES:
         side, over = swap_x(cross_q), swap_y(cross_q)
         half = cross_q.shape[0] // 2
-        far = jnp.concatenate([swap_x(over[:half]), swap_y(side[half:])], axis=0)
+        far = (swap_x(over[:half]), swap_y(side[half:]))
+        far = jnp.concatenate(far, axis=0)
         cross_q = [[q.reshape(shape) for q in pair] for pair in ((cross_q, side), (over, far))]
     else:
         cross_q = in_order(x == 0, cross_q, swap_x(cross_q), 1)
         cross_q = [[q] for q in gather_y(cross_q.reshape(shape))]
     second_rows = (first_rows.astype(F32) + core_rows_sum(partial, core)).astype(BF16)
-    normed = both_cores(rms_normed(second_rows), core)
+    normed = rms_normed(second_rows)
+    dec_ff = join(dec_ff_z, 2)
+    normed = both_cores(normed, core)
     cross_weights = attn_pieces(cross_block_z, cross_near, cross_far)
 
     begin = jnp.clip(starts - row_begin, 0, rows)
     end = jnp.clip(ends - row_begin, 0, rows)
     questions = slot_question[0]
     questions = z_place(questions // 2) * 2 + questions % 2
-    cross_q, normed, dec_ff = meet(cross_q, normed, join(dec_ff_z, 2))
+    cross_q, normed, dec_ff = meet(cross_q, normed, dec_ff)
 
     def answer_part(index):
         sums = cross_block(
@@ -921,16 +924,24 @@
         )
         return by_column_x(sums, length)
 
+    def of_x(values, index):
+        return lax.dynamic_index_in_dim(values, index, 1, keepdims=False)
+
     if size_y == 2:
         other = answer_part(1)
-        other = swap_y(other)
+        other_far = swap_y(of_x(other, 1 - x))
+        other_near = of_x(other, x)
         own = answer_part(0)
-        summed = own.astype(F32) + other.astype(F32)
+        own, other_near = meet(own, other_near)
+        other_near = swap_y(other_near)
+        far = of_x(own, 1 - x).astype(F32) + other_far.astype(F32)
+        far = swap_x(far.astype(BF16))
+        summed = of_x(own, x).astype(F32) + other_near.astype(F32) + far.astype(F32)
     else:
         packed = [answer_part(index) for index in range(size_y)]
         summed = packed[0].astype(F32) if size_y == 1 else scatter_y_sum(jnp.stack(packed))
-    other = swap_x(lax.dynamic_index_in_dim(summed, 1 - x, 1, keepdims=False).astype(BF16))
-    summed = lax.dynamic_index_in_dim(summed, x, 1, keepdims=False) + other.astype(F32)
+        far = swap_x(of_x(summed, 1 - x).astype(BF16))
+        summed = of_x(summed, x) + far.astype(F32)
     if few_z():
         own = summed[0]
         for step in range(1, size_z):

time: 380 us -> 373 us (0.982)
  waiting for transfers between devices: 164 us -> 157 us
    ppermute x18, waiting for transfers between devices: 37.8 us -> 32.3 us  [swap_x(): return lax.ppermute(value, 'dp', [(i, i ^ 1) for i in range(count)])]
    unnamed x143 -> x113, local copies, waits for them, and re-layouts: 14.7 us -> 12 us
    ppermute x15 -> x16, waiting for transfers between devices: 20.8 us -> 18.5 us  [swap_y(): return lax.ppermute(value, 'mp', [(i, i ^ 2) for i in range(4)])]
    ppermute x15 -> x16, starting transfers between devices: 17.7 us -> 18.2 us  [swap_y(): return lax.ppermute(value, 'mp', [(i, i ^ 2) for i in range(4)])]
  transfers between devices with their start and end apart: 67 -> 68, of which waited for: 30 -> 30; matrix products, arithmetic and copies ran while one was open for 5% -> 6% of each run, Pallas kernels for 17% -> 17%
where the time goes in v2:
time: 373 us; the launch traced here: 371 us
  waiting for transfers between devices  157 us (42%)
  Pallas kernels  90.7 us (24%)
  starting transfers between devices  74.1 us (20%)
  local copies, waits for them, and re-layouts  26.5 us (7%)
  other arithmetic  21.7 us (6%)
    ppermute x24, waiting for transfers between devices, swap_z(): return lax.ppermute(value, 'dp', [(i, i ^ 2 * step) for i in range(count)])  96.2 us
    ppermute x24, starting transfers between devices, swap_z(): return lax.ppermute(value, 'dp', [(i, i ^ 2 * step) for i in range(count)])  35.2 us
    ppermute x18, waiting for transfers between devices, swap_x(): return lax.ppermute(value, 'dp', [(i, i ^ 1) for i in range(count)])  32.3 us
    pallas_call x4, Pallas kernels, ff(): pl.pallas_call(functools.partial(ff_kernel, chunks=plan, done=before, las...  22 us
    pallas_call x2, Pallas kernels, enc_block(): pl.pallas_call(functools.partial(enc_block_kernel, rows=query_rows), out_...  21.1 us
    ppermute x18, starting transfers between devices, swap_x(): return lax.ppermute(value, 'dp', [(i, i ^ 1) for i in range(count)])  19.3 us
    ppermute x16, waiting for transfers between devices, swap_y(): return lax.ppermute(value, 'mp', [(i, i ^ 2) for i in range(4)])  18.5 us
    ppermute x16, starting transfers between devices, swap_y(): return lax.ppermute(value, 'mp', [(i, i ^ 2) for i in range(4)])  18.2 us
  transfers between devices with their start and end apart: 68, of which 30 were waited for; matrix products, arithmetic and copies ran while one was open for 6% of the time, Pallas kernels for 17%

profile of v2, /device:TPU:0, one launch (start us, length us, event | category | flops | bytes accessed | tf_op | source)
XLA Modules:
  0.0 371.4 jit_solution(6186927258309881399)
XLA Ops:
  1.8 3.0 collective-permute-start.3
  6.5 2.0 collective-permute-start.5
  8.6 2.6 collective-permute-start.1
  14.7 6.3 %collective-permute-done.5 = bf16[128,1024]{1,0:T(8,128)(2,1)S(1)} collective-permute-done((bf16[128,1024]{1,0:T(8,128)(2,1)}, bf16[128,1024]{1,0:T(8,128)(2,1)S(1)}, u32[]{:S(2)}, u32[]{:S(2)}) %collective-permute-start.5) | collective-permute-done | bytes 262176 | tf_op jit(solution)/shard_map/ppermute | solution.py:37
  21.1 4.5 %collective-permute-done.1.refs_2_ = bf16[4,128,256]{2,1,0:T(8,128)(2,1)S(1)} collective-permute-done((bf16[4,128,256]{2,1,0:T(8,128)(2,1)}, bf16[4,128,256]{2,1,0:T(8,128)(2,1)S(1)}, u32[]{:S(2)}, u32[]{:S(2)}) %collective-permute-start.1) | collective-permute-done | bytes 262176 | tf_op jit(solution)/shard_map/ppermute | solution.py:65
  25.6 3.7 collective-permute-done.2.refs_3_
  30.1 2.2 join.7.refs_0_.refs_1_
  35.1 2.5 collective-permute-start.10
  37.7 4.7 %collective-permute-start.9 = (bf16[1,704,128]{2,1,0:T(8,128)(2,1)S(1)}, bf16[1,704,128]{2,1,0:T(8,128)(2,1)S(1)}, u32[]{:S(2)}, u32[]{:S(2)}) collective-permute-start(bf16[1,704,128]{2,1,0:T(8,128)(2,1)S(1)} %slice.101.refs_0_), channel_id=1, source_target_pairs={{0,16},{4,20},{8,24},{12,28},{16,0},{20,4},{24,8},{28,12},{1,17},{... | collective-permute-start | bytes 540680 | tf_op jit(solution)/shard_map/ppermute | solution.py:65
  43.9 10.3 %collective-permute-done.9.refs_2_ = bf16[1,704,128]{2,1,0:T(8,128)(2,1)S(1)} collective-permute-done((bf16[1,704,128]{2,1,0:T(8,128)(2,1)S(1)}, bf16[1,704,128]{2,1,0:T(8,128)(2,1)S(1)}, u32[]{:S(2)}, u32[]{:S(2)}) %collective-permute-start.9) | collective-permute-done | bytes 180256 | tf_op jit(solution)/shard_map/ppermute | solution.py:65
  54.2 3.0 collective-permute-start.17
  57.4 9.9 %prepare.1 = (bf16[1408,1024]{1,0:T(8,128)(2,1)}, bf16[1408,1024]{1,0:T(8,128)(2,1)}) custom-call(s32[1]{0:T(128)} %bitcast.3.begin_ref, s32[8]{0:T(128)} %stack.78.order_ref, bf16[2304,1024]{1,0:T(8,128)(2,1)} %x_ref), custom_call_target="tpu_custom_call" | custom-call | flops 5767168 | bytes 8650752 | tf_op jit(solution)/shard_map/prepare/pallas_call | solution.py:350
  67.4 2.9 join.8.refs_1_
  76.2 10.0 %collective-permute-done.16.refs_2_ = bf16[2,704,128]{2,1,0:T(8,128)(2,1)} collective-permute-done((bf16[2,704,128]{2,1,0:T(8,128)(2,1)}, bf16[2,704,128]{2,1,0:T(8,128)(2,1)}, u32[]{:S(2)}, u32[]{:S(2)}) %collective-permute-start.16) | collective-permute-done | bytes 360480 | tf_op jit(solution)/shard_map/ppermute | solution.py:65
  88.5 10.2 %enc_block.2.refs_0_ = bf16[1152,256]{1,0:T(8,128)(2,1)S(1)} custom-call(s32[3]{0:T(128)S(1)} %get-tuple-element.231.low_ref, s32[3]{0:T(128)S(1)} %get-tuple-element.230.high_ref, s32[1]{0:T(128)} %bitcast.14.first_ref, s32[1152,128]{1,0:T(8,128)S(1)} %broadcast_in_dim.27.seg_q_ref, s32[11,1,128]{2,1,0:T(1,128)S(1)} %reshape.182.seg_k_ref, ...), custom_call_target="tpu_custom_call" | custom-call | flops 3321888768 | bytes 2883584 | tf_op jit(solution)/shard_map/enc_block/pallas_call | solution.py:474
  98.8 10.9 %enc_block.3.refs_3_ = bf16[1152,256]{1,0:T(8,128)(2,1)S(1)} custom-call(s32[3]{0:T(128)S(1)} %get-tuple-element.231.low_ref, s32[3]{0:T(128)S(1)} %get-tuple-element.230.high_ref, s32[1]{0:T(128)} %bitcast.14.first_ref, s32[1152,128]{1,0:T(8,128)S(1)} %broadcast_in_dim.27.seg_q_ref, s32[11,1,128]{2,1,0:T(1,128)S(1)} %reshape.182.seg_k_ref, ...), custom_call_target="tpu_custom_call" | custom-call | flops 3321888768 | bytes 2883584 | tf_op jit(solution)/shard_map/enc_block/pallas_call | solution.py:474
  110.9 3.0 out_project.1
  114.3 2.9 collective-permute-done.24
  117.1 2.4 fusion.2
  121.2 2.5 join.9.refs_3_.refs_1_
  123.7 2.2 collective-permute-start.20
  128.9 2.9 collective-permute-start.22
  135.7 6.1 %collective-permute-done.23.refs_3_ = bf16[6,2,128,128]{3,2,1,0:T(8,128)(2,1)S(1)} collective-permute-done((bf16[6,2,128,128]{3,2,1,0:T(8,128)(2,1)S(1)}, bf16[6,2,128,128]{3,2,1,0:T(8,128)(2,1)S(1)}, u32[]{:S(2)}, u32[]{:S(2)}) %collective-permute-start.23) | collective-permute-done | bytes 393248 | tf_op jit(solution)/shard_map/ppermute | solution.py:65
  141.8 23.7 %collective-permute-done.22.refs_2_ = bf16[6,2,128,128]{3,2,1,0:T(8,128)(2,1)S(1)} collective-permute-done((bf16[6,2,128,128]{3,2,1,0:T(8,128)(2,1)S(1)}, bf16[6,2,128,128]{3,2,1,0:T(8,128)(2,1)S(1)}, u32[]{:S(2)}, u32[]{:S(2)}) %collective-permute-start.22) | collective-permute-done | bytes 393248 | tf_op jit(solution)/shard_map/ppermute | solution.py:65
  168.7 2.5 join.10
  171.2 3.7 %self_block.1 = bf16[256,1024]{1,0:T(8,128)(2,1)} custom-call(bf16[256,1024]{1,0:T(8,128)(2,1)} %fusion.6.x_ref, bf16[6,1024,128]{2,1,0:T(8,128)(2,1)} %bitcast.114), custom_call_target="tpu_custom_call" | custom-call | flops 268435456 | bytes 1572864 | tf_op jit(solution)/shard_map/self_block/pallas_call | solution.py:678
  178.2 3.3 collective-permute-start.30
  182.5 12.3 %collective-permute-done.18.refs_2_ = bf16[1,704,512]{2,1,0:T(8,128)(2,1)S(1)} collective-permute-done((bf16[1,704,512]{2,1,0:T(8,128)(2,1)}, bf16[1,704,512]{2,1,0:T(8,128)(2,1)S(1)}, u32[]{:S(2)}, u32[]{:S(2)}) %collective-permute-start.18) | collective-permute-done | bytes 720928 | tf_op jit(solution)/shard_map/ppermute | solution.py:37
  197.7 6.1 %ff.4.refs_0_ = bf16[1152,704]{1,0:T(8,128)(2,1)S(1)} custom-call(bf16[1152,1024]{1,0:T(8,128)(2,1)} %pad_maximum_fusion.refs_0_, bf16[1,704,512]{2,1,0:T(8,128)(2,1)S(1)} %copy-done.7, bf16[1,704,512]{2,1,0:T(8,128)(2,1)} %collective-permute-done.13.refs_2_, bf16[2,704,512]{2,1,0:T(8,128)(2,1)S(1)} %copy-done.6, ...), custom_call_target="tpu_custom_call" | custom-call | flops 3321888768 | bytes 3981312 | tf_op jit(solution)/shard_map/ff/pallas_call | solution.py:253
  215.8 6.2 %ff.5.refs_3_ = bf16[1152,704]{1,0:T(8,128)(2,1)S(1)} custom-call(bf16[1152,1024]{1,0:T(8,128)(2,1)} %pad_maximum_fusion.refs_0_, bf16[1,704,512]{2,1,0:T(8,128)(2,1)} %collective-permute-done.14.refs_1_, bf16[1,704,512]{2,1,0:T(8,128)(2,1)S(1)} %collective-permute-done.18.refs_2_, bf16[2,704,512]{2,1,0:T(8,128)(2,1)S(1)} %copy-done.13, ...), custom_call_target="tpu_custom_call" | custom-call | flops 3321888768 | bytes 3981312 | tf_op jit(solution)/shard_map/ff/pallas_call | solution.py:253
  222.0 2.3 collective-permute-done.33
  230.5 3.3 collective-permute-start.38
  233.8 7.4 %ff.6 = bf16[1152,1024]{1,0:T(8,128)(2,1)} custom-call(bf16[1152,704]{1,0:T(8,128)(2,1)} %copy-done.15, bf16[2,704,512]{2,1,0:T(8,128)(2,1)S(1)} %copy-done.6, bf16[2,704,512]{2,1,0:T(8,128)(2,1)} %collective-permute-done.19.refs_4_.refs_2_, bf16[1152,704]{1,0:T(8,128)(2,1)} %copy-done.16, bf16[2,704,512]{2,1,0:T(8,128)(2,1)S(1)} %copy-done.14, ...), custom_call_target="tpu_custom_call" | custom-call | flops 3321888768 | bytes 4718592 | tf_op jit(solution)/shard_map/ff/pallas_call | solution.py:253
  242.9 2.8 collective-permute-done.47
  254.3 6.3 %collective-permute-done.44 = bf16[1024,128]{1,0:T(8,128)(2,1)S(1)} collective-permute-done((bf16[1024,128]{1,0:T(8,128)(2,1)}, bf16[1024,128]{1,0:T(8,128)(2,1)S(1)}, u32[]{:S(2)}, u32[]{:S(2)}) %collective-permute-start.44) | collective-permute-done | bytes 262176 | tf_op jit(solution)/shard_map/ppermute | solution.py:83
  262.2 4.3 %collective-permute-done.51.refs_3_ = bf16[6,352,128]{2,1,0:T(8,128)(2,1)} collective-permute-done((bf16[6,352,128]{2,1,0:T(8,128)(2,1)S(1)}, bf16[6,352,128]{2,1,0:T(8,128)(2,1)}, u32[]{:S(2)}, u32[]{:S(2)}) %collective-permute-start.51) | collective-permute-done | bytes 540704 | tf_op jit(solution)/shard_map/ppermute | solution.py:65
  269.3 28.8 %collective-permute-done.50.refs_2_ = bf16[6,352,128]{2,1,0:T(8,128)(2,1)S(1)} collective-permute-done((bf16[6,352,128]{2,1,0:T(8,128)(2,1)S(1)}, bf16[6,352,128]{2,1,0:T(8,128)(2,1)S(1)}, u32[]{:S(2)}, u32[]{:S(2)}) %collective-permute-start.50) | collective-permute-done | bytes 540704 | tf_op jit(solution)/shard_map/ppermute | solution.py:65
  298.9 3.0 join.13.refs_1_
  302.9 2.2 broadcast_select_fusion.1
  305.3 7.1 %cross_block.3 = bf16[4,2,272,128]{3,2,1,0:T(8,128)(2,1)S(1)} custom-call(s32[2]{0:T(128)S(1)} %pad_add_fusion.active_ref, s32[24]{0:T(128)S(1)} %get-tuple-element.181.begin_ref, s32[24]{0:T(128)S(1)} %get-tuple-element.182.end_ref, s32[24]{0:T(128)S(1)} %fusion.44.question_ref, s32[1]{0:T(128)} %bitcast.22.x_ref, bf16[8,128,128]{2,1,0:T(8,128)(2,1)S(1)} %bitcast.113, ...), custom_call_target="tpu_custom_call" | custom-call | flops 1811939328 | bytes 2359296 | tf_op jit(solution)/shard_map/cross_block/pallas_call | solution.py:622
  313.5 7.1 %cross_block.2 = bf16[4,2,272,128]{3,2,1,0:T(8,128)(2,1)S(1)} custom-call(s32[2]{0:T(128)S(1)} %pad_add_fusion.active_ref, s32[24]{0:T(128)S(1)} %get-tuple-element.181.begin_ref, s32[24]{0:T(128)S(1)} %get-tuple-element.182.end_ref, s32[24]{0:T(128)S(1)} %fusion.44.question_ref, s32[1]{0:T(128)} %bitcast.22.x_ref, bf16[8,128,128]{2,1,0:T(8,128)(2,1)S(1)} %bitcast.110, ...), custom_call_target="tpu_custom_call" | custom-call | flops 1811939328 | bytes 2359296 | tf_op jit(solution)/shard_map/cross_block/pallas_call | solution.py:622
  323.4 5.1 %collective-permute-done.52 = bf16[4,272,128]{2,1,0:T(8,128)(2,1)S(1)} collective-permute-done((bf16[4,272,128]{2,1,0:T(8,128)(2,1)S(1)}, bf16[4,272,128]{2,1,0:T(8,128)(2,1)S(1)}, u32[]{:S(2)}, u32[]{:S(2)}) %collective-permute-start.52) | collective-permute-done | bytes 278560 | tf_op jit(solution)/shard_map/ppermute | solution.py:83
  329.7 2.2 collective-permute-start.57
  342.2 3.6 collective-permute-done.59
  348.5 3.3 collective-permute-done.62
  354.8 2.3 ff.7
  361.9 4.3 %collective-permute-done.66 = bf16[128,2,2,128]{0,3,1,2:T(8,128)(2,1)S(1)} collective-permute-done((bf16[128,2,2,128]{0,3,1,2:T(8,128)(2,1)S(1)}, bf16[128,2,2,128]{0,3,1,2:T(8,128)(2,1)S(1)}, u32[]{:S(2)}, u32[]{:S(2)}) %collective-permute-start.66) | collective-permute-done | bytes 131104 | tf_op jit(solution)/shard_map/ppermute | solution.py:37
  367.5 3.1 collective-permute-done.67
  (328 shorter events, 102.9 us)
Async XLA Ops:
  1.8 11.0 %collective-permute-start.3 = (bf16[6,128,128]{2,1,0:T(8,128)(2,1)S(1)}, bf16[6,128,128]{2,1,0:T(8,128)(2,1)}, u32[]{:S(2)}, u32[]{:S(2)}) collective-permute-start(bf16[6,128,128]{2,1,0:T(8,128)(2,1)S(1)} %get-tuple-element.207), channel_id=1, source_target_pairs={{0,4},{4,0},{8,12},{12,8},{16,20},{20,16},{24,28},{28,24},{1,5},{5... | collective-permute-start | bytes 589832 | tf_op jit(solution)/shard_map/ppermute | solution.py:37
  6.5 22.7 %collective-permute-start.4 = (bf16[3,352,128]{2,1,0:T(8,128)(2,1)S(1)}, bf16[3,352,128]{2,1,0:T(8,128)(2,1)S(1)}, u32[]{:S(2)}, u32[]{:S(2)}) collective-permute-start(bf16[3,352,128]{2,1,0:T(8,128)(2,1)S(1)} %get-tuple-element.193), channel_id=1, source_target_pairs={{0,4},{4,0},{8,12},{12,8},{16,20},{20,16},{24,28},{28,24},{1,5},{5... | collective-permute-start | bytes 811016 | tf_op jit(solution)/shard_map/ppermute | solution.py:37
  6.5 14.5 %collective-permute-start.5 = (bf16[128,1024]{1,0:T(8,128)(2,1)}, bf16[128,1024]{1,0:T(8,128)(2,1)S(1)}, u32[]{:S(2)}, u32[]{:S(2)}) collective-permute-start(bf16[128,1024]{1,0:T(8,128)(2,1)} %param.12), channel_id=1, source_target_pairs={{0,4},{4,0},{8,12},{12,8},{16,20},{20,16},{24,28},{28,24},{1,5},{5... | collective-permute-start | bytes 786440 | tf_op jit(solution)/shard_map/ppermute | solution.py:37
  8.6 17.0 %collective-permute-start.1 = (bf16[4,128,256]{2,1,0:T(8,128)(2,1)}, bf16[4,128,256]{2,1,0:T(8,128)(2,1)S(1)}, u32[]{:S(2)}, u32[]{:S(2)}) collective-permute-start(bf16[4,128,256]{2,1,0:T(8,128)(2,1)} %refs_0_), channel_id=1, source_target_pairs={{0,16},{4,20},{8,24},{12,28},{16,0},{20,4},{24,8},{28,12},{1,17},{... | collective-permute-start | bytes 786440 | tf_op jit(solution)/shard_map/ppermute | solution.py:65
  11.2 14.4 %collective-permute-start = (bf16[4,128,256]{2,1,0:T(8,128)(2,1)}, bf16[4,128,256]{2,1,0:T(8,128)(2,1)S(1)}, u32[]{:S(2)}, u32[]{:S(2)}) collective-permute-start(bf16[4,128,256]{2,1,0:T(8,128)(2,1)} %refs_0_), channel_id=1, source_target_pairs={{0,8},{4,12},{8,0},{12,4},{16,24},{20,28},{24,16},{28,20},{1,9},{5... | collective-permute-start | bytes 786440 | tf_op jit(solution)/shard_map/ppermute | solution.py:65
  12.7 16.5 %collective-permute-start.2 = (bf16[4,128,256]{2,1,0:T(8,128)(2,1)}, bf16[4,128,256]{2,1,0:T(8,128)(2,1)S(1)}, u32[]{:S(2)}, u32[]{:S(2)}) collective-permute-start(bf16[4,128,256]{2,1,0:T(8,128)(2,1)} %refs_0_), channel_id=1, source_target_pairs={{0,24},{4,28},{8,16},{12,20},{16,8},{20,12},{24,0},{28,4},{1,25},{... | collective-permute-start | bytes 786440 | tf_op jit(solution)/shard_map/ppermute | solution.py:65
  32.3 35.0 %collective-permute-start.7 = (bf16[4,512,256]{2,1,0:T(8,128)(2,1)}, bf16[4,512,256]{2,1,0:T(8,128)(2,1)S(1)}, u32[]{:S(2)}, u32[]{:S(2)}) collective-permute-start(bf16[4,512,256]{2,1,0:T(8,128)(2,1)} %join.7.refs_0_.refs_1_), channel_id=1, source_target_pairs={{0,2},{1,3},{2,0},{3,1},{4,6},{5,7},{6,4},{7,5},{8,10},{9,11},{10,... | collective-permute-start | bytes 3145736 | tf_op jit(solution)/shard_map/ppermute | solution.py:83
  33.9 33.5 %collective-permute-start.6 = (bf16[4,512,256]{2,1,0:T(8,128)(2,1)}, bf16[4,512,256]{2,1,0:T(8,128)(2,1)S(1)}, u32[]{:S(2)}, u32[]{:S(2)}) collective-permute-start(bf16[4,512,256]{2,1,0:T(8,128)(2,1)} %join.7.refs_0_.refs_1_), channel_id=1, source_target_pairs={{0,4},{4,0},{8,12},{12,8},{16,20},{20,16},{24,28},{28,24},{1,5},{5... | collective-permute-start | bytes 3145736 | tf_op jit(solution)/shard_map/ppermute | solution.py:37
  35.1 8.7 %collective-permute-start.10 = (bf16[1,704,128]{2,1,0:T(8,128)(2,1)S(1)}, bf16[1,704,128]{2,1,0:T(8,128)(2,1)S(1)}, u32[]{:S(2)}, u32[]{:S(2)}) collective-permute-start(bf16[1,704,128]{2,1,0:T(8,128)(2,1)S(1)} %slice.101.refs_0_), channel_id=1, source_target_pairs={{0,24},{4,28},{8,16},{12,20},{16,8},{20,12},{24,0},{28,4},{1,25},{... | collective-permute-start | bytes 540680 | tf_op jit(solution)/shard_map/ppermute | solution.py:65
  37.7 16.5 %collective-permute-start.9 = (bf16[1,704,128]{2,1,0:T(8,128)(2,1)S(1)}, bf16[1,704,128]{2,1,0:T(8,128)(2,1)S(1)}, u32[]{:S(2)}, u32[]{:S(2)}) collective-permute-start(bf16[1,704,128]{2,1,0:T(8,128)(2,1)S(1)} %slice.101.refs_0_), channel_id=1, source_target_pairs={{0,16},{4,20},{8,24},{12,28},{16,0},{20,4},{24,8},{28,12},{1,17},{... | collective-permute-start | bytes 540680 | tf_op jit(solution)/shard_map/ppermute | solution.py:65
  42.3 11.8 %collective-permute-start.8 = (bf16[1,704,128]{2,1,0:T(8,128)(2,1)S(1)}, bf16[1,704,128]{2,1,0:T(8,128)(2,1)S(1)}, u32[]{:S(2)}, u32[]{:S(2)}) collective-permute-start(bf16[1,704,128]{2,1,0:T(8,128)(2,1)S(1)} %slice.101.refs_0_), channel_id=1, source_target_pairs={{0,8},{4,12},{8,0},{12,4},{16,24},{20,28},{24,16},{28,20},{1,9},{5... | collective-permute-start | bytes 540680 | tf_op jit(solution)/shard_map/ppermute | solution.py:65
  54.2 21.5 %collective-permute-start.17 = (bf16[2,704,128]{2,1,0:T(8,128)(2,1)}, bf16[2,704,128]{2,1,0:T(8,128)(2,1)}, u32[]{:S(2)}, u32[]{:S(2)}) collective-permute-start(bf16[2,704,128]{2,1,0:T(8,128)(2,1)} %slice.102.refs_0_), channel_id=1, source_target_pairs={{0,24},{4,28},{8,16},{12,20},{16,8},{20,12},{24,0},{28,4},{1,25},{... | collective-permute-start | bytes 1081352 | tf_op jit(solution)/shard_map/ppermute | solution.py:65
  57.2 29.1 %collective-permute-start.16 = (bf16[2,704,128]{2,1,0:T(8,128)(2,1)}, bf16[2,704,128]{2,1,0:T(8,128)(2,1)}, u32[]{:S(2)}, u32[]{:S(2)}) collective-permute-start(bf16[2,704,128]{2,1,0:T(8,128)(2,1)} %slice.102.refs_0_), channel_id=1, source_target_pairs={{0,16},{4,20},{8,24},{12,28},{16,0},{20,4},{24,8},{28,12},{1,17},{... | collective-permute-start | bytes 1081352 | tf_op jit(solution)/shard_map/ppermute | solution.py:65
  70.2 28.5 %collective-permute-start.14 = (bf16[1,704,512]{2,1,0:T(8,128)(2,1)}, bf16[1,704,512]{2,1,0:T(8,128)(2,1)}, u32[]{:S(2)}, u32[]{:S(2)}) collective-permute-start(bf16[1,704,512]{2,1,0:T(8,128)(2,1)} %join.8.refs_1_), channel_id=1, source_target_pairs={{0,2},{1,3},{2,0},{3,1},{4,6},{5,7},{6,4},{7,5},{8,10},{9,11},{10,... | collective-permute-start | bytes 2162696 | tf_op jit(solution)/shard_map/ppermute | solution.py:83
  70.8 27.9 %collective-permute-start.13 = (bf16[1,704,512]{2,1,0:T(8,128)(2,1)}, bf16[1,704,512]{2,1,0:T(8,128)(2,1)}, u32[]{:S(2)}, u32[]{:S(2)}) collective-permute-start(bf16[1,704,512]{2,1,0:T(8,128)(2,1)} %join.8.refs_1_), channel_id=1, source_target_pairs={{0,4},{4,0},{8,12},{12,8},{16,20},{20,16},{24,28},{28,24},{1,5},{5... | collective-permute-start | bytes 2162696 | tf_op jit(solution)/shard_map/ppermute | solution.py:37
  74.2 24.5 %collective-permute-start.12 = (bf16[4,256,256]{2,1,0:T(8,128)(2,1)}, bf16[4,256,256]{2,1,0:T(8,128)(2,1)}, u32[]{:S(2)}, u32[]{:S(2)}) collective-permute-start(bf16[4,256,256]{2,1,0:T(8,128)(2,1)} %slice.104), channel_id=1, source_target_pairs={{0,2},{1,3},{2,0},{3,1},{4,6},{5,7},{6,4},{7,5},{8,10},{9,11},{10,... | collective-permute-start | bytes 1572872 | tf_op jit(solution)/shard_map/ppermute | solution.py:83
  75.7 23.0 %collective-permute-start.11 = (bf16[4,256,256]{2,1,0:T(8,128)(2,1)}, bf16[4,256,256]{2,1,0:T(8,128)(2,1)}, u32[]{:S(2)}, u32[]{:S(2)}) collective-permute-start(bf16[4,256,256]{2,1,0:T(8,128)(2,1)} %slice.103), channel_id=1, source_target_pairs={{0,4},{4,0},{8,12},{12,8},{16,20},{20,16},{24,28},{28,24},{1,5},{5... | collective-permute-start | bytes 1572872 | tf_op jit(solution)/shard_map/ppermute | solution.py:37
  86.3 12.4 %collective-permute-start.15 = (bf16[2,704,128]{2,1,0:T(8,128)(2,1)}, bf16[2,704,128]{2,1,0:T(8,128)(2,1)}, u32[]{:S(2)}, u32[]{:S(2)}) collective-permute-start(bf16[2,704,128]{2,1,0:T(8,128)(2,1)} %slice.102.refs_0_), channel_id=1, source_target_pairs={{0,8},{4,12},{8,0},{12,4},{16,24},{20,28},{24,16},{28,20},{1,9},{5... | collective-permute-start | bytes 1081352 | tf_op jit(solution)/shard_map/ppermute | solution.py:65
  119.9 11.9 %collective-permute-start.25 = (bf16[576,1024]{1,0:T(8,128)(2,1)S(1)}, bf16[576,1024]{1,0:T(8,128)(2,1)}, u32[]{:S(2)}, u32[]{:S(2)}) collective-permute-start(bf16[576,1024]{1,0:T(8,128)(2,1)S(1)} %fusion.3), channel_id=1, source_target_pairs={{0,1},{1,0},{2,3},{3,2},{4,5},{5,4},{6,7},{7,6},{8,9},{9,8},{10,11... | collective-permute-start | bytes 3538952 | tf_op jit(solution)/shard_map/ppermute | solution.py:42
  123.7 41.9 %collective-permute-start.20 = (bf16[2,704,512]{2,1,0:T(8,128)(2,1)}, bf16[2,704,512]{2,1,0:T(8,128)(2,1)S(1)}, u32[]{:S(2)}, u32[]{:S(2)}) collective-permute-start(bf16[2,704,512]{2,1,0:T(8,128)(2,1)} %join.9.refs_3_.refs_1_), channel_id=1, source_target_pairs={{0,2},{1,3},{2,0},{3,1},{4,6},{5,7},{6,4},{7,5},{8,10},{9,11},{10,... | collective-permute-start | bytes 4325384 | tf_op jit(solution)/shard_map/ppermute | solution.py:83
  125.8 41.0 %collective-permute-start.19 = (bf16[2,704,512]{2,1,0:T(8,128)(2,1)}, bf16[2,704,512]{2,1,0:T(8,128)(2,1)}, u32[]{:S(2)}, u32[]{:S(2)}) collective-permute-start(bf16[2,704,512]{2,1,0:T(8,128)(2,1)} %join.9.refs_3_.refs_1_), channel_id=1, source_target_pairs={{0,4},{4,0},{8,12},{12,8},{16,20},{20,16},{24,28},{28,24},{1,5},{5... | collective-permute-start | bytes 4325384 | tf_op jit(solution)/shard_map/ppermute | solution.py:37
  127.8 14.0 %collective-permute-start.23 = (bf16[6,2,128,128]{3,2,1,0:T(8,128)(2,1)S(1)}, bf16[6,2,128,128]{3,2,1,0:T(8,128)(2,1)S(1)}, u32[]{:S(2)}, u32[]{:S(2)}) collective-permute-start(bf16[6,2,128,128]{3,2,1,0:T(8,128)(2,1)S(1)} %pad_maximum_fusion.4.refs_0_), channel_id=1, source_target_pairs={{0,24},{4,28},{8,16},{12,20},{16,8},{20,12},{24,0},{28,4},{1,25},{... | collective-permute-start | bytes 1179656 | tf_op jit(solution)/shard_map/ppermute | solution.py:65
  128.9 36.6 %collective-permute-start.22 = (bf16[6,2,128,128]{3,2,1,0:T(8,128)(2,1)S(1)}, bf16[6,2,128,128]{3,2,1,0:T(8,128)(2,1)S(1)}, u32[]{:S(2)}, u32[]{:S(2)}) collective-permute-start(bf16[6,2,128,128]{3,2,1,0:T(8,128)(2,1)S(1)} %pad_maximum_fusion.4.refs_0_), channel_id=1, source_target_pairs={{0,16},{4,20},{8,24},{12,28},{16,0},{20,4},{24,8},{28,12},{1,17},{... | collective-permute-start | bytes 1179656 | tf_op jit(solution)/shard_map/ppermute | solution.py:65
  131.8 33.8 %collective-permute-start.21 = (bf16[6,2,128,128]{3,2,1,0:T(8,128)(2,1)S(1)}, bf16[6,2,128,128]{3,2,1,0:T(8,128)(2,1)S(1)}, u32[]{:S(2)}, u32[]{:S(2)}) collective-permute-start(bf16[6,2,128,128]{3,2,1,0:T(8,128)(2,1)S(1)} %pad_maximum_fusion.4.refs_0_), channel_id=1, source_target_pairs={{0,8},{4,12},{8,0},{12,4},{16,24},{20,28},{24,16},{28,20},{1,9},{5... | collective-permute-start | bytes 1179656 | tf_op jit(solution)/shard_map/ppermute | solution.py:65
  166.9 38.8 %collective-permute-start.26 = (bf16[2,704,512]{2,1,0:T(8,128)(2,1)}, bf16[2,704,512]{2,1,0:T(8,128)(2,1)}, u32[]{:S(2)}, u32[]{:S(2)}) collective-permute-start(bf16[2,704,512]{2,1,0:T(8,128)(2,1)} %collective-permute-done.19.refs_4_.refs_2_), channel_id=1, source_target_pairs={{0,2},{1,3},{2,0},{3,1},{4,6},{5,7},{6,4},{7,5},{8,10},{9,11},{10,... | collective-permute-start | bytes 4325384 | tf_op jit(solution)/shard_map/ppermute | solution.py:83
  176.0 18.7 %collective-permute-start.18 = (bf16[1,704,512]{2,1,0:T(8,128)(2,1)}, bf16[1,704,512]{2,1,0:T(8,128)(2,1)S(1)}, u32[]{:S(2)}, u32[]{:S(2)}) collective-permute-start(bf16[1,704,512]{2,1,0:T(8,128)(2,1)} %collective-permute-done.14.refs_1_), channel_id=1, source_target_pairs={{0,4},{4,0},{8,12},{12,8},{16,20},{20,16},{24,28},{28,24},{1,5},{5... | collective-permute-start | bytes 2162696 | tf_op jit(solution)/shard_map/ppermute | solution.py:37
  177.1 19.0 %collective-permute-start.32 = (bf16[2,128,256]{2,1,0:T(8,128)(2,1)}, bf16[2,128,256]{2,1,0:T(8,128)(2,1)S(1)}, u32[]{:S(2)}, u32[]{:S(2)}) collective-permute-start(bf16[2,128,256]{2,1,0:T(8,128)(2,1)} %refs_0_.1), channel_id=1, source_target_pairs={{0,24},{4,28},{8,16},{12,20},{16,8},{20,12},{24,0},{28,4},{1,25},{... | collective-permute-start | bytes 393224 | tf_op jit(solution)/shard_map/ppermute | solution.py:65
  178.2 26.9 %collective-permute-start.31 = (bf16[2,128,256]{2,1,0:T(8,128)(2,1)}, bf16[2,128,256]{2,1,0:T(8,128)(2,1)S(1)}, u32[]{:S(2)}, u32[]{:S(2)}) collective-permute-start(bf16[2,128,256]{2,1,0:T(8,128)(2,1)} %refs_0_.1), channel_id=1, source_target_pairs={{0,16},{4,20},{8,24},{12,28},{16,0},{20,4},{24,8},{28,12},{1,17},{... | collective-permute-start | bytes 393224 | tf_op jit(solution)/shard_map/ppermute | solution.py:65
  178.2 26.9 %collective-permute-start.30 = (bf16[2,128,256]{2,1,0:T(8,128)(2,1)}, bf16[2,128,256]{2,1,0:T(8,128)(2,1)S(1)}, u32[]{:S(2)}, u32[]{:S(2)}) collective-permute-start(bf16[2,128,256]{2,1,0:T(8,128)(2,1)} %refs_0_.1), channel_id=1, source_target_pairs={{0,8},{4,12},{8,0},{12,4},{16,24},{20,28},{24,16},{28,20},{1,9},{5... | collective-permute-start | bytes 393224 | tf_op jit(solution)/shard_map/ppermute | solution.py:65
  194.8 10.3 %collective-permute-start.29 = (bf16[64,1024]{1,0:T(8,128)(2,1)S(1)}, bf16[64,1024]{1,0:T(8,128)(2,1)S(1)}, u32[]{:S(2)}, u32[]{:S(2)}) collective-permute-start(bf16[64,1024]{1,0:T(8,128)(2,1)S(1)} %get-tuple-element.140), channel_id=1, source_target_pairs={{0,2},{1,3},{2,0},{3,1},{4,6},{5,7},{6,4},{7,5},{8,10},{9,11},{10,... | collective-permute-start | bytes 393224 | tf_op jit(solution)/shard_map/ppermute | solution.py:83
  196.7 8.4 %collective-permute-start.28 = (bf16[64,1024]{1,0:T(8,128)(2,1)S(1)}, bf16[64,1024]{1,0:T(8,128)(2,1)S(1)}, u32[]{:S(2)}, u32[]{:S(2)}) collective-permute-start(bf16[64,1024]{1,0:T(8,128)(2,1)S(1)} %get-tuple-element.138), channel_id=1, source_target_pairs={{0,4},{4,0},{8,12},{12,8},{16,20},{20,16},{24,28},{28,24},{1,5},{5... | collective-permute-start | bytes 393224 | tf_op jit(solution)/shard_map/ppermute | solution.py:37
  208.3 16.5 %collective-permute-start.36 = (bf16[2,512,256]{2,1,0:T(8,128)(2,1)}, bf16[2,512,256]{2,1,0:T(8,128)(2,1)S(1)}, u32[]{:S(2)}, u32[]{:S(2)}) collective-permute-start(bf16[2,512,256]{2,1,0:T(8,128)(2,1)} %join.11.refs_3_), channel_id=1, source_target_pairs={{0,2},{1,3},{2,0},{3,1},{4,6},{5,7},{6,4},{7,5},{8,10},{9,11},{10,... | collective-permute-start | bytes 1572872 | tf_op jit(solution)/shard_map/ppermute | solution.py:83
  209.1 15.7 %collective-permute-start.35 = (bf16[2,512,256]{2,1,0:T(8,128)(2,1)}, bf16[2,512,256]{2,1,0:T(8,128)(2,1)S(1)}, u32[]{:S(2)}, u32[]{:S(2)}) collective-permute-start(bf16[2,512,256]{2,1,0:T(8,128)(2,1)} %join.11.refs_3_), channel_id=1, source_target_pairs={{0,4},{4,0},{8,12},{12,8},{16,20},{20,16},{24,28},{28,24},{1,5},{5... | collective-permute-start | bytes 1572872 | tf_op jit(solution)/shard_map/ppermute | solution.py:37
  211.1 13.2 %collective-permute-start.33 = (bf16[64,1024]{1,0:T(8,128)(2,1)S(1)}, bf16[64,1024]{1,0:T(8,128)(2,1)S(1)}, u32[]{:S(2)}, u32[]{:S(2)}) collective-permute-start(bf16[64,1024]{1,0:T(8,128)(2,1)S(1)} %add_convert_fusion.6), channel_id=1, source_target_pairs={{0,2},{1,3},{2,0},{3,1},{4,6},{5,7},{6,4},{7,5},{8,10},{9,11},{10,... | collective-permute-start | bytes 393224 | tf_op jit(solution)/shard_map/ppermute | solution.py:83
  213.4 11.5 %collective-permute-start.34 = (bf16[64,1024]{1,0:T(8,128)(2,1)S(1)}, bf16[64,1024]{1,0:T(8,128)(2,1)S(1)}, u32[]{:S(2)}, u32[]{:S(2)}) collective-permute-start(bf16[64,1024]{1,0:T(8,128)(2,1)S(1)} %add_convert_fusion.5), channel_id=1, source_target_pairs={{0,4},{4,0},{8,12},{12,8},{16,20},{20,16},{24,28},{28,24},{1,5},{5... | collective-permute-start | bytes 393224 | tf_op jit(solution)/shard_map/ppermute | solution.py:37
  226.5 14.7 %collective-permute-start.42 = (bf16[2,256,256]{2,1,0:T(8,128)(2,1)S(1)}, bf16[2,256,256]{2,1,0:T(8,128)(2,1)S(1)}, u32[]{:S(2)}, u32[]{:S(2)}) collective-permute-start(bf16[2,256,256]{2,1,0:T(8,128)(2,1)S(1)} %slice.113), channel_id=1, source_target_pairs={{0,2},{1,3},{2,0},{3,1},{4,6},{5,7},{6,4},{7,5},{8,10},{9,11},{10,... | collective-permute-start | bytes 786440 | tf_op jit(solution)/shard_map/ppermute | solution.py:83
  227.9 13.3 %collective-permute-start.41 = (bf16[2,256,256]{2,1,0:T(8,128)(2,1)S(1)}, bf16[2,256,256]{2,1,0:T(8,128)(2,1)S(1)}, u32[]{:S(2)}, u32[]{:S(2)}) collective-permute-start(bf16[2,256,256]{2,1,0:T(8,128)(2,1)S(1)} %slice.112), channel_id=1, source_target_pairs={{0,4},{4,0},{8,12},{12,8},{16,20},{20,16},{24,28},{28,24},{1,5},{5... | collective-permute-start | bytes 786440 | tf_op jit(solution)/shard_map/ppermute | solution.py:37
  229.4 11.8 %collective-permute-start.40 = (bf16[256,128]{1,0:T(8,128)(2,1)S(1)}, bf16[256,128]{1,0:T(8,128)(2,1)S(1)}, u32[]{:S(2)}, u32[]{:S(2)}) collective-permute-start(bf16[256,128]{1,0:T(8,128)(2,1)S(1)} %convolution_convert_fusion.1.refs_0_), channel_id=1, source_target_pairs={{0,24},{4,28},{8,16},{12,20},{16,8},{20,12},{24,0},{28,4},{1,25},{... | collective-permute-start | bytes 196616 | tf_op jit(solution)/shard_map/ppermute | solution.py:65
  230.5 10.8 %collective-permute-start.39 = (bf16[256,128]{1,0:T(8,128)(2,1)S(1)}, bf16[256,128]{1,0:T(8,128)(2,1)S(1)}, u32[]{:S(2)}, u32[]{:S(2)}) collective-permute-start(bf16[256,128]{1,0:T(8,128)(2,1)S(1)} %convolution_convert_fusion.1.refs_0_), channel_id=1, source_target_pairs={{0,16},{4,20},{8,24},{12,28},{16,0},{20,4},{24,8},{28,12},{1,17},{... | collective-permute-start | bytes 196616 | tf_op jit(solution)/shard_map/ppermute | solution.py:65
  230.5 10.8 %collective-permute-start.38 = (bf16[256,128]{1,0:T(8,128)(2,1)S(1)}, bf16[256,128]{1,0:T(8,128)(2,1)S(1)}, u32[]{:S(2)}, u32[]{:S(2)}) collective-permute-start(bf16[256,128]{1,0:T(8,128)(2,1)S(1)} %convolution_convert_fusion.1.refs_0_), channel_id=1, source_target_pairs={{0,8},{4,12},{8,0},{12,4},{16,24},{20,28},{24,16},{28,20},{1,9},{5... | collective-permute-start | bytes 196616 | tf_op jit(solution)/shard_map/ppermute | solution.py:65
  249.0 53.9 %collective-permute-start.48 = (bf16[576,1024]{1,0:T(8,128)(2,1)}, bf16[576,1024]{1,0:T(8,128)(2,1)}, u32[]{:S(2)}, u32[]{:S(2)}) collective-permute-start(bf16[576,1024]{1,0:T(8,128)(2,1)} %fusion.1), channel_id=1, source_target_pairs={{0,1},{1,0},{2,3},{3,2},{4,5},{5,4},{6,7},{7,6},{8,9},{9,8},{10,11... | collective-permute-start | bytes 3538952 | tf_op jit(solution)/shard_map/ppermute | solution.py:42
  249.3 17.3 %collective-permute-start.51 = (bf16[6,352,128]{2,1,0:T(8,128)(2,1)S(1)}, bf16[6,352,128]{2,1,0:T(8,128)(2,1)}, u32[]{:S(2)}, u32[]{:S(2)}) collective-permute-start(bf16[6,352,128]{2,1,0:T(8,128)(2,1)S(1)} %bitcast.115), channel_id=1, source_target_pairs={{0,24},{4,28},{8,16},{12,20},{16,8},{20,12},{24,0},{28,4},{1,25},{... | collective-permute-start | bytes 1622024 | tf_op jit(solution)/shard_map/ppermute | solution.py:65
  252.0 8.6 %collective-permute-start.44 = (bf16[1024,128]{1,0:T(8,128)(2,1)}, bf16[1024,128]{1,0:T(8,128)(2,1)S(1)}, u32[]{:S(2)}, u32[]{:S(2)}) collective-permute-start(bf16[1024,128]{1,0:T(8,128)(2,1)} %join.12), channel_id=1, source_target_pairs={{0,2},{1,3},{2,0},{3,1},{4,6},{5,7},{6,4},{7,5},{8,10},{9,11},{10,... | collective-permute-start | bytes 786440 | tf_op jit(solution)/shard_map/ppermute | solution.py:83
  253.9 44.2 %collective-permute-start.50 = (bf16[6,352,128]{2,1,0:T(8,128)(2,1)S(1)}, bf16[6,352,128]{2,1,0:T(8,128)(2,1)S(1)}, u32[]{:S(2)}, u32[]{:S(2)}) collective-permute-start(bf16[6,352,128]{2,1,0:T(8,128)(2,1)S(1)} %bitcast.116), channel_id=1, source_target_pairs={{0,16},{4,20},{8,24},{12,28},{16,0},{20,4},{24,8},{28,12},{1,17},{... | collective-permute-start | bytes 1622024 | tf_op jit(solution)/shard_map/ppermute | solution.py:65
  260.6 38.3 %collective-permute-start.49 = (bf16[6,352,128]{2,1,0:T(8,128)(2,1)S(1)}, bf16[6,352,128]{2,1,0:T(8,128)(2,1)}, u32[]{:S(2)}, u32[]{:S(2)}) collective-permute-start(bf16[6,352,128]{2,1,0:T(8,128)(2,1)S(1)} %bitcast.117), channel_id=1, source_target_pairs={{0,8},{4,12},{8,0},{12,4},{16,24},{20,28},{24,16},{28,20},{1,9},{5... | collective-permute-start | bytes 1622024 | tf_op jit(solution)/shard_map/ppermute | solution.py:65
  261.6 40.3 %collective-permute-start.45 = (bf16[512,128]{1,0:T(8,128)(2,1)S(1)}, bf16[512,128]{1,0:T(8,128)(2,1)}, u32[]{:S(2)}, u32[]{:S(2)}) collective-permute-start(bf16[512,128]{1,0:T(8,128)(2,1)S(1)} %slice.136), channel_id=1, source_target_pairs={{0,4},{4,0},{8,12},{12,8},{16,20},{20,16},{24,28},{28,24},{1,5},{5... | collective-permute-start | bytes 393224 | tf_op jit(solution)/shard_map/ppermute | solution.py:37
  266.5 35.4 %collective-permute-start.46 = (bf16[512,128]{1,0:T(8,128)(2,1)S(1)}, bf16[512,128]{1,0:T(8,128)(2,1)}, u32[]{:S(2)}, u32[]{:S(2)}) collective-permute-start(bf16[512,128]{1,0:T(8,128)(2,1)S(1)} %slice.137), channel_id=1, source_target_pairs={{0,2},{1,3},{2,0},{3,1},{4,6},{5,7},{6,4},{7,5},{8,10},{9,11},{10,... | collective-permute-start | bytes 393224 | tf_op jit(solution)/shard_map/ppermute | solution.py:83
  312.5 9.3 %collective-permute-start.53 = (bf16[4,272,128]{2,1,0:T(8,128)(2,1)S(1)}, bf16[4,272,128]{2,1,0:T(8,128)(2,1)S(1)}, u32[]{:S(2)}, u32[]{:S(2)}) collective-permute-start(bf16[4,272,128]{2,1,0:T(8,128)(2,1)S(1)} %get-tuple-element.192), channel_id=1, source_target_pairs={{0,2},{1,3},{2,0},{3,1},{4,6},{5,7},{6,4},{7,5},{8,10},{9,11},{10,... | collective-permute-start | bytes 835592 | tf_op jit(solution)/shard_map/ppermute | solution.py:83
  (74 other events, 640.6 us)

commit v3 on v2

--- a/solution.py
+++ b/solution.py
@@ -395,51 +395,93 @@
     return dot(first, vals[:count]) + dot(second, vals[count:])
 
 
-def enc_attention_kernel(
-    low_ref, high_ref, first_ref, seg_q_ref, seg_k_ref, q_ref, k_ref, v_ref, o_ref, acc, *, rows
-):
-    width = q_ref.shape[1]
-    first_row = first_ref[0]
-    key_rows = seg_k_ref.shape[2]
-    last = seg_k_ref.shape[0] - 1
+def active_range(begin, end):
+    place = jnp.arange(begin.shape[0], dtype=jnp.int32)
+    here = end > begin
+    first = jnp.min(jnp.where(here, place, begin.shape[0]))
+    return jnp.stack([first, jnp.max(jnp.where(here, place + 1, 0))])
+
+
+def enc_attention_kernel(active_ref, query_ref, key_ref, first_ref, q_ref, k_ref, v_ref, o_ref, acc):
+    window, width = q_ref.shape
+    pairs = width // LANES
+    acc[...] = jnp.zeros_like(acc)
     low_half = lax.broadcasted_iota(jnp.int32, (1, LANES), 1) < HEAD_DIM
-
-    def block(i, carry):
-        begin = pl.multiple_of(i * rows, rows)
-        query_begin = pl.multiple_of(first_row + i * rows, math.gcd(rows, LANES))
-        low, high = low_ref[i], high_ref[i]
-        acc[...] = jnp.zeros_like(acc)
-
-        def step(j, inner):
-            for p in range(width // LANES):
-                columns = slice(p * LANES, (p + 1) * LANES)
-                total = None
-                for u in range(2):
-                    index = low + 2 * j + u
-                    clipped = jnp.minimum(index, last)
-                    offset = pl.multiple_of(clipped * key_rows, key_rows)
-                    seg_k = jnp.where(index < high, seg_k_ref[clipped], -1)
-                    allowed = seg_q_ref[pl.ds(begin, rows), :key_rows] == seg_k
-                    part = two_heads(
-                        q_ref[pl.ds(query_begin, rows), columns],
-                        k_ref[pl.ds(offset, key_rows), columns],
-                        v_ref[pl.ds(offset, key_rows), columns],
-                        allowed,
-                        low_half,
-                    )
-                    total = part if total is None else total + part
-                acc[p] += total
-            return inner
-
-        lax.fori_loop(0, (high - low + 1) // 2, step, 0)
-        for p in range(width // LANES):
-            sums = acc[p]
-            o_ref[pl.ds(begin, rows), p * LANES : (p + 1) * LANES] = (
+    row = lax.broadcasted_iota(jnp.int32, (LANES, 1), 0)
+    column = lax.broadcasted_iota(jnp.int32, (1, LANES), 1)
+    count = query_ref.shape[1]
+
+    def bounds(s):
+        clipped = jnp.minimum(s, count - 1)
+        begin = query_ref[0, clipped]
+        end = jnp.where(s < active_ref[1], query_ref[1, clipped], begin)
+        return begin, end, key_ref[0, clipped], key_ref[1, clipped]
+
+    def tiles(begin, end):
+        return (end - begin // 16 * 16 + LANES - 1) // LANES
+
+    def offset_of(begin, index):
+        low = begin // 16 * 16 + index * LANES
+        return low, pl.multiple_of(jnp.minimum(low, window - LANES), 16)
+
+    def sums_of(place, i, j):
+        begin, end, key_begin, key_end = place
+        low, offset = offset_of(begin, i)
+        key_low, key_offset = offset_of(key_begin, j)
+        rows = offset + row
+        keys = key_offset + column
+        least = jnp.where((rows >= jnp.maximum(begin, low)) & (rows < end), 0, window)
+        keys = jnp.where((keys >= jnp.maximum(key_begin, key_low)) & (keys < key_end), keys, -1)
+        allowed = keys >= least
+        return offset, [
+            two_heads(
+                q_ref[pl.ds(offset, LANES), p * LANES : (p + 1) * LANES],
+                k_ref[pl.ds(key_offset, LANES), p * LANES : (p + 1) * LANES],
+                v_ref[pl.ds(key_offset, LANES), p * LANES : (p + 1) * LANES],
+                allowed,
+                low_half,
+            )
+            for p in range(pairs)
+        ]
+
+    def add(offset, sums):
+        for p in range(pairs):
+            acc[p, pl.ds(offset, LANES), :] += sums[p]
+
+    def two_passages(n, carry):
+        first = active_ref[0] + 2 * n
+        places = [bounds(first), bounds(first + 1)]
+        both = [sums_of(place, 0, 0) for place in places]
+        for offset, sums in both:
+            add(offset, sums)
+        for place in places:
+            key_tiles = tiles(place[2], place[3])
+
+            def over_rows(i, outer, place=place, key_tiles=key_tiles):
+                def over_keys(j, inner):
+                    add(*sums_of(place, i, j))
+                    return inner
+
+                lax.fori_loop(jnp.where(i == 0, 1, 0), key_tiles, over_keys, 0)
+                return outer
+
+            lax.fori_loop(0, jnp.where(place[1] > place[0], tiles(place[0], place[1]), 0), over_rows, 0)
+        return carry
+
+    lax.fori_loop(0, (active_ref[1] - active_ref[0] + 1) // 2, two_passages, 0)
+    block = math.gcd(o_ref.shape[0], LANES)
+
+    def finish(n, carry):
+        begin = pl.multiple_of(n * block, block)
+        source = pl.multiple_of(first_ref[0] + n * block, block)
+        for p in range(pairs):
+            sums = acc[p, pl.ds(source, block), :]
+            o_ref[pl.ds(begin, block), p * LANES : (p + 1) * LANES] = (
                 sums[:, :LANES] / sums[:, LANES:]
             ).astype(BF16)
         return carry
 
-    lax.fori_loop(0, low_ref.shape[0], block, 0)
+    lax.fori_loop(0, o_ref.shape[0] // block, finish, 0)
 
 
 def project_into(h_ref, weights, mats, outs):
@@ -455,33 +497,29 @@
         out[pl.ds(begin, rows), :] = total.astype(BF16)
 
 
-def enc_block_kernel(low_ref, high_ref, first_ref, seg_q_ref, seg_k_ref, h_ref, *refs, rows):
+def enc_block_kernel(active_ref, query_ref, key_ref, first_ref, h_ref, *refs):
     *weights, o_ref, q, k, v, acc = refs
     project_into(h_ref, weights, (0, 1, 2), (q, k, v))
 
     @pl.when(pl.program_id(0) == pl.num_programs(0) - 1)
     def _():
-        enc_attention_kernel(
-            low_ref, high_ref, first_ref, seg_q_ref, seg_k_ref, q, k, v, o_ref, acc, rows=rows
-        )
-
-
-def enc_block(low, high, first_row, seg_q, seg_k, h, weights):
-    rows, window, width = seg_q.shape[0], h.shape[0], weights[0].shape[2]
-    query_rows = rows // low.shape[0]
+        enc_attention_kernel(active_ref, query_ref, key_ref, first_ref, q, k, v, o_ref, acc)
+
+
+def enc_block(query_range, key_range, first_row, rows, h, weights):
+    window, width = h.shape[0], weights[0].shape[2]
     step = row_block(window, 400)
     smem = pl.BlockSpec(memory_space=pltpu.SMEM)
     return pl.pallas_call(
-        functools.partial(enc_block_kernel, rows=query_rows),
+        enc_block_kernel,
         out_shape=jax.ShapeDtypeStruct((rows, width), BF16),
         grid=(window // step,),
-        in_specs=[smem] * 3
-        + [resident(seg_q), resident(seg_k)]
+        in_specs=[smem] * 4
         + [pl.BlockSpec((step, h.shape[1]), lambda i: (i, 0))]
         + [resident(weight) for weight in weights],
         out_specs=pl.BlockSpec((rows, width), lambda i: (0, 0)),
         scratch_shapes=[pltpu.VMEM((window, width), BF16)] * 3
-        + [pltpu.VMEM((width // LANES, query_rows, 2 * LANES), F32)],
+        + [pltpu.VMEM((width // LANES, window, 2 * LANES), F32)],
         compiler_params=pltpu.CompilerParams(vmem_limit_bytes=32 * 2**20),
         cost_estimate=pl.CostEstimate(
             flops=window * width * (6 * h.shape[1] + 3072),
@@ -489,7 +527,7 @@
             transcendentals=0,
         ),
         name="enc_block",
-    )(low, high, first_row.reshape(1), seg_q, seg_k, h, *weights)
+    )(active_range(*query_range), query_range, key_range, first_row.reshape(1), h, *weights)
 
 
 def cross_block_kernel(
@@ -609,14 +647,7 @@
     key_rows = min(rows, LANES)
     pairs = width // LANES
     step = row_block(rows, 400)
-    place = jnp.arange(begin.shape[0], dtype=jnp.int32)
-    here = end > begin
-    active = jnp.stack(
-        [
-            jnp.min(jnp.where(here, place, begin.shape[0])),
-            jnp.max(jnp.where(here, place + 1, 0)),
-        ]
-    )
+    active = active_range(begin, end)
     smem = pl.BlockSpec(memory_space=pltpu.SMEM)
     shape = (questions // 2, pairs, 2 * length + 16, LANES)
     return pl.pallas_call(
@@ -801,25 +832,9 @@
     lengths = passage_lengths[0]
     ends = jnp.cumsum(lengths)
     starts = ends - lengths
-    positions = window_begin + jnp.arange(window, dtype=jnp.int32)
-    segment = jnp.sum((positions[:, None] >= ends[None, :]).astype(jnp.int32), axis=1)
-    query_block = math.gcd(rows, 3 * LANES)
-    key_block = math.gcd(window, LANES)
-    block_first = row_begin + jnp.arange(rows // query_block, dtype=jnp.int32) * query_block
-    block_last = block_first + query_block - 1
-    inside_first = jnp.max(
-        jnp.where(starts[None, :] <= block_first[:, None], starts[None, :], 0), axis=1
-    )
-    inside_last = jnp.min(
-        jnp.where(ends[None, :] > block_last[:, None], ends[None, :], row_count), axis=1
-    )
-    low = (inside_first - window_begin) // key_block
-    high = (inside_last - window_begin + key_block - 1) // key_block
-    seg_k = segment.reshape(window // key_block, 1, key_block)
-    seg_q = jnp.broadcast_to(
-        lax.dynamic_slice_in_dim(segment, row_begin - window_begin, rows, 0)[:, None],
-        (rows, LANES),
-    )
+    limits = jnp.stack([starts, ends]) - window_begin
+    query_range = jnp.clip(limits, row_begin - window_begin, row_begin - window_begin + rows)
+    key_range = jnp.clip(limits, 0, window)
 
     own_begin = row_begin - window_begin
     if shard_width % LANES == 0 and window % LANES == 0 and rows % LANES == 0:
@@ -842,7 +857,7 @@
     gate_near = spread_near(gate_block)
 
     def attend(parts):
-        return enc_block(low, high, own_begin, seg_q, seg_k, normed, parts)
+        return enc_block(query_range, key_range, own_begin, rows, normed, parts)
 
     if size_y == 2:
         mixes = [attend([attn_block, attn_near[0]])]

time: 373 us -> 376 us (level)
    unnamed x113 -> x125, local copies, waits for them, and re-layouts: 12 us -> 13.7 us
where the time goes in v3:
time: 376 us; the launch traced here: 375 us
  waiting for transfers between devices  155 us (41%)
  Pallas kernels  90.8 us (24%)
  starting transfers between devices  75.6 us (20%)
  local copies, waits for them, and re-layouts  28 us (7%)
  other arithmetic  23.3 us (6%)
    ppermute x24, waiting for transfers between devices, swap_z(): return lax.ppermute(value, 'dp', [(i, i ^ 2 * step) for i in range(count)])  95.4 us
    ppermute x24, starting transfers between devices, swap_z(): return lax.ppermute(value, 'dp', [(i, i ^ 2 * step) for i in range(count)])  35.2 us
    ppermute x18, waiting for transfers between devices, swap_x(): return lax.ppermute(value, 'dp', [(i, i ^ 1) for i in range(count)])  32.3 us
    pallas_call x2, Pallas kernels, enc_block(): pl.pallas_call(enc_block_kernel, out_shape=jax.ShapeDtypeStruct((rows, wi...  22.6 us
    pallas_call x4, Pallas kernels, ff(): pl.pallas_call(functools.partial(ff_kernel, chunks=plan, done=before, las...  21.8 us
    ppermute x18, starting transfers between devices, swap_x(): return lax.ppermute(value, 'dp', [(i, i ^ 1) for i in range(count)])  21.7 us
    ppermute x16, waiting for transfers between devices, swap_y(): return lax.ppermute(value, 'mp', [(i, i ^ 2) for i in range(4)])  17.5 us
    ppermute x16, starting transfers between devices, swap_y(): return lax.ppermute(value, 'mp', [(i, i ^ 2) for i in range(4)])  17.4 us
  transfers between devices with their start and end apart: 68, of which 30 were waited for; matrix products, arithmetic and copies ran while one was open for 6% of the time, Pallas kernels for 17%

profile of v3, /device:TPU:0, one launch (start us, length us, event | category | flops | bytes accessed | tf_op | source)
XLA Modules:
  0.0 374.7 jit_solution(3199594390022951712)
XLA Ops:
  1.8 3.0 collective-permute-start.3
  6.5 2.0 collective-permute-start.5
  8.6 2.6 collective-permute-start.1
  12.7 2.0 collective-permute-start.2
  14.7 6.3 %collective-permute-done.5 = bf16[128,1024]{1,0:T(8,128)(2,1)S(1)} collective-permute-done((bf16[128,1024]{1,0:T(8,128)(2,1)}, bf16[128,1024]{1,0:T(8,128)(2,1)S(1)}, u32[]{:S(2)}, u32[]{:S(2)}) %collective-permute-start.5) | collective-permute-done | bytes 262176 | tf_op jit(solution)/shard_map/ppermute | solution.py:37
  21.1 4.5 %collective-permute-done.1.refs_2_ = bf16[4,128,256]{2,1,0:T(8,128)(2,1)S(1)} collective-permute-done((bf16[4,128,256]{2,1,0:T(8,128)(2,1)}, bf16[4,128,256]{2,1,0:T(8,128)(2,1)S(1)}, u32[]{:S(2)}, u32[]{:S(2)}) %collective-permute-start.1) | collective-permute-done | bytes 262176 | tf_op jit(solution)/shard_map/ppermute | solution.py:65
  25.6 3.7 collective-permute-done.2.refs_3_
  30.1 2.3 join.7.refs_0_.refs_1_
  34.5 2.5 collective-permute-start.10
  37.1 4.7 %collective-permute-start.9 = (bf16[1,704,128]{2,1,0:T(8,128)(2,1)S(1)}, bf16[1,704,128]{2,1,0:T(8,128)(2,1)S(1)}, u32[]{:S(2)}, u32[]{:S(2)}) collective-permute-start(bf16[1,704,128]{2,1,0:T(8,128)(2,1)S(1)} %slice.101.refs_0_), channel_id=1, source_target_pairs={{0,16},{4,20},{8,24},{12,28},{16,0},{20,4},{24,8},{28,12},{1,17},{... | collective-permute-start | bytes 540680 | tf_op jit(solution)/shard_map/ppermute | solution.py:65
  43.0 10.6 %collective-permute-done.9.refs_2_ = bf16[1,704,128]{2,1,0:T(8,128)(2,1)S(1)} collective-permute-done((bf16[1,704,128]{2,1,0:T(8,128)(2,1)S(1)}, bf16[1,704,128]{2,1,0:T(8,128)(2,1)S(1)}, u32[]{:S(2)}, u32[]{:S(2)}) %collective-permute-start.9) | collective-permute-done | bytes 180256 | tf_op jit(solution)/shard_map/ppermute | solution.py:65
  54.9 2.6 collective-permute-start.17
  58.5 9.9 %prepare.1 = (bf16[1408,1024]{1,0:T(8,128)(2,1)}, bf16[1408,1024]{1,0:T(8,128)(2,1)}) custom-call(s32[1]{0:T(128)} %bitcast.3.begin_ref, s32[8]{0:T(128)} %stack.95.order_ref, bf16[2304,1024]{1,0:T(8,128)(2,1)} %x_ref), custom_call_target="tpu_custom_call" | custom-call | flops 5767168 | bytes 8650752 | tf_op jit(solution)/shard_map/prepare/pallas_call | solution.py:350
  68.4 2.9 join.8.refs_1_
  76.3 10.7 %collective-permute-done.16.refs_2_ = bf16[2,704,128]{2,1,0:T(8,128)(2,1)} collective-permute-done((bf16[2,704,128]{2,1,0:T(8,128)(2,1)}, bf16[2,704,128]{2,1,0:T(8,128)(2,1)}, u32[]{:S(2)}, u32[]{:S(2)}) %collective-permute-start.16) | collective-permute-done | bytes 360480 | tf_op jit(solution)/shard_map/ppermute | solution.py:65
  90.1 11.3 %enc_block.2.refs_0_ = bf16[1152,256]{1,0:T(8,128)(2,1)S(1)} custom-call(s32[2]{0:T(128)S(1)} %pad_add_fusion.active_ref, s32[2,24]{1,0:T(2,128)S(1)} %get-tuple-element.233.query_ref, s32[2,24]{1,0:T(2,128)S(1)} %get-tuple-element.232.key_ref, s32[1]{0:T(128)} %bitcast.16.first_ref, bf16[1408,1024]{1,0:T(8,128)(2,1)S(1)} %copy-done.10, ...), custom_call_target="tpu_custom_call" | custom-call | flops 3321888768 | bytes 2883584 | tf_op jit(solution)/shard_map/enc_block/pallas_call | solution.py:513
  101.5 11.3 %enc_block.3.refs_3_ = bf16[1152,256]{1,0:T(8,128)(2,1)S(1)} custom-call(s32[2]{0:T(128)S(1)} %pad_add_fusion.active_ref, s32[2,24]{1,0:T(2,128)S(1)} %get-tuple-element.233.query_ref, s32[2,24]{1,0:T(2,128)S(1)} %get-tuple-element.232.key_ref, s32[1]{0:T(128)} %bitcast.16.first_ref, bf16[1408,1024]{1,0:T(8,128)(2,1)S(1)} %copy-done.11, ...), custom_call_target="tpu_custom_call" | custom-call | flops 3321888768 | bytes 2883584 | tf_op jit(solution)/shard_map/enc_block/pallas_call | solution.py:513
  117.0 3.2 collective-permute-done.24
  120.2 2.4 fusion.2
  124.3 2.5 join.9.refs_3_.refs_1_
  126.8 2.2 collective-permute-start.19
  131.3 4.0 %collective-permute-start.22 = (bf16[6,2,128,128]{3,2,1,0:T(8,128)(2,1)S(1)}, bf16[6,2,128,128]{3,2,1,0:T(8,128)(2,1)S(1)}, u32[]{:S(2)}, u32[]{:S(2)}) collective-permute-start(bf16[6,2,128,128]{3,2,1,0:T(8,128)(2,1)S(1)} %pad_maximum_fusion.4.refs_0_), channel_id=1, source_target_pairs={{0,16},{4,20},{8,24},{12,28},{16,0},{20,4},{24,8},{28,12},{1,17},{... | collective-permute-start | bytes 1179656 | tf_op jit(solution)/shard_map/ppermute | solution.py:65
  138.7 5.7 %collective-permute-done.23.refs_3_ = bf16[6,2,128,128]{3,2,1,0:T(8,128)(2,1)S(1)} collective-permute-done((bf16[6,2,128,128]{3,2,1,0:T(8,128)(2,1)S(1)}, bf16[6,2,128,128]{3,2,1,0:T(8,128)(2,1)S(1)}, u32[]{:S(2)}, u32[]{:S(2)}) %collective-permute-start.23) | collective-permute-done | bytes 393248 | tf_op jit(solution)/shard_map/ppermute | solution.py:65
  144.4 23.7 %collective-permute-done.22.refs_2_ = bf16[6,2,128,128]{3,2,1,0:T(8,128)(2,1)S(1)} collective-permute-done((bf16[6,2,128,128]{3,2,1,0:T(8,128)(2,1)S(1)}, bf16[6,2,128,128]{3,2,1,0:T(8,128)(2,1)S(1)}, u32[]{:S(2)}, u32[]{:S(2)}) %collective-permute-start.22) | collective-permute-done | bytes 393248 | tf_op jit(solution)/shard_map/ppermute | solution.py:65
  171.1 2.6 join.10
  173.7 3.7 self_block.1
  179.8 2.6 collective-permute-start.32
  185.4 11.8 %collective-permute-done.18.refs_2_ = bf16[1,704,512]{2,1,0:T(8,128)(2,1)} collective-permute-done((bf16[1,704,512]{2,1,0:T(8,128)(2,1)S(1)}, bf16[1,704,512]{2,1,0:T(8,128)(2,1)}, u32[]{:S(2)}, u32[]{:S(2)}) %collective-permute-start.18) | collective-permute-done | bytes 720928 | tf_op jit(solution)/shard_map/ppermute | solution.py:37
  200.7 5.9 %ff.4.refs_0_ = bf16[1152,704]{1,0:T(8,128)(2,1)S(1)} custom-call(bf16[1152,1024]{1,0:T(8,128)(2,1)} %pad_maximum_fusion.refs_0_, bf16[1,704,512]{2,1,0:T(8,128)(2,1)S(1)} %copy-done.7, bf16[1,704,512]{2,1,0:T(8,128)(2,1)S(1)} %copy-done.18, bf16[2,704,512]{2,1,0:T(8,128)(2,1)S(1)} %copy-done.6, bf16[2,704,512]{2,1,0:T(8,128)(2,1)} %collective-permute-done.19.refs_4_.refs_2_), custom_call_target="tpu_custom_call" | custom-call | flops 3321888768 | bytes 3981312 | tf_op jit(solution)/shard_map/ff/pallas_call | solution.py:253
  218.6 6.2 %ff.5.refs_3_ = bf16[1152,704]{1,0:T(8,128)(2,1)S(1)} custom-call(bf16[1152,1024]{1,0:T(8,128)(2,1)} %pad_maximum_fusion.refs_0_, bf16[1,704,512]{2,1,0:T(8,128)(2,1)S(1)} %copy-done.16, bf16[1,704,512]{2,1,0:T(8,128)(2,1)} %collective-permute-done.18.refs_2_, bf16[2,704,512]{2,1,0:T(8,128)(2,1)S(1)} %copy-done.13, ...), custom_call_target="tpu_custom_call" | custom-call | flops 3321888768 | bytes 3981312 | tf_op jit(solution)/shard_map/ff/pallas_call | solution.py:253
  224.8 2.2 collective-permute-done.33
  234.9 3.1 collective-permute-start.38
  238.0 7.4 %ff.6 = bf16[1152,1024]{1,0:T(8,128)(2,1)} custom-call(bf16[1152,704]{1,0:T(8,128)(2,1)} %copy-done.19, bf16[2,704,512]{2,1,0:T(8,128)(2,1)S(1)} %copy-done.6, bf16[2,704,512]{2,1,0:T(8,128)(2,1)} %collective-permute-done.19.refs_4_.refs_2_, bf16[1152,704]{1,0:T(8,128)(2,1)} %copy-done.20, bf16[2,704,512]{2,1,0:T(8,128)(2,1)S(1)} %copy-done.14, ...), custom_call_target="tpu_custom_call" | custom-call | flops 3321888768 | bytes 4718592 | tf_op jit(solution)/shard_map/ff/pallas_call | solution.py:253
  247.0 2.8 collective-permute-done.47
  259.5 5.5 %collective-permute-done.44 = bf16[1024,128]{1,0:T(8,128)(2,1)S(1)} collective-permute-done((bf16[1024,128]{1,0:T(8,128)(2,1)}, bf16[1024,128]{1,0:T(8,128)(2,1)S(1)}, u32[]{:S(2)}, u32[]{:S(2)}) %collective-permute-start.44) | collective-permute-done | bytes 262176 | tf_op jit(solution)/shard_map/ppermute | solution.py:83
  267.8 2.8 collective-permute-done.51.refs_3_
  273.3 29.0 %collective-permute-done.50.refs_2_ = bf16[6,352,128]{2,1,0:T(8,128)(2,1)} collective-permute-done((bf16[6,352,128]{2,1,0:T(8,128)(2,1)S(1)}, bf16[6,352,128]{2,1,0:T(8,128)(2,1)}, u32[]{:S(2)}, u32[]{:S(2)}) %collective-permute-start.50) | collective-permute-done | bytes 540704 | tf_op jit(solution)/shard_map/ppermute | solution.py:65
  302.3 2.9 join.13.refs_1_
  306.1 2.2 broadcast_select_fusion.1
  308.5 7.1 %cross_block.3 = bf16[4,2,272,128]{3,2,1,0:T(8,128)(2,1)S(1)} custom-call(s32[2]{0:T(128)S(1)} %pad_add_fusion.1.active_ref, s32[24]{0:T(128)S(1)} %get-tuple-element.183.begin_ref, s32[24]{0:T(128)S(1)} %get-tuple-element.184.end_ref, s32[24]{0:T(128)S(1)} %get-tuple-element.234.question_ref, s32[1]{0:T(128)} %bitcast.24.x_ref, ...), custom_call_target="tpu_custom_call" | custom-call | flops 1811939328 | bytes 2359296 | tf_op jit(solution)/shard_map/cross_block/pallas_call | solution.py:653
  316.5 7.1 %cross_block.2 = bf16[4,2,272,128]{3,2,1,0:T(8,128)(2,1)S(1)} custom-call(s32[2]{0:T(128)S(1)} %pad_add_fusion.1.active_ref, s32[24]{0:T(128)S(1)} %get-tuple-element.183.begin_ref, s32[24]{0:T(128)S(1)} %get-tuple-element.184.end_ref, s32[24]{0:T(128)S(1)} %get-tuple-element.234.question_ref, s32[1]{0:T(128)} %bitcast.24.x_ref, ...), custom_call_target="tpu_custom_call" | custom-call | flops 1811939328 | bytes 2359296 | tf_op jit(solution)/shard_map/cross_block/pallas_call | solution.py:653
  326.0 5.4 %collective-permute-done.52 = bf16[4,272,128]{2,1,0:T(8,128)(2,1)S(1)} collective-permute-done((bf16[4,272,128]{2,1,0:T(8,128)(2,1)S(1)}, bf16[4,272,128]{2,1,0:T(8,128)(2,1)S(1)}, u32[]{:S(2)}, u32[]{:S(2)}) %collective-permute-start.52) | collective-permute-done | bytes 278560 | tf_op jit(solution)/shard_map/ppermute | solution.py:83
  333.0 2.2 collective-permute-start.57
  345.7 3.3 collective-permute-done.59
  352.1 2.8 collective-permute-done.62
  358.0 2.3 ff.7
  365.0 4.4 %collective-permute-done.66 = bf16[128,2,2,128]{0,3,1,2:T(8,128)(2,1)S(1)} collective-permute-done((bf16[128,2,2,128]{0,3,1,2:T(8,128)(2,1)S(1)}, bf16[128,2,2,128]{0,3,1,2:T(8,128)(2,1)S(1)}, u32[]{:S(2)}, u32[]{:S(2)}) %collective-permute-start.66) | collective-permute-done | bytes 131104 | tf_op jit(solution)/shard_map/ppermute | solution.py:37
  371.1 2.7 collective-permute-done.67
  (332 shorter events, 108.6 us)
Async XLA Ops:
  1.8 10.9 %collective-permute-start.3 = (bf16[6,128,128]{2,1,0:T(8,128)(2,1)S(1)}, bf16[6,128,128]{2,1,0:T(8,128)(2,1)}, u32[]{:S(2)}, u32[]{:S(2)}) collective-permute-start(bf16[6,128,128]{2,1,0:T(8,128)(2,1)S(1)} %get-tuple-element.209), channel_id=1, source_target_pairs={{0,4},{4,0},{8,12},{12,8},{16,20},{20,16},{24,28},{28,24},{1,5},{5... | collective-permute-start | bytes 589832 | tf_op jit(solution)/shard_map/ppermute | solution.py:37
  6.5 22.7 %collective-permute-start.4 = (bf16[3,352,128]{2,1,0:T(8,128)(2,1)S(1)}, bf16[3,352,128]{2,1,0:T(8,128)(2,1)S(1)}, u32[]{:S(2)}, u32[]{:S(2)}) collective-permute-start(bf16[3,352,128]{2,1,0:T(8,128)(2,1)S(1)} %get-tuple-element.195), channel_id=1, source_target_pairs={{0,4},{4,0},{8,12},{12,8},{16,20},{20,16},{24,28},{28,24},{1,5},{5... | collective-permute-start | bytes 811016 | tf_op jit(solution)/shard_map/ppermute | solution.py:37
  6.5 14.5 %collective-permute-start.5 = (bf16[128,1024]{1,0:T(8,128)(2,1)}, bf16[128,1024]{1,0:T(8,128)(2,1)S(1)}, u32[]{:S(2)}, u32[]{:S(2)}) collective-permute-start(bf16[128,1024]{1,0:T(8,128)(2,1)} %param.12), channel_id=1, source_target_pairs={{0,4},{4,0},{8,12},{12,8},{16,20},{20,16},{24,28},{28,24},{1,5},{5... | collective-permute-start | bytes 786440 | tf_op jit(solution)/shard_map/ppermute | solution.py:37
  8.6 17.0 %collective-permute-start.1 = (bf16[4,128,256]{2,1,0:T(8,128)(2,1)}, bf16[4,128,256]{2,1,0:T(8,128)(2,1)S(1)}, u32[]{:S(2)}, u32[]{:S(2)}) collective-permute-start(bf16[4,128,256]{2,1,0:T(8,128)(2,1)} %refs_0_), channel_id=1, source_target_pairs={{0,16},{4,20},{8,24},{12,28},{16,0},{20,4},{24,8},{28,12},{1,17},{... | collective-permute-start | bytes 786440 | tf_op jit(solution)/shard_map/ppermute | solution.py:65
  11.1 14.4 %collective-permute-start = (bf16[4,128,256]{2,1,0:T(8,128)(2,1)}, bf16[4,128,256]{2,1,0:T(8,128)(2,1)S(1)}, u32[]{:S(2)}, u32[]{:S(2)}) collective-permute-start(bf16[4,128,256]{2,1,0:T(8,128)(2,1)} %refs_0_), channel_id=1, source_target_pairs={{0,8},{4,12},{8,0},{12,4},{16,24},{20,28},{24,16},{28,20},{1,9},{5... | collective-permute-start | bytes 786440 | tf_op jit(solution)/shard_map/ppermute | solution.py:65
  12.7 16.5 %collective-permute-start.2 = (bf16[4,128,256]{2,1,0:T(8,128)(2,1)}, bf16[4,128,256]{2,1,0:T(8,128)(2,1)S(1)}, u32[]{:S(2)}, u32[]{:S(2)}) collective-permute-start(bf16[4,128,256]{2,1,0:T(8,128)(2,1)} %refs_0_), channel_id=1, source_target_pairs={{0,24},{4,28},{8,16},{12,20},{16,8},{20,12},{24,0},{28,4},{1,25},{... | collective-permute-start | bytes 786440 | tf_op jit(solution)/shard_map/ppermute | solution.py:65
  32.4 36.0 %collective-permute-start.7 = (bf16[4,512,256]{2,1,0:T(8,128)(2,1)}, bf16[4,512,256]{2,1,0:T(8,128)(2,1)S(1)}, u32[]{:S(2)}, u32[]{:S(2)}) collective-permute-start(bf16[4,512,256]{2,1,0:T(8,128)(2,1)} %join.7.refs_0_.refs_1_), channel_id=1, source_target_pairs={{0,2},{1,3},{2,0},{3,1},{4,6},{5,7},{6,4},{7,5},{8,10},{9,11},{10,... | collective-permute-start | bytes 3145736 | tf_op jit(solution)/shard_map/ppermute | solution.py:83
  34.0 34.5 %collective-permute-start.6 = (bf16[4,512,256]{2,1,0:T(8,128)(2,1)}, bf16[4,512,256]{2,1,0:T(8,128)(2,1)S(1)}, u32[]{:S(2)}, u32[]{:S(2)}) collective-permute-start(bf16[4,512,256]{2,1,0:T(8,128)(2,1)} %join.7.refs_0_.refs_1_), channel_id=1, source_target_pairs={{0,4},{4,0},{8,12},{12,8},{16,20},{20,16},{24,28},{28,24},{1,5},{5... | collective-permute-start | bytes 3145736 | tf_op jit(solution)/shard_map/ppermute | solution.py:37
  34.5 8.5 %collective-permute-start.10 = (bf16[1,704,128]{2,1,0:T(8,128)(2,1)S(1)}, bf16[1,704,128]{2,1,0:T(8,128)(2,1)S(1)}, u32[]{:S(2)}, u32[]{:S(2)}) collective-permute-start(bf16[1,704,128]{2,1,0:T(8,128)(2,1)S(1)} %slice.101.refs_0_), channel_id=1, source_target_pairs={{0,24},{4,28},{8,16},{12,20},{16,8},{20,12},{24,0},{28,4},{1,25},{... | collective-permute-start | bytes 540680 | tf_op jit(solution)/shard_map/ppermute | solution.py:65
  37.1 16.5 %collective-permute-start.9 = (bf16[1,704,128]{2,1,0:T(8,128)(2,1)S(1)}, bf16[1,704,128]{2,1,0:T(8,128)(2,1)S(1)}, u32[]{:S(2)}, u32[]{:S(2)}) collective-permute-start(bf16[1,704,128]{2,1,0:T(8,128)(2,1)S(1)} %slice.101.refs_0_), channel_id=1, source_target_pairs={{0,16},{4,20},{8,24},{12,28},{16,0},{20,4},{24,8},{28,12},{1,17},{... | collective-permute-start | bytes 540680 | tf_op jit(solution)/shard_map/ppermute | solution.py:65
  41.7 11.8 %collective-permute-start.8 = (bf16[1,704,128]{2,1,0:T(8,128)(2,1)S(1)}, bf16[1,704,128]{2,1,0:T(8,128)(2,1)S(1)}, u32[]{:S(2)}, u32[]{:S(2)}) collective-permute-start(bf16[1,704,128]{2,1,0:T(8,128)(2,1)S(1)} %slice.101.refs_0_), channel_id=1, source_target_pairs={{0,8},{4,12},{8,0},{12,4},{16,24},{20,28},{24,16},{28,20},{1,9},{5... | collective-permute-start | bytes 540680 | tf_op jit(solution)/shard_map/ppermute | solution.py:65
  54.9 20.2 %collective-permute-start.17 = (bf16[2,704,128]{2,1,0:T(8,128)(2,1)}, bf16[2,704,128]{2,1,0:T(8,128)(2,1)}, u32[]{:S(2)}, u32[]{:S(2)}) collective-permute-start(bf16[2,704,128]{2,1,0:T(8,128)(2,1)} %slice.102.refs_0_), channel_id=1, source_target_pairs={{0,24},{4,28},{8,16},{12,20},{16,8},{20,12},{24,0},{28,4},{1,25},{... | collective-permute-start | bytes 1081352 | tf_op jit(solution)/shard_map/ppermute | solution.py:65
  58.4 28.6 %collective-permute-start.16 = (bf16[2,704,128]{2,1,0:T(8,128)(2,1)}, bf16[2,704,128]{2,1,0:T(8,128)(2,1)}, u32[]{:S(2)}, u32[]{:S(2)}) collective-permute-start(bf16[2,704,128]{2,1,0:T(8,128)(2,1)} %slice.102.refs_0_), channel_id=1, source_target_pairs={{0,16},{4,20},{8,24},{12,28},{16,0},{20,4},{24,8},{28,12},{1,17},{... | collective-permute-start | bytes 1081352 | tf_op jit(solution)/shard_map/ppermute | solution.py:65
  71.4 30.1 %collective-permute-start.14 = (bf16[1,704,512]{2,1,0:T(8,128)(2,1)}, bf16[1,704,512]{2,1,0:T(8,128)(2,1)S(1)}, u32[]{:S(2)}, u32[]{:S(2)}) collective-permute-start(bf16[1,704,512]{2,1,0:T(8,128)(2,1)} %join.8.refs_1_), channel_id=1, source_target_pairs={{0,2},{1,3},{2,0},{3,1},{4,6},{5,7},{6,4},{7,5},{8,10},{9,11},{10,... | collective-permute-start | bytes 2162696 | tf_op jit(solution)/shard_map/ppermute | solution.py:83
  71.9 29.5 %collective-permute-start.13 = (bf16[1,704,512]{2,1,0:T(8,128)(2,1)}, bf16[1,704,512]{2,1,0:T(8,128)(2,1)S(1)}, u32[]{:S(2)}, u32[]{:S(2)}) collective-permute-start(bf16[1,704,512]{2,1,0:T(8,128)(2,1)} %join.8.refs_1_), channel_id=1, source_target_pairs={{0,4},{4,0},{8,12},{12,8},{16,20},{20,16},{24,28},{28,24},{1,5},{5... | collective-permute-start | bytes 2162696 | tf_op jit(solution)/shard_map/ppermute | solution.py:37
  73.5 27.9 %collective-permute-start.12 = (bf16[4,256,256]{2,1,0:T(8,128)(2,1)S(1)}, bf16[4,256,256]{2,1,0:T(8,128)(2,1)S(1)}, u32[]{:S(2)}, u32[]{:S(2)}) collective-permute-start(bf16[4,256,256]{2,1,0:T(8,128)(2,1)S(1)} %slice.104), channel_id=1, source_target_pairs={{0,2},{1,3},{2,0},{3,1},{4,6},{5,7},{6,4},{7,5},{8,10},{9,11},{10,... | collective-permute-start | bytes 1572872 | tf_op jit(solution)/shard_map/ppermute | solution.py:83
  75.1 26.3 %collective-permute-start.11 = (bf16[4,256,256]{2,1,0:T(8,128)(2,1)S(1)}, bf16[4,256,256]{2,1,0:T(8,128)(2,1)S(1)}, u32[]{:S(2)}, u32[]{:S(2)}) collective-permute-start(bf16[4,256,256]{2,1,0:T(8,128)(2,1)S(1)} %slice.103), channel_id=1, source_target_pairs={{0,4},{4,0},{8,12},{12,8},{16,20},{20,16},{24,28},{28,24},{1,5},{5... | collective-permute-start | bytes 1572872 | tf_op jit(solution)/shard_map/ppermute | solution.py:37
  87.0 14.4 %collective-permute-start.15 = (bf16[2,704,128]{2,1,0:T(8,128)(2,1)}, bf16[2,704,128]{2,1,0:T(8,128)(2,1)S(1)}, u32[]{:S(2)}, u32[]{:S(2)}) collective-permute-start(bf16[2,704,128]{2,1,0:T(8,128)(2,1)} %slice.102.refs_0_), channel_id=1, source_target_pairs={{0,8},{4,12},{8,0},{12,4},{16,24},{20,28},{24,16},{28,20},{1,9},{5... | collective-permute-start | bytes 1081352 | tf_op jit(solution)/shard_map/ppermute | solution.py:65
  123.0 12.3 %collective-permute-start.25 = (bf16[576,1024]{1,0:T(8,128)(2,1)S(1)}, bf16[576,1024]{1,0:T(8,128)(2,1)}, u32[]{:S(2)}, u32[]{:S(2)}) collective-permute-start(bf16[576,1024]{1,0:T(8,128)(2,1)S(1)} %fusion.3), channel_id=1, source_target_pairs={{0,1},{1,0},{2,3},{3,2},{4,5},{5,4},{6,7},{7,6},{8,9},{9,8},{10,11... | collective-permute-start | bytes 3538952 | tf_op jit(solution)/shard_map/ppermute | solution.py:42
  126.8 41.4 %collective-permute-start.20 = (bf16[2,704,512]{2,1,0:T(8,128)(2,1)}, bf16[2,704,512]{2,1,0:T(8,128)(2,1)S(1)}, u32[]{:S(2)}, u32[]{:S(2)}) collective-permute-start(bf16[2,704,512]{2,1,0:T(8,128)(2,1)} %join.9.refs_3_.refs_1_), channel_id=1, source_target_pairs={{0,2},{1,3},{2,0},{3,1},{4,6},{5,7},{6,4},{7,5},{8,10},{9,11},{10,... | collective-permute-start | bytes 4325384 | tf_op jit(solution)/shard_map/ppermute | solution.py:83
  126.8 42.6 %collective-permute-start.19 = (bf16[2,704,512]{2,1,0:T(8,128)(2,1)}, bf16[2,704,512]{2,1,0:T(8,128)(2,1)}, u32[]{:S(2)}, u32[]{:S(2)}) collective-permute-start(bf16[2,704,512]{2,1,0:T(8,128)(2,1)} %join.9.refs_3_.refs_1_), channel_id=1, source_target_pairs={{0,4},{4,0},{8,12},{12,8},{16,20},{20,16},{24,28},{28,24},{1,5},{5... | collective-permute-start | bytes 4325384 | tf_op jit(solution)/shard_map/ppermute | solution.py:37
  130.4 14.0 %collective-permute-start.23 = (bf16[6,2,128,128]{3,2,1,0:T(8,128)(2,1)S(1)}, bf16[6,2,128,128]{3,2,1,0:T(8,128)(2,1)S(1)}, u32[]{:S(2)}, u32[]{:S(2)}) collective-permute-start(bf16[6,2,128,128]{3,2,1,0:T(8,128)(2,1)S(1)} %pad_maximum_fusion.4.refs_0_), channel_id=1, source_target_pairs={{0,24},{4,28},{8,16},{12,20},{16,8},{20,12},{24,0},{28,4},{1,25},{... | collective-permute-start | bytes 1179656 | tf_op jit(solution)/shard_map/ppermute | solution.py:65
  131.3 36.9 %collective-permute-start.22 = (bf16[6,2,128,128]{3,2,1,0:T(8,128)(2,1)S(1)}, bf16[6,2,128,128]{3,2,1,0:T(8,128)(2,1)S(1)}, u32[]{:S(2)}, u32[]{:S(2)}) collective-permute-start(bf16[6,2,128,128]{3,2,1,0:T(8,128)(2,1)S(1)} %pad_maximum_fusion.4.refs_0_), channel_id=1, source_target_pairs={{0,16},{4,20},{8,24},{12,28},{16,0},{20,4},{24,8},{28,12},{1,17},{... | collective-permute-start | bytes 1179656 | tf_op jit(solution)/shard_map/ppermute | solution.py:65
  135.3 32.9 %collective-permute-start.21 = (bf16[6,2,128,128]{3,2,1,0:T(8,128)(2,1)S(1)}, bf16[6,2,128,128]{3,2,1,0:T(8,128)(2,1)S(1)}, u32[]{:S(2)}, u32[]{:S(2)}) collective-permute-start(bf16[6,2,128,128]{3,2,1,0:T(8,128)(2,1)S(1)} %pad_maximum_fusion.4.refs_0_), channel_id=1, source_target_pairs={{0,8},{4,12},{8,0},{12,4},{16,24},{20,28},{24,16},{28,20},{1,9},{5... | collective-permute-start | bytes 1179656 | tf_op jit(solution)/shard_map/ppermute | solution.py:65
  169.5 39.0 %collective-permute-start.26 = (bf16[2,704,512]{2,1,0:T(8,128)(2,1)}, bf16[2,704,512]{2,1,0:T(8,128)(2,1)}, u32[]{:S(2)}, u32[]{:S(2)}) collective-permute-start(bf16[2,704,512]{2,1,0:T(8,128)(2,1)} %collective-permute-done.19.refs_4_.refs_2_), channel_id=1, source_target_pairs={{0,2},{1,3},{2,0},{3,1},{4,6},{5,7},{6,4},{7,5},{8,10},{9,11},{10,... | collective-permute-start | bytes 4325384 | tf_op jit(solution)/shard_map/ppermute | solution.py:83
  178.6 18.6 %collective-permute-start.18 = (bf16[1,704,512]{2,1,0:T(8,128)(2,1)S(1)}, bf16[1,704,512]{2,1,0:T(8,128)(2,1)}, u32[]{:S(2)}, u32[]{:S(2)}) collective-permute-start(bf16[1,704,512]{2,1,0:T(8,128)(2,1)S(1)} %copy-done.16), channel_id=1, source_target_pairs={{0,4},{4,0},{8,12},{12,8},{16,20},{20,16},{24,28},{28,24},{1,5},{5... | collective-permute-start | bytes 2162696 | tf_op jit(solution)/shard_map/ppermute | solution.py:37
  179.8 18.8 %collective-permute-start.32 = (bf16[2,128,256]{2,1,0:T(8,128)(2,1)}, bf16[2,128,256]{2,1,0:T(8,128)(2,1)S(1)}, u32[]{:S(2)}, u32[]{:S(2)}) collective-permute-start(bf16[2,128,256]{2,1,0:T(8,128)(2,1)} %refs_0_.1), channel_id=1, source_target_pairs={{0,24},{4,28},{8,16},{12,20},{16,8},{20,12},{24,0},{28,4},{1,25},{... | collective-permute-start | bytes 393224 | tf_op jit(solution)/shard_map/ppermute | solution.py:65
  182.4 25.4 %collective-permute-start.31 = (bf16[2,128,256]{2,1,0:T(8,128)(2,1)}, bf16[2,128,256]{2,1,0:T(8,128)(2,1)S(1)}, u32[]{:S(2)}, u32[]{:S(2)}) collective-permute-start(bf16[2,128,256]{2,1,0:T(8,128)(2,1)} %refs_0_.1), channel_id=1, source_target_pairs={{0,16},{4,20},{8,24},{12,28},{16,0},{20,4},{24,8},{28,12},{1,17},{... | collective-permute-start | bytes 393224 | tf_op jit(solution)/shard_map/ppermute | solution.py:65
  182.4 25.4 %collective-permute-start.30 = (bf16[2,128,256]{2,1,0:T(8,128)(2,1)}, bf16[2,128,256]{2,1,0:T(8,128)(2,1)S(1)}, u32[]{:S(2)}, u32[]{:S(2)}) collective-permute-start(bf16[2,128,256]{2,1,0:T(8,128)(2,1)} %refs_0_.1), channel_id=1, source_target_pairs={{0,8},{4,12},{8,0},{12,4},{16,24},{20,28},{24,16},{28,20},{1,9},{5... | collective-permute-start | bytes 393224 | tf_op jit(solution)/shard_map/ppermute | solution.py:65
  197.2 10.6 %collective-permute-start.29 = (bf16[64,1024]{1,0:T(8,128)(2,1)S(1)}, bf16[64,1024]{1,0:T(8,128)(2,1)S(1)}, u32[]{:S(2)}, u32[]{:S(2)}) collective-permute-start(bf16[64,1024]{1,0:T(8,128)(2,1)S(1)} %get-tuple-element.140), channel_id=1, source_target_pairs={{0,2},{1,3},{2,0},{3,1},{4,6},{5,7},{6,4},{7,5},{8,10},{9,11},{10,... | collective-permute-start | bytes 393224 | tf_op jit(solution)/shard_map/ppermute | solution.py:83
  199.3 8.6 %collective-permute-start.28 = (bf16[64,1024]{1,0:T(8,128)(2,1)S(1)}, bf16[64,1024]{1,0:T(8,128)(2,1)S(1)}, u32[]{:S(2)}, u32[]{:S(2)}) collective-permute-start(bf16[64,1024]{1,0:T(8,128)(2,1)S(1)} %get-tuple-element.138), channel_id=1, source_target_pairs={{0,4},{4,0},{8,12},{12,8},{16,20},{20,16},{24,28},{28,24},{1,5},{5... | collective-permute-start | bytes 393224 | tf_op jit(solution)/shard_map/ppermute | solution.py:37
  211.1 17.2 %collective-permute-start.36 = (bf16[2,512,256]{2,1,0:T(8,128)(2,1)}, bf16[2,512,256]{2,1,0:T(8,128)(2,1)S(1)}, u32[]{:S(2)}, u32[]{:S(2)}) collective-permute-start(bf16[2,512,256]{2,1,0:T(8,128)(2,1)} %join.11.refs_3_), channel_id=1, source_target_pairs={{0,2},{1,3},{2,0},{3,1},{4,6},{5,7},{6,4},{7,5},{8,10},{9,11},{10,... | collective-permute-start | bytes 1572872 | tf_op jit(solution)/shard_map/ppermute | solution.py:83
  212.7 15.6 %collective-permute-start.35 = (bf16[2,512,256]{2,1,0:T(8,128)(2,1)}, bf16[2,512,256]{2,1,0:T(8,128)(2,1)S(1)}, u32[]{:S(2)}, u32[]{:S(2)}) collective-permute-start(bf16[2,512,256]{2,1,0:T(8,128)(2,1)} %join.11.refs_3_), channel_id=1, source_target_pairs={{0,4},{4,0},{8,12},{12,8},{16,20},{20,16},{24,28},{28,24},{1,5},{5... | collective-permute-start | bytes 1572872 | tf_op jit(solution)/shard_map/ppermute | solution.py:37
  214.4 12.6 %collective-permute-start.33 = (bf16[64,1024]{1,0:T(8,128)(2,1)S(1)}, bf16[64,1024]{1,0:T(8,128)(2,1)S(1)}, u32[]{:S(2)}, u32[]{:S(2)}) collective-permute-start(bf16[64,1024]{1,0:T(8,128)(2,1)S(1)} %add_convert_fusion.6), channel_id=1, source_target_pairs={{0,2},{1,3},{2,0},{3,1},{4,6},{5,7},{6,4},{7,5},{8,10},{9,11},{10,... | collective-permute-start | bytes 393224 | tf_op jit(solution)/shard_map/ppermute | solution.py:83
  216.9 11.4 %collective-permute-start.34 = (bf16[64,1024]{1,0:T(8,128)(2,1)S(1)}, bf16[64,1024]{1,0:T(8,128)(2,1)S(1)}, u32[]{:S(2)}, u32[]{:S(2)}) collective-permute-start(bf16[64,1024]{1,0:T(8,128)(2,1)S(1)} %add_convert_fusion.5), channel_id=1, source_target_pairs={{0,4},{4,0},{8,12},{12,8},{16,20},{20,16},{24,28},{28,24},{1,5},{5... | collective-permute-start | bytes 393224 | tf_op jit(solution)/shard_map/ppermute | solution.py:37
  230.7 14.6 %collective-permute-start.42 = (bf16[2,256,256]{2,1,0:T(8,128)(2,1)S(1)}, bf16[2,256,256]{2,1,0:T(8,128)(2,1)S(1)}, u32[]{:S(2)}, u32[]{:S(2)}) collective-permute-start(bf16[2,256,256]{2,1,0:T(8,128)(2,1)S(1)} %slice.113), channel_id=1, source_target_pairs={{0,2},{1,3},{2,0},{3,1},{4,6},{5,7},{6,4},{7,5},{8,10},{9,11},{10,... | collective-permute-start | bytes 786440 | tf_op jit(solution)/shard_map/ppermute | solution.py:83
  231.3 14.1 %collective-permute-start.41 = (bf16[2,256,256]{2,1,0:T(8,128)(2,1)S(1)}, bf16[2,256,256]{2,1,0:T(8,128)(2,1)S(1)}, u32[]{:S(2)}, u32[]{:S(2)}) collective-permute-start(bf16[2,256,256]{2,1,0:T(8,128)(2,1)S(1)} %slice.112), channel_id=1, source_target_pairs={{0,4},{4,0},{8,12},{12,8},{16,20},{20,16},{24,28},{28,24},{1,5},{5... | collective-permute-start | bytes 786440 | tf_op jit(solution)/shard_map/ppermute | solution.py:37
  233.5 11.8 %collective-permute-start.40 = (bf16[256,128]{1,0:T(8,128)(2,1)S(1)}, bf16[256,128]{1,0:T(8,128)(2,1)S(1)}, u32[]{:S(2)}, u32[]{:S(2)}) collective-permute-start(bf16[256,128]{1,0:T(8,128)(2,1)S(1)} %convolution_convert_fusion.1.refs_0_), channel_id=1, source_target_pairs={{0,24},{4,28},{8,16},{12,20},{16,8},{20,12},{24,0},{28,4},{1,25},{... | collective-permute-start | bytes 196616 | tf_op jit(solution)/shard_map/ppermute | solution.py:65
  234.9 10.5 %collective-permute-start.39 = (bf16[256,128]{1,0:T(8,128)(2,1)S(1)}, bf16[256,128]{1,0:T(8,128)(2,1)S(1)}, u32[]{:S(2)}, u32[]{:S(2)}) collective-permute-start(bf16[256,128]{1,0:T(8,128)(2,1)S(1)} %convolution_convert_fusion.1.refs_0_), channel_id=1, source_target_pairs={{0,16},{4,20},{8,24},{12,28},{16,0},{20,4},{24,8},{28,12},{1,17},{... | collective-permute-start | bytes 196616 | tf_op jit(solution)/shard_map/ppermute | solution.py:65
  234.9 10.5 %collective-permute-start.38 = (bf16[256,128]{1,0:T(8,128)(2,1)S(1)}, bf16[256,128]{1,0:T(8,128)(2,1)S(1)}, u32[]{:S(2)}, u32[]{:S(2)}) collective-permute-start(bf16[256,128]{1,0:T(8,128)(2,1)S(1)} %convolution_convert_fusion.1.refs_0_), channel_id=1, source_target_pairs={{0,8},{4,12},{8,0},{12,4},{16,24},{20,28},{24,16},{28,20},{1,9},{5... | collective-permute-start | bytes 196616 | tf_op jit(solution)/shard_map/ppermute | solution.py:65
  253.1 53.0 %collective-permute-start.48 = (bf16[576,1024]{1,0:T(8,128)(2,1)}, bf16[576,1024]{1,0:T(8,128)(2,1)}, u32[]{:S(2)}, u32[]{:S(2)}) collective-permute-start(bf16[576,1024]{1,0:T(8,128)(2,1)} %fusion.1), channel_id=1, source_target_pairs={{0,1},{1,0},{2,3},{3,2},{4,5},{5,4},{6,7},{7,6},{8,9},{9,8},{10,11... | collective-permute-start | bytes 3538952 | tf_op jit(solution)/shard_map/ppermute | solution.py:42
  253.3 17.3 %collective-permute-start.51 = (bf16[6,352,128]{2,1,0:T(8,128)(2,1)S(1)}, bf16[6,352,128]{2,1,0:T(8,128)(2,1)}, u32[]{:S(2)}, u32[]{:S(2)}) collective-permute-start(bf16[6,352,128]{2,1,0:T(8,128)(2,1)S(1)} %bitcast.120), channel_id=1, source_target_pairs={{0,24},{4,28},{8,16},{12,20},{16,8},{20,12},{24,0},{28,4},{1,25},{... | collective-permute-start | bytes 1622024 | tf_op jit(solution)/shard_map/ppermute | solution.py:65
  256.4 8.6 %collective-permute-start.44 = (bf16[1024,128]{1,0:T(8,128)(2,1)}, bf16[1024,128]{1,0:T(8,128)(2,1)S(1)}, u32[]{:S(2)}, u32[]{:S(2)}) collective-permute-start(bf16[1024,128]{1,0:T(8,128)(2,1)} %join.12), channel_id=1, source_target_pairs={{0,2},{1,3},{2,0},{3,1},{4,6},{5,7},{6,4},{7,5},{8,10},{9,11},{10,... | collective-permute-start | bytes 786440 | tf_op jit(solution)/shard_map/ppermute | solution.py:83
  259.5 42.8 %collective-permute-start.50 = (bf16[6,352,128]{2,1,0:T(8,128)(2,1)S(1)}, bf16[6,352,128]{2,1,0:T(8,128)(2,1)}, u32[]{:S(2)}, u32[]{:S(2)}) collective-permute-start(bf16[6,352,128]{2,1,0:T(8,128)(2,1)S(1)} %bitcast.121), channel_id=1, source_target_pairs={{0,16},{4,20},{8,24},{12,28},{16,0},{20,4},{24,8},{28,12},{1,17},{... | collective-permute-start | bytes 1622024 | tf_op jit(solution)/shard_map/ppermute | solution.py:65
  265.0 37.3 %collective-permute-start.49 = (bf16[6,352,128]{2,1,0:T(8,128)(2,1)S(1)}, bf16[6,352,128]{2,1,0:T(8,128)(2,1)}, u32[]{:S(2)}, u32[]{:S(2)}) collective-permute-start(bf16[6,352,128]{2,1,0:T(8,128)(2,1)S(1)} %bitcast.122), channel_id=1, source_target_pairs={{0,8},{4,12},{8,0},{12,4},{16,24},{20,28},{24,16},{28,20},{1,9},{5... | collective-permute-start | bytes 1622024 | tf_op jit(solution)/shard_map/ppermute | solution.py:65
  266.0 39.1 %collective-permute-start.45 = (bf16[512,128]{1,0:T(8,128)(2,1)S(1)}, bf16[512,128]{1,0:T(8,128)(2,1)S(1)}, u32[]{:S(2)}, u32[]{:S(2)}) collective-permute-start(bf16[512,128]{1,0:T(8,128)(2,1)S(1)} %slice.136), channel_id=1, source_target_pairs={{0,4},{4,0},{8,12},{12,8},{16,20},{20,16},{24,28},{28,24},{1,5},{5... | collective-permute-start | bytes 393224 | tf_op jit(solution)/shard_map/ppermute | solution.py:37
  270.6 34.6 %collective-permute-start.46 = (bf16[512,128]{1,0:T(8,128)(2,1)S(1)}, bf16[512,128]{1,0:T(8,128)(2,1)}, u32[]{:S(2)}, u32[]{:S(2)}) collective-permute-start(bf16[512,128]{1,0:T(8,128)(2,1)S(1)} %slice.137), channel_id=1, source_target_pairs={{0,2},{1,3},{2,0},{3,1},{4,6},{5,7},{6,4},{7,5},{8,10},{9,11},{10,... | collective-permute-start | bytes 393224 | tf_op jit(solution)/shard_map/ppermute | solution.py:83
  315.7 9.4 %collective-permute-start.53 = (bf16[4,272,128]{2,1,0:T(8,128)(2,1)S(1)}, bf16[4,272,128]{2,1,0:T(8,128)(2,1)S(1)}, u32[]{:S(2)}, u32[]{:S(2)}) collective-permute-start(bf16[4,272,128]{2,1,0:T(8,128)(2,1)S(1)} %get-tuple-element.194), channel_id=1, source_target_pairs={{0,2},{1,3},{2,0},{3,1},{4,6},{5,7},{6,4},{7,5},{8,10},{9,11},{10,... | collective-permute-start | bytes 835592 | tf_op jit(solution)/shard_map/ppermute | solution.py:83
  (80 other events, 702.7 us)

commit v4 on v2

--- a/solution.py
+++ b/solution.py
@@ -844,14 +844,16 @@
     def attend(parts):
         return enc_block(low, high, own_begin, seg_q, seg_k, normed, parts)
 
+    dec_attn_own = jnp.stack(dec_attn_pair, axis=1)
+    dec_ff_own = jnp.stack(dec_ff_pair, axis=1).reshape(-1, *dec_ff_pair[0].shape[1:])
     if size_y == 2:
         mixes = [attend([attn_block, attn_near[0]])]
-        attn_far, gate_near, rest_z, mixes, w_cross_kv, dec_attn_pair = meet(
-            attn_far, gate_near, rest_z, mixes, w_cross_kv, dec_attn_pair
+        attn_far, gate_near, rest_z, mixes, w_cross_kv, dec_attn_own, dec_ff_own, answer_normed = meet(
+            attn_far, gate_near, rest_z, mixes, w_cross_kv, dec_attn_own, dec_ff_own, answer_normed
         )
     rest_block = join(rest_z, 2)
     rest_near = spread_near(rest_block)
-    dec_attn_z = pieces_z(jnp.stack(dec_attn_pair, axis=1), 2)
+    dec_attn_z = pieces_z(dec_attn_own, 2)
     attn_weights = attn_pieces(attn_block, attn_near, attn_far)
     if size_y == 2:
         mixes.append(attend(attn_weights[1]))
@@ -862,13 +864,13 @@
     first_rows = (own_embeds.astype(F32) + core_rows_sum(partial, core)).astype(BF16)
     normed = both_cores(rms_normed(first_rows), core)
 
-    rest_near, dec_attn_z, normed, w_cross_kv, dec_ff_pair = meet(
-        rest_near, dec_attn_z, normed, w_cross_kv, dec_ff_pair
+    rest_near, dec_attn_z, normed, w_cross_kv, dec_ff_own = meet(
+        rest_near, dec_attn_z, normed, w_cross_kv, dec_ff_own
     )
     gate_far = (swap_x(gate_near[1]),) if size_y == 2 else ()
     rest_far = (swap_y(rest_near[0]),) if size_y == 2 else ()
     cross_z = pieces_z(w_cross_kv, 1)
-    dec_ff_z = pieces_z(jnp.stack(dec_ff_pair, axis=1).reshape(-1, *dec_ff_pair[0].shape[1:]), 2)
+    dec_ff_z = pieces_z(dec_ff_own, 2)
     dec_attn = join(dec_attn_z, 2).reshape(w_dec_attn.shape[0], features, -1)
     self_partial = self_block(answer_normed, dec_attn, 2)
     exchange = answer_start(self_partial, core, size_y)

time: 373 us -> 369 us (0.989)
  waiting for transfers between devices: 157 us -> 145 us
  starting transfers between devices: 74.1 us -> 77.9 us
    ppermute x24, waiting for transfers between devices: 96.2 us -> 82 us  [swap_z(): return lax.ppermute(value, 'dp', [(i, i ^ 2 * step) for i in range(count)])]
    ppermute x16, waiting for transfers between devices: 18.5 us -> 22.6 us  [swap_y(): return lax.ppermute(value, 'mp', [(i, i ^ 2) for i in range(4)])]
    unnamed x113 -> x105, local copies, waits for them, and re-layouts: 12 us -> 12.1 us
  transfers between devices with their start and end apart: 68 -> 68, of which waited for: 30 -> 34; matrix products, arithmetic and copies ran while one was open for 6% -> 7% of each run, Pallas kernels for 17% -> 18%
where the time goes in v4:
time: 369 us; the launch traced here: 368 us
  waiting for transfers between devices  145 us (39%)
  Pallas kernels  90.5 us (25%)
  starting transfers between devices  77.9 us (21%)
  local copies, waits for them, and re-layouts  27.8 us (8%)
  other arithmetic  24.7 us (7%)
    ppermute x24, waiting for transfers between devices, swap_z(): return lax.ppermute(value, 'dp', [(i, i ^ 2 * step) for i in range(count)])  82 us
    ppermute x24, starting transfers between devices, swap_z(): return lax.ppermute(value, 'dp', [(i, i ^ 2 * step) for i in range(count)])  37.6 us
    ppermute x18, waiting for transfers between devices, swap_x(): return lax.ppermute(value, 'dp', [(i, i ^ 1) for i in range(count)])  31 us
    ppermute x16, waiting for transfers between devices, swap_y(): return lax.ppermute(value, 'mp', [(i, i ^ 2) for i in range(4)])  22.6 us
    pallas_call x4, Pallas kernels, ff(): pl.pallas_call(functools.partial(ff_kernel, chunks=plan, done=before, las...  22.2 us
    pallas_call x2, Pallas kernels, enc_block(): pl.pallas_call(functools.partial(enc_block_kernel, rows=query_rows), out_...  21.1 us
    ppermute x18, starting transfers between devices, swap_x(): return lax.ppermute(value, 'dp', [(i, i ^ 1) for i in range(count)])  21 us
    ppermute x16, starting transfers between devices, swap_y(): return lax.ppermute(value, 'mp', [(i, i ^ 2) for i in range(4)])  18 us
  transfers between devices with their start and end apart: 68, of which 34 were waited for; matrix products, arithmetic and copies ran while one was open for 7% of the time, Pallas kernels for 18%

profile of v4, /device:TPU:0, one launch (start us, length us, event | category | flops | bytes accessed | tf_op | source)
XLA Modules:
  0.0 367.8 jit_solution(11971874747994810032)
XLA Ops:
  1.8 3.0 collective-permute-start.3
  4.8 2.6 collective-permute-start.1
  14.8 3.7 %collective-permute-done.5 = bf16[128,1024]{1,0:T(8,128)(2,1)S(1)} collective-permute-done((bf16[128,1024]{1,0:T(8,128)(2,1)}, bf16[128,1024]{1,0:T(8,128)(2,1)S(1)}, u32[]{:S(2)}, u32[]{:S(2)}) %collective-permute-start.5) | collective-permute-done | bytes 262176 | tf_op jit(solution)/shard_map/ppermute | solution.py:37
  18.5 3.2 collective-permute-done.1.refs_2_
  21.8 4.2 %collective-permute-done.2.refs_3_ = bf16[4,128,256]{2,1,0:T(8,128)(2,1)S(1)} collective-permute-done((bf16[4,128,256]{2,1,0:T(8,128)(2,1)}, bf16[4,128,256]{2,1,0:T(8,128)(2,1)S(1)}, u32[]{:S(2)}, u32[]{:S(2)}) %collective-permute-start.2) | collective-permute-done | bytes 262176 | tf_op jit(solution)/shard_map/ppermute | solution.py:65
  26.1 2.5 collective-permute-start.10
  28.6 8.5 %collective-permute-start.9 = (bf16[1,704,128]{2,1,0:T(8,128)(2,1)S(1)}, bf16[1,704,128]{2,1,0:T(8,128)(2,1)}, u32[]{:S(2)}, u32[]{:S(2)}) collective-permute-start(bf16[1,704,128]{2,1,0:T(8,128)(2,1)S(1)} %slice.101.refs_0_), channel_id=1, source_target_pairs={{0,16},{4,20},{8,24},{12,28},{16,0},{20,4},{24,8},{28,12},{1,17},{... | collective-permute-start | bytes 540680 | tf_op jit(solution)/shard_map/ppermute | solution.py:65
  38.4 2.2 join.7.refs_0_.refs_1_
  45.2 4.4 %collective-permute-done.9.refs_2_ = bf16[1,704,128]{2,1,0:T(8,128)(2,1)} collective-permute-done((bf16[1,704,128]{2,1,0:T(8,128)(2,1)S(1)}, bf16[1,704,128]{2,1,0:T(8,128)(2,1)}, u32[]{:S(2)}, u32[]{:S(2)}) %collective-permute-start.9) | collective-permute-done | bytes 180256 | tf_op jit(solution)/shard_map/ppermute | solution.py:65
  49.6 2.6 collective-permute-start.17
  52.4 9.9 %prepare.1 = (bf16[1408,1024]{1,0:T(8,128)(2,1)}, bf16[1408,1024]{1,0:T(8,128)(2,1)}) custom-call(s32[1]{0:T(128)} %bitcast.3.begin_ref, s32[8]{0:T(128)} %stack.78.order_ref, bf16[2304,1024]{1,0:T(8,128)(2,1)} %x_ref), custom_call_target="tpu_custom_call" | custom-call | flops 5767168 | bytes 8650752 | tf_op jit(solution)/shard_map/prepare/pallas_call | solution.py:350
  62.4 3.0 collective-permute-done.7.refs_0_.refs_4_
  66.7 2.5 join.8.refs_1_
  76.7 5.1 %collective-permute-done.16.refs_2_ = bf16[2,704,128]{2,1,0:T(8,128)(2,1)} collective-permute-done((bf16[2,704,128]{2,1,0:T(8,128)(2,1)}, bf16[2,704,128]{2,1,0:T(8,128)(2,1)}, u32[]{:S(2)}, u32[]{:S(2)}) %collective-permute-start.16) | collective-permute-done | bytes 360480 | tf_op jit(solution)/shard_map/ppermute | solution.py:65
  85.9 10.2 %enc_block.2.refs_0_ = bf16[1152,256]{1,0:T(8,128)(2,1)S(1)} custom-call(s32[3]{0:T(128)S(1)} %get-tuple-element.231.low_ref, s32[3]{0:T(128)S(1)} %get-tuple-element.230.high_ref, s32[1]{0:T(128)} %bitcast.14.first_ref, s32[1152,128]{1,0:T(8,128)S(1)} %broadcast_in_dim.27.seg_q_ref, s32[11,1,128]{2,1,0:T(1,128)S(1)} %reshape.182.seg_k_ref, ...), custom_call_target="tpu_custom_call" | custom-call | flops 3321888768 | bytes 2883584 | tf_op jit(solution)/shard_map/enc_block/pallas_call | solution.py:474
  97.8 10.9 %enc_block.3.refs_3_ = bf16[1152,256]{1,0:T(8,128)(2,1)S(1)} custom-call(s32[3]{0:T(128)S(1)} %get-tuple-element.231.low_ref, s32[3]{0:T(128)S(1)} %get-tuple-element.230.high_ref, s32[1]{0:T(128)} %bitcast.14.first_ref, s32[1152,128]{1,0:T(8,128)S(1)} %broadcast_in_dim.27.seg_q_ref, s32[11,1,128]{2,1,0:T(1,128)S(1)} %reshape.182.seg_k_ref, ...), custom_call_target="tpu_custom_call" | custom-call | flops 3321888768 | bytes 2883584 | tf_op jit(solution)/shard_map/enc_block/pallas_call | solution.py:474
  110.0 3.1 out_project.1
  113.3 2.9 collective-permute-done.24
  116.2 2.4 fusion.2
  120.2 2.4 join.9.refs_3_.refs_1_
  132.5 6.0 %collective-permute-done.23.refs_3_ = bf16[6,2,128,128]{3,2,1,0:T(8,128)(2,1)S(1)} collective-permute-done((bf16[6,2,128,128]{3,2,1,0:T(8,128)(2,1)S(1)}, bf16[6,2,128,128]{3,2,1,0:T(8,128)(2,1)S(1)}, u32[]{:S(2)}, u32[]{:S(2)}) %collective-permute-start.23) | collective-permute-done | bytes 393248 | tf_op jit(solution)/shard_map/ppermute | solution.py:65
  138.5 23.1 %collective-permute-done.22.refs_2_ = bf16[6,2,128,128]{3,2,1,0:T(8,128)(2,1)S(1)} collective-permute-done((bf16[6,2,128,128]{3,2,1,0:T(8,128)(2,1)S(1)}, bf16[6,2,128,128]{3,2,1,0:T(8,128)(2,1)S(1)}, u32[]{:S(2)}, u32[]{:S(2)}) %collective-permute-start.22) | collective-permute-done | bytes 393248 | tf_op jit(solution)/shard_map/ppermute | solution.py:65
  164.2 2.5 join.10
  166.7 3.7 %self_block.1 = bf16[256,1024]{1,0:T(8,128)(2,1)} custom-call(bf16[256,1024]{1,0:T(8,128)(2,1)} %fusion.6.x_ref, bf16[6,1024,128]{2,1,0:T(8,128)(2,1)} %bitcast.114), custom_call_target="tpu_custom_call" | custom-call | flops 268435456 | bytes 1572864 | tf_op jit(solution)/shard_map/self_block/pallas_call | solution.py:678
  172.3 2.3 collective-permute-start.32
  177.8 12.5 %collective-permute-done.18.refs_2_ = bf16[1,704,512]{2,1,0:T(8,128)(2,1)S(1)} collective-permute-done((bf16[1,704,512]{2,1,0:T(8,128)(2,1)}, bf16[1,704,512]{2,1,0:T(8,128)(2,1)S(1)}, u32[]{:S(2)}, u32[]{:S(2)}) %collective-permute-start.18) | collective-permute-done | bytes 720928 | tf_op jit(solution)/shard_map/ppermute | solution.py:37
  192.8 6.1 %ff.4.refs_0_ = bf16[1152,704]{1,0:T(8,128)(2,1)S(1)} custom-call(bf16[1152,1024]{1,0:T(8,128)(2,1)} %pad_maximum_fusion.refs_0_, bf16[1,704,512]{2,1,0:T(8,128)(2,1)S(1)} %copy-done.7, bf16[1,704,512]{2,1,0:T(8,128)(2,1)} %collective-permute-done.13.refs_2_, bf16[2,704,512]{2,1,0:T(8,128)(2,1)S(1)} %copy-done.6, ...), custom_call_target="tpu_custom_call" | custom-call | flops 3321888768 | bytes 3981312 | tf_op jit(solution)/shard_map/ff/pallas_call | solution.py:253
  210.9 6.4 %ff.5.refs_3_ = bf16[1152,704]{1,0:T(8,128)(2,1)S(1)} custom-call(bf16[1152,1024]{1,0:T(8,128)(2,1)} %pad_maximum_fusion.refs_0_, bf16[1,704,512]{2,1,0:T(8,128)(2,1)} %collective-permute-done.14.refs_1_, bf16[1,704,512]{2,1,0:T(8,128)(2,1)S(1)} %collective-permute-done.18.refs_2_, bf16[2,704,512]{2,1,0:T(8,128)(2,1)S(1)} %copy-done.12, ...), custom_call_target="tpu_custom_call" | custom-call | flops 3321888768 | bytes 3981312 | tf_op jit(solution)/shard_map/ff/pallas_call | solution.py:253
  217.3 2.2 collective-permute-done.33
  224.1 2.3 collective-permute-start.40
  228.6 7.4 %ff.6 = bf16[1152,1024]{1,0:T(8,128)(2,1)} custom-call(bf16[1152,704]{1,0:T(8,128)(2,1)} %copy-done.14, bf16[2,704,512]{2,1,0:T(8,128)(2,1)S(1)} %copy-done.6, bf16[2,704,512]{2,1,0:T(8,128)(2,1)} %collective-permute-done.19.refs_4_.refs_2_, bf16[1152,704]{1,0:T(8,128)(2,1)} %copy-done.15, bf16[2,704,512]{2,1,0:T(8,128)(2,1)S(1)} %copy-done.13, ...), custom_call_target="tpu_custom_call" | custom-call | flops 3321888768 | bytes 4718592 | tf_op jit(solution)/shard_map/ff/pallas_call | solution.py:253
  237.6 2.8 collective-permute-done.47
  244.8 2.2 collective-permute-start.51
  251.2 6.1 %collective-permute-done.44 = bf16[1024,128]{1,0:T(8,128)(2,1)S(1)} collective-permute-done((bf16[1024,128]{1,0:T(8,128)(2,1)}, bf16[1024,128]{1,0:T(8,128)(2,1)S(1)}, u32[]{:S(2)}, u32[]{:S(2)}) %collective-permute-start.44) | collective-permute-done | bytes 262176 | tf_op jit(solution)/shard_map/ppermute | solution.py:83
  259.5 2.5 collective-permute-done.51.refs_3_
  265.6 28.0 %collective-permute-done.50.refs_2_ = bf16[6,352,128]{2,1,0:T(8,128)(2,1)S(1)} collective-permute-done((bf16[6,352,128]{2,1,0:T(8,128)(2,1)S(1)}, bf16[6,352,128]{2,1,0:T(8,128)(2,1)S(1)}, u32[]{:S(2)}, u32[]{:S(2)}) %collective-permute-start.50) | collective-permute-done | bytes 540704 | tf_op jit(solution)/shard_map/ppermute | solution.py:65
  294.4 3.0 join.13.refs_1_
  298.4 2.2 broadcast_select_fusion.1
  300.9 7.1 %cross_block.3 = bf16[4,2,272,128]{3,2,1,0:T(8,128)(2,1)S(1)} custom-call(s32[2]{0:T(128)S(1)} %pad_add_fusion.active_ref, s32[24]{0:T(128)S(1)} %get-tuple-element.181.begin_ref, s32[24]{0:T(128)S(1)} %get-tuple-element.182.end_ref, s32[24]{0:T(128)S(1)} %fusion.44.question_ref, s32[1]{0:T(128)} %bitcast.25.x_ref, bf16[8,128,128]{2,1,0:T(8,128)(2,1)S(1)} %bitcast.113, ...), custom_call_target="tpu_custom_call" | custom-call | flops 1811939328 | bytes 2359296 | tf_op jit(solution)/shard_map/cross_block/pallas_call | solution.py:622
  309.8 7.1 %cross_block.2 = bf16[4,2,272,128]{3,2,1,0:T(8,128)(2,1)S(1)} custom-call(s32[2]{0:T(128)S(1)} %pad_add_fusion.active_ref, s32[24]{0:T(128)S(1)} %get-tuple-element.181.begin_ref, s32[24]{0:T(128)S(1)} %get-tuple-element.182.end_ref, s32[24]{0:T(128)S(1)} %fusion.44.question_ref, s32[1]{0:T(128)} %bitcast.25.x_ref, bf16[8,128,128]{2,1,0:T(8,128)(2,1)S(1)} %bitcast.110, ...), custom_call_target="tpu_custom_call" | custom-call | flops 1811939328 | bytes 2359296 | tf_op jit(solution)/shard_map/cross_block/pallas_call | solution.py:622
  319.3 5.5 %collective-permute-done.52 = bf16[4,272,128]{2,1,0:T(8,128)(2,1)S(1)} collective-permute-done((bf16[4,272,128]{2,1,0:T(8,128)(2,1)S(1)}, bf16[4,272,128]{2,1,0:T(8,128)(2,1)S(1)}, u32[]{:S(2)}, u32[]{:S(2)}) %collective-permute-start.52) | collective-permute-done | bytes 278560 | tf_op jit(solution)/shard_map/ppermute | solution.py:83
  325.4 2.9 collective-permute-start.57
  329.6 2.4 collective-permute-done.57
  338.3 3.8 %collective-permute-done.59 = bf16[64,1024]{1,0:T(8,128)(2,1)S(1)} collective-permute-done((bf16[64,1024]{1,0:T(8,128)(2,1)S(1)}, bf16[64,1024]{1,0:T(8,128)(2,1)S(1)}, u32[]{:S(2)}, u32[]{:S(2)}) %collective-permute-start.59) | collective-permute-done | bytes 131104 | tf_op jit(solution)/shard_map/ppermute | solution.py:37
  344.9 2.9 collective-permute-done.62
  351.1 2.3 ff.7
  357.9 4.7 %collective-permute-done.66 = bf16[128,2,2,128]{0,3,1,2:T(8,128)(2,1)S(1)} collective-permute-done((bf16[128,2,2,128]{0,3,1,2:T(8,128)(2,1)S(1)}, bf16[128,2,2,128]{0,3,1,2:T(8,128)(2,1)S(1)}, u32[]{:S(2)}, u32[]{:S(2)}) %collective-permute-start.66) | collective-permute-done | bytes 131104 | tf_op jit(solution)/shard_map/ppermute | solution.py:37
  363.9 3.0 collective-permute-done.67
  (320 shorter events, 114.0 us)
Async XLA Ops:
  1.8 8.8 %collective-permute-start.3 = (bf16[6,128,128]{2,1,0:T(8,128)(2,1)S(1)}, bf16[6,128,128]{2,1,0:T(8,128)(2,1)S(1)}, u32[]{:S(2)}, u32[]{:S(2)}) collective-permute-start(bf16[6,128,128]{2,1,0:T(8,128)(2,1)S(1)} %get-tuple-element.207), channel_id=1, source_target_pairs={{0,4},{4,0},{8,12},{12,8},{16,20},{20,16},{24,28},{28,24},{1,5},{5... | collective-permute-start | bytes 589832 | tf_op jit(solution)/shard_map/ppermute | solution.py:37
  4.8 17.0 %collective-permute-start.1 = (bf16[4,128,256]{2,1,0:T(8,128)(2,1)}, bf16[4,128,256]{2,1,0:T(8,128)(2,1)S(1)}, u32[]{:S(2)}, u32[]{:S(2)}) collective-permute-start(bf16[4,128,256]{2,1,0:T(8,128)(2,1)} %refs_0_), channel_id=1, source_target_pairs={{0,16},{4,20},{8,24},{12,28},{16,0},{20,4},{24,8},{28,12},{1,17},{... | collective-permute-start | bytes 786440 | tf_op jit(solution)/shard_map/ppermute | solution.py:65
  7.3 14.4 %collective-permute-start = (bf16[4,128,256]{2,1,0:T(8,128)(2,1)}, bf16[4,128,256]{2,1,0:T(8,128)(2,1)S(1)}, u32[]{:S(2)}, u32[]{:S(2)}) collective-permute-start(bf16[4,128,256]{2,1,0:T(8,128)(2,1)} %refs_0_), channel_id=1, source_target_pairs={{0,8},{4,12},{8,0},{12,4},{16,24},{20,28},{24,16},{28,20},{1,9},{5... | collective-permute-start | bytes 786440 | tf_op jit(solution)/shard_map/ppermute | solution.py:65
  8.9 17.1 %collective-permute-start.2 = (bf16[4,128,256]{2,1,0:T(8,128)(2,1)}, bf16[4,128,256]{2,1,0:T(8,128)(2,1)S(1)}, u32[]{:S(2)}, u32[]{:S(2)}) collective-permute-start(bf16[4,128,256]{2,1,0:T(8,128)(2,1)} %refs_0_), channel_id=1, source_target_pairs={{0,24},{4,28},{8,16},{12,20},{16,8},{20,12},{24,0},{28,4},{1,25},{... | collective-permute-start | bytes 786440 | tf_op jit(solution)/shard_map/ppermute | solution.py:65
  9.1 9.4 %collective-permute-start.5 = (bf16[128,1024]{1,0:T(8,128)(2,1)}, bf16[128,1024]{1,0:T(8,128)(2,1)S(1)}, u32[]{:S(2)}, u32[]{:S(2)}) collective-permute-start(bf16[128,1024]{1,0:T(8,128)(2,1)} %param.12), channel_id=1, source_target_pairs={{0,4},{4,0},{8,12},{12,8},{16,20},{20,16},{24,28},{28,24},{1,5},{5... | collective-permute-start | bytes 786440 | tf_op jit(solution)/shard_map/ppermute | solution.py:37
  11.3 14.7 %collective-permute-start.4 = (bf16[3,352,128]{2,1,0:T(8,128)(2,1)S(1)}, bf16[3,352,128]{2,1,0:T(8,128)(2,1)S(1)}, u32[]{:S(2)}, u32[]{:S(2)}) collective-permute-start(bf16[3,352,128]{2,1,0:T(8,128)(2,1)S(1)} %get-tuple-element.193), channel_id=1, source_target_pairs={{0,4},{4,0},{8,12},{12,8},{16,20},{20,16},{24,28},{28,24},{1,5},{5... | collective-permute-start | bytes 811016 | tf_op jit(solution)/shard_map/ppermute | solution.py:37
  26.1 19.1 %collective-permute-start.10 = (bf16[1,704,128]{2,1,0:T(8,128)(2,1)S(1)}, bf16[1,704,128]{2,1,0:T(8,128)(2,1)S(1)}, u32[]{:S(2)}, u32[]{:S(2)}) collective-permute-start(bf16[1,704,128]{2,1,0:T(8,128)(2,1)S(1)} %slice.101.refs_0_), channel_id=1, source_target_pairs={{0,24},{4,28},{8,16},{12,20},{16,8},{20,12},{24,0},{28,4},{1,25},{... | collective-permute-start | bytes 540680 | tf_op jit(solution)/shard_map/ppermute | solution.py:65
  28.6 21.0 %collective-permute-start.9 = (bf16[1,704,128]{2,1,0:T(8,128)(2,1)S(1)}, bf16[1,704,128]{2,1,0:T(8,128)(2,1)}, u32[]{:S(2)}, u32[]{:S(2)}) collective-permute-start(bf16[1,704,128]{2,1,0:T(8,128)(2,1)S(1)} %slice.101.refs_0_), channel_id=1, source_target_pairs={{0,16},{4,20},{8,24},{12,28},{16,0},{20,4},{24,8},{28,12},{1,17},{... | collective-permute-start | bytes 540680 | tf_op jit(solution)/shard_map/ppermute | solution.py:65
  37.1 12.5 %collective-permute-start.8 = (bf16[1,704,128]{2,1,0:T(8,128)(2,1)S(1)}, bf16[1,704,128]{2,1,0:T(8,128)(2,1)}, u32[]{:S(2)}, u32[]{:S(2)}) collective-permute-start(bf16[1,704,128]{2,1,0:T(8,128)(2,1)S(1)} %slice.101.refs_0_), channel_id=1, source_target_pairs={{0,8},{4,12},{8,0},{12,4},{16,24},{20,28},{24,16},{28,20},{1,9},{5... | collective-permute-start | bytes 540680 | tf_op jit(solution)/shard_map/ppermute | solution.py:65
  40.6 24.8 %collective-permute-start.7 = (bf16[4,512,256]{2,1,0:T(8,128)(2,1)}, bf16[4,512,256]{2,1,0:T(8,128)(2,1)S(1)}, u32[]{:S(2)}, u32[]{:S(2)}) collective-permute-start(bf16[4,512,256]{2,1,0:T(8,128)(2,1)} %join.7.refs_0_.refs_1_), channel_id=1, source_target_pairs={{0,2},{1,3},{2,0},{3,1},{4,6},{5,7},{6,4},{7,5},{8,10},{9,11},{10,... | collective-permute-start | bytes 3145736 | tf_op jit(solution)/shard_map/ppermute | solution.py:83
  42.2 24.5 %collective-permute-start.6 = (bf16[4,512,256]{2,1,0:T(8,128)(2,1)}, bf16[4,512,256]{2,1,0:T(8,128)(2,1)S(1)}, u32[]{:S(2)}, u32[]{:S(2)}) collective-permute-start(bf16[4,512,256]{2,1,0:T(8,128)(2,1)} %join.7.refs_0_.refs_1_), channel_id=1, source_target_pairs={{0,4},{4,0},{8,12},{12,8},{16,20},{20,16},{24,28},{28,24},{1,5},{5... | collective-permute-start | bytes 3145736 | tf_op jit(solution)/shard_map/ppermute | solution.py:37
  49.6 24.8 %collective-permute-start.17 = (bf16[2,704,128]{2,1,0:T(8,128)(2,1)}, bf16[2,704,128]{2,1,0:T(8,128)(2,1)}, u32[]{:S(2)}, u32[]{:S(2)}) collective-permute-start(bf16[2,704,128]{2,1,0:T(8,128)(2,1)} %slice.102.refs_0_), channel_id=1, source_target_pairs={{0,24},{4,28},{8,16},{12,20},{16,8},{20,12},{24,0},{28,4},{1,25},{... | collective-permute-start | bytes 1081352 | tf_op jit(solution)/shard_map/ppermute | solution.py:65
  62.4 19.4 %collective-permute-start.16 = (bf16[2,704,128]{2,1,0:T(8,128)(2,1)}, bf16[2,704,128]{2,1,0:T(8,128)(2,1)}, u32[]{:S(2)}, u32[]{:S(2)}) collective-permute-start(bf16[2,704,128]{2,1,0:T(8,128)(2,1)} %slice.102.refs_0_), channel_id=1, source_target_pairs={{0,16},{4,20},{8,24},{12,28},{16,0},{20,4},{24,8},{28,12},{1,17},{... | collective-permute-start | bytes 1081352 | tf_op jit(solution)/shard_map/ppermute | solution.py:65
  69.2 28.6 %collective-permute-start.14 = (bf16[1,704,512]{2,1,0:T(8,128)(2,1)}, bf16[1,704,512]{2,1,0:T(8,128)(2,1)}, u32[]{:S(2)}, u32[]{:S(2)}) collective-permute-start(bf16[1,704,512]{2,1,0:T(8,128)(2,1)} %join.8.refs_1_), channel_id=1, source_target_pairs={{0,2},{1,3},{2,0},{3,1},{4,6},{5,7},{6,4},{7,5},{8,10},{9,11},{10,... | collective-permute-start | bytes 2162696 | tf_op jit(solution)/shard_map/ppermute | solution.py:83
  69.9 27.9 %collective-permute-start.13 = (bf16[1,704,512]{2,1,0:T(8,128)(2,1)}, bf16[1,704,512]{2,1,0:T(8,128)(2,1)}, u32[]{:S(2)}, u32[]{:S(2)}) collective-permute-start(bf16[1,704,512]{2,1,0:T(8,128)(2,1)} %join.8.refs_1_), channel_id=1, source_target_pairs={{0,4},{4,0},{8,12},{12,8},{16,20},{20,16},{24,28},{28,24},{1,5},{5... | collective-permute-start | bytes 2162696 | tf_op jit(solution)/shard_map/ppermute | solution.py:37
  73.0 24.1 %collective-permute-start.12 = (bf16[4,256,256]{2,1,0:T(8,128)(2,1)}, bf16[4,256,256]{2,1,0:T(8,128)(2,1)}, u32[]{:S(2)}, u32[]{:S(2)}) collective-permute-start(bf16[4,256,256]{2,1,0:T(8,128)(2,1)} %slice.104), channel_id=1, source_target_pairs={{0,2},{1,3},{2,0},{3,1},{4,6},{5,7},{6,4},{7,5},{8,10},{9,11},{10,... | collective-permute-start | bytes 1572872 | tf_op jit(solution)/shard_map/ppermute | solution.py:83
  74.4 23.4 %collective-permute-start.11 = (bf16[4,256,256]{2,1,0:T(8,128)(2,1)}, bf16[4,256,256]{2,1,0:T(8,128)(2,1)}, u32[]{:S(2)}, u32[]{:S(2)}) collective-permute-start(bf16[4,256,256]{2,1,0:T(8,128)(2,1)} %slice.103), channel_id=1, source_target_pairs={{0,4},{4,0},{8,12},{12,8},{16,20},{20,16},{24,28},{28,24},{1,5},{5... | collective-permute-start | bytes 1572872 | tf_op jit(solution)/shard_map/ppermute | solution.py:37
  81.7 14.3 %collective-permute-start.15 = (bf16[2,704,128]{2,1,0:T(8,128)(2,1)}, bf16[2,704,128]{2,1,0:T(8,128)(2,1)}, u32[]{:S(2)}, u32[]{:S(2)}) collective-permute-start(bf16[2,704,128]{2,1,0:T(8,128)(2,1)} %slice.102.refs_0_), channel_id=1, source_target_pairs={{0,8},{4,12},{8,0},{12,4},{16,24},{20,28},{24,16},{28,20},{1,9},{5... | collective-permute-start | bytes 1081352 | tf_op jit(solution)/shard_map/ppermute | solution.py:65
  122.7 39.0 %collective-permute-start.20 = (bf16[2,704,512]{2,1,0:T(8,128)(2,1)}, bf16[2,704,512]{2,1,0:T(8,128)(2,1)S(1)}, u32[]{:S(2)}, u32[]{:S(2)}) collective-permute-start(bf16[2,704,512]{2,1,0:T(8,128)(2,1)} %join.9.refs_3_.refs_1_), channel_id=1, source_target_pairs={{0,2},{1,3},{2,0},{3,1},{4,6},{5,7},{6,4},{7,5},{8,10},{9,11},{10,... | collective-permute-start | bytes 4325384 | tf_op jit(solution)/shard_map/ppermute | solution.py:83
  124.6 37.8 %collective-permute-start.19 = (bf16[2,704,512]{2,1,0:T(8,128)(2,1)}, bf16[2,704,512]{2,1,0:T(8,128)(2,1)}, u32[]{:S(2)}, u32[]{:S(2)}) collective-permute-start(bf16[2,704,512]{2,1,0:T(8,128)(2,1)} %join.9.refs_3_.refs_1_), channel_id=1, source_target_pairs={{0,4},{4,0},{8,12},{12,8},{16,20},{20,16},{24,28},{28,24},{1,5},{5... | collective-permute-start | bytes 4325384 | tf_op jit(solution)/shard_map/ppermute | solution.py:37
  124.6 13.9 %collective-permute-start.23 = (bf16[6,2,128,128]{3,2,1,0:T(8,128)(2,1)S(1)}, bf16[6,2,128,128]{3,2,1,0:T(8,128)(2,1)S(1)}, u32[]{:S(2)}, u32[]{:S(2)}) collective-permute-start(bf16[6,2,128,128]{3,2,1,0:T(8,128)(2,1)S(1)} %copy-done.22), channel_id=1, source_target_pairs={{0,24},{4,28},{8,16},{12,20},{16,8},{20,12},{24,0},{28,4},{1,25},{... | collective-permute-start | bytes 1179656 | tf_op jit(solution)/shard_map/ppermute | solution.py:65
  126.7 34.9 %collective-permute-start.22 = (bf16[6,2,128,128]{3,2,1,0:T(8,128)(2,1)S(1)}, bf16[6,2,128,128]{3,2,1,0:T(8,128)(2,1)S(1)}, u32[]{:S(2)}, u32[]{:S(2)}) collective-permute-start(bf16[6,2,128,128]{3,2,1,0:T(8,128)(2,1)S(1)} %copy-done.22), channel_id=1, source_target_pairs={{0,16},{4,20},{8,24},{12,28},{16,0},{20,4},{24,8},{28,12},{1,17},{... | collective-permute-start | bytes 1179656 | tf_op jit(solution)/shard_map/ppermute | solution.py:65
  127.4 34.2 %collective-permute-start.21 = (bf16[6,2,128,128]{3,2,1,0:T(8,128)(2,1)S(1)}, bf16[6,2,128,128]{3,2,1,0:T(8,128)(2,1)S(1)}, u32[]{:S(2)}, u32[]{:S(2)}) collective-permute-start(bf16[6,2,128,128]{3,2,1,0:T(8,128)(2,1)S(1)} %copy-done.22), channel_id=1, source_target_pairs={{0,8},{4,12},{8,0},{12,4},{16,24},{20,28},{24,16},{28,20},{1,9},{5... | collective-permute-start | bytes 1179656 | tf_op jit(solution)/shard_map/ppermute | solution.py:65
  162.5 38.3 %collective-permute-start.26 = (bf16[2,704,512]{2,1,0:T(8,128)(2,1)}, bf16[2,704,512]{2,1,0:T(8,128)(2,1)}, u32[]{:S(2)}, u32[]{:S(2)}) collective-permute-start(bf16[2,704,512]{2,1,0:T(8,128)(2,1)} %collective-permute-done.19.refs_4_.refs_2_), channel_id=1, source_target_pairs={{0,2},{1,3},{2,0},{3,1},{4,6},{5,7},{6,4},{7,5},{8,10},{9,11},{10,... | collective-permute-start | bytes 4325384 | tf_op jit(solution)/shard_map/ppermute | solution.py:83
  171.5 18.7 %collective-permute-start.18 = (bf16[1,704,512]{2,1,0:T(8,128)(2,1)}, bf16[1,704,512]{2,1,0:T(8,128)(2,1)S(1)}, u32[]{:S(2)}, u32[]{:S(2)}) collective-permute-start(bf16[1,704,512]{2,1,0:T(8,128)(2,1)} %collective-permute-done.14.refs_1_), channel_id=1, source_target_pairs={{0,4},{4,0},{8,12},{12,8},{16,20},{20,16},{24,28},{28,24},{1,5},{5... | collective-permute-start | bytes 2162696 | tf_op jit(solution)/shard_map/ppermute | solution.py:37
  172.3 18.4 %collective-permute-start.32 = (bf16[2,128,256]{2,1,0:T(8,128)(2,1)}, bf16[2,128,256]{2,1,0:T(8,128)(2,1)S(1)}, u32[]{:S(2)}, u32[]{:S(2)}) collective-permute-start(bf16[2,128,256]{2,1,0:T(8,128)(2,1)} %refs_0_.1), channel_id=1, source_target_pairs={{0,24},{4,28},{8,16},{12,20},{16,8},{20,12},{24,0},{28,4},{1,25},{... | collective-permute-start | bytes 393224 | tf_op jit(solution)/shard_map/ppermute | solution.py:65
  174.6 25.5 %collective-permute-start.31 = (bf16[2,128,256]{2,1,0:T(8,128)(2,1)}, bf16[2,128,256]{2,1,0:T(8,128)(2,1)S(1)}, u32[]{:S(2)}, u32[]{:S(2)}) collective-permute-start(bf16[2,128,256]{2,1,0:T(8,128)(2,1)} %refs_0_.1), channel_id=1, source_target_pairs={{0,16},{4,20},{8,24},{12,28},{16,0},{20,4},{24,8},{28,12},{1,17},{... | collective-permute-start | bytes 393224 | tf_op jit(solution)/shard_map/ppermute | solution.py:65
  174.6 25.5 %collective-permute-start.30 = (bf16[2,128,256]{2,1,0:T(8,128)(2,1)}, bf16[2,128,256]{2,1,0:T(8,128)(2,1)S(1)}, u32[]{:S(2)}, u32[]{:S(2)}) collective-permute-start(bf16[2,128,256]{2,1,0:T(8,128)(2,1)} %refs_0_.1), channel_id=1, source_target_pairs={{0,8},{4,12},{8,0},{12,4},{16,24},{20,28},{24,16},{28,20},{1,9},{5... | collective-permute-start | bytes 393224 | tf_op jit(solution)/shard_map/ppermute | solution.py:65
  190.3 9.9 %collective-permute-start.29 = (bf16[64,1024]{1,0:T(8,128)(2,1)S(1)}, bf16[64,1024]{1,0:T(8,128)(2,1)S(1)}, u32[]{:S(2)}, u32[]{:S(2)}) collective-permute-start(bf16[64,1024]{1,0:T(8,128)(2,1)S(1)} %get-tuple-element.141), channel_id=1, source_target_pairs={{0,2},{1,3},{2,0},{3,1},{4,6},{5,7},{6,4},{7,5},{8,10},{9,11},{10,... | collective-permute-start | bytes 393224 | tf_op jit(solution)/shard_map/ppermute | solution.py:83
  191.3 8.8 %collective-permute-start.28 = (bf16[64,1024]{1,0:T(8,128)(2,1)S(1)}, bf16[64,1024]{1,0:T(8,128)(2,1)S(1)}, u32[]{:S(2)}, u32[]{:S(2)}) collective-permute-start(bf16[64,1024]{1,0:T(8,128)(2,1)S(1)} %get-tuple-element.139), channel_id=1, source_target_pairs={{0,4},{4,0},{8,12},{12,8},{16,20},{20,16},{24,28},{28,24},{1,5},{5... | collective-permute-start | bytes 393224 | tf_op jit(solution)/shard_map/ppermute | solution.py:37
  203.5 16.7 %collective-permute-start.36 = (bf16[2,512,256]{2,1,0:T(8,128)(2,1)}, bf16[2,512,256]{2,1,0:T(8,128)(2,1)S(1)}, u32[]{:S(2)}, u32[]{:S(2)}) collective-permute-start(bf16[2,512,256]{2,1,0:T(8,128)(2,1)} %join.11.refs_3_), channel_id=1, source_target_pairs={{0,2},{1,3},{2,0},{3,1},{4,6},{5,7},{6,4},{7,5},{8,10},{9,11},{10,... | collective-permute-start | bytes 1572872 | tf_op jit(solution)/shard_map/ppermute | solution.py:83
  204.5 15.7 %collective-permute-start.35 = (bf16[2,512,256]{2,1,0:T(8,128)(2,1)}, bf16[2,512,256]{2,1,0:T(8,128)(2,1)S(1)}, u32[]{:S(2)}, u32[]{:S(2)}) collective-permute-start(bf16[2,512,256]{2,1,0:T(8,128)(2,1)} %join.11.refs_3_), channel_id=1, source_target_pairs={{0,4},{4,0},{8,12},{12,8},{16,20},{20,16},{24,28},{28,24},{1,5},{5... | collective-permute-start | bytes 1572872 | tf_op jit(solution)/shard_map/ppermute | solution.py:37
  206.7 12.8 %collective-permute-start.33 = (bf16[64,1024]{1,0:T(8,128)(2,1)S(1)}, bf16[64,1024]{1,0:T(8,128)(2,1)S(1)}, u32[]{:S(2)}, u32[]{:S(2)}) collective-permute-start(bf16[64,1024]{1,0:T(8,128)(2,1)S(1)} %add_convert_fusion.6), channel_id=1, source_target_pairs={{0,2},{1,3},{2,0},{3,1},{4,6},{5,7},{6,4},{7,5},{8,10},{9,11},{10,... | collective-permute-start | bytes 393224 | tf_op jit(solution)/shard_map/ppermute | solution.py:83
  208.1 12.1 %collective-permute-start.34 = (bf16[64,1024]{1,0:T(8,128)(2,1)S(1)}, bf16[64,1024]{1,0:T(8,128)(2,1)S(1)}, u32[]{:S(2)}, u32[]{:S(2)}) collective-permute-start(bf16[64,1024]{1,0:T(8,128)(2,1)S(1)} %add_convert_fusion.5), channel_id=1, source_target_pairs={{0,4},{4,0},{8,12},{12,8},{16,20},{20,16},{24,28},{28,24},{1,5},{5... | collective-permute-start | bytes 393224 | tf_op jit(solution)/shard_map/ppermute | solution.py:37
  221.9 14.1 %collective-permute-start.42 = (bf16[2,256,256]{2,1,0:T(8,128)(2,1)S(1)}, bf16[2,256,256]{2,1,0:T(8,128)(2,1)S(1)}, u32[]{:S(2)}, u32[]{:S(2)}) collective-permute-start(bf16[2,256,256]{2,1,0:T(8,128)(2,1)S(1)} %slice.113), channel_id=1, source_target_pairs={{0,2},{1,3},{2,0},{3,1},{4,6},{5,7},{6,4},{7,5},{8,10},{9,11},{10,... | collective-permute-start | bytes 786440 | tf_op jit(solution)/shard_map/ppermute | solution.py:83
  223.0 12.9 %collective-permute-start.41 = (bf16[2,256,256]{2,1,0:T(8,128)(2,1)S(1)}, bf16[2,256,256]{2,1,0:T(8,128)(2,1)S(1)}, u32[]{:S(2)}, u32[]{:S(2)}) collective-permute-start(bf16[2,256,256]{2,1,0:T(8,128)(2,1)S(1)} %slice.112), channel_id=1, source_target_pairs={{0,4},{4,0},{8,12},{12,8},{16,20},{20,16},{24,28},{28,24},{1,5},{5... | collective-permute-start | bytes 786440 | tf_op jit(solution)/shard_map/ppermute | solution.py:37
  224.1 11.8 %collective-permute-start.40 = (bf16[256,128]{1,0:T(8,128)(2,1)S(1)}, bf16[256,128]{1,0:T(8,128)(2,1)S(1)}, u32[]{:S(2)}, u32[]{:S(2)}) collective-permute-start(bf16[256,128]{1,0:T(8,128)(2,1)S(1)} %convolution_convert_fusion.1.refs_0_), channel_id=1, source_target_pairs={{0,24},{4,28},{8,16},{12,20},{16,8},{20,12},{24,0},{28,4},{1,25},{... | collective-permute-start | bytes 196616 | tf_op jit(solution)/shard_map/ppermute | solution.py:65
  226.4 9.6 %collective-permute-start.39 = (bf16[256,128]{1,0:T(8,128)(2,1)S(1)}, bf16[256,128]{1,0:T(8,128)(2,1)S(1)}, u32[]{:S(2)}, u32[]{:S(2)}) collective-permute-start(bf16[256,128]{1,0:T(8,128)(2,1)S(1)} %convolution_convert_fusion.1.refs_0_), channel_id=1, source_target_pairs={{0,16},{4,20},{8,24},{12,28},{16,0},{20,4},{24,8},{28,12},{1,17},{... | collective-permute-start | bytes 196616 | tf_op jit(solution)/shard_map/ppermute | solution.py:65
  226.4 9.6 %collective-permute-start.38 = (bf16[256,128]{1,0:T(8,128)(2,1)S(1)}, bf16[256,128]{1,0:T(8,128)(2,1)S(1)}, u32[]{:S(2)}, u32[]{:S(2)}) collective-permute-start(bf16[256,128]{1,0:T(8,128)(2,1)S(1)} %convolution_convert_fusion.1.refs_0_), channel_id=1, source_target_pairs={{0,8},{4,12},{8,0},{12,4},{16,24},{20,28},{24,16},{28,20},{1,9},{5... | collective-permute-start | bytes 196616 | tf_op jit(solution)/shard_map/ppermute | solution.py:65
  244.7 53.7 %collective-permute-start.48 = (bf16[576,1024]{1,0:T(8,128)(2,1)}, bf16[576,1024]{1,0:T(8,128)(2,1)}, u32[]{:S(2)}, u32[]{:S(2)}) collective-permute-start(bf16[576,1024]{1,0:T(8,128)(2,1)} %fusion.1), channel_id=1, source_target_pairs={{0,1},{1,0},{2,3},{3,2},{4,5},{5,4},{6,7},{7,6},{8,9},{9,8},{10,11... | collective-permute-start | bytes 3538952 | tf_op jit(solution)/shard_map/ppermute | solution.py:42
  244.8 17.1 %collective-permute-start.51 = (bf16[6,352,128]{2,1,0:T(8,128)(2,1)S(1)}, bf16[6,352,128]{2,1,0:T(8,128)(2,1)}, u32[]{:S(2)}, u32[]{:S(2)}) collective-permute-start(bf16[6,352,128]{2,1,0:T(8,128)(2,1)S(1)} %bitcast.116), channel_id=1, source_target_pairs={{0,24},{4,28},{8,16},{12,20},{16,8},{20,12},{24,0},{28,4},{1,25},{... | collective-permute-start | bytes 1622024 | tf_op jit(solution)/shard_map/ppermute | solution.py:65
  248.8 8.6 %collective-permute-start.44 = (bf16[1024,128]{1,0:T(8,128)(2,1)}, bf16[1024,128]{1,0:T(8,128)(2,1)S(1)}, u32[]{:S(2)}, u32[]{:S(2)}) collective-permute-start(bf16[1024,128]{1,0:T(8,128)(2,1)} %join.12), channel_id=1, source_target_pairs={{0,2},{1,3},{2,0},{3,1},{4,6},{5,7},{6,4},{7,5},{8,10},{9,11},{10,... | collective-permute-start | bytes 786440 | tf_op jit(solution)/shard_map/ppermute | solution.py:83
  249.8 8.2 %collective-permute-start.43 = (bf16[1024,128]{1,0:T(8,128)(2,1)}, bf16[1024,128]{1,0:T(8,128)(2,1)S(1)}, u32[]{:S(2)}, u32[]{:S(2)}) collective-permute-start(bf16[1024,128]{1,0:T(8,128)(2,1)} %join.12), channel_id=1, source_target_pairs={{0,4},{4,0},{8,12},{12,8},{16,20},{20,16},{24,28},{28,24},{1,5},{5... | collective-permute-start | bytes 786440 | tf_op jit(solution)/shard_map/ppermute | solution.py:37
  251.2 42.4 %collective-permute-start.50 = (bf16[6,352,128]{2,1,0:T(8,128)(2,1)S(1)}, bf16[6,352,128]{2,1,0:T(8,128)(2,1)S(1)}, u32[]{:S(2)}, u32[]{:S(2)}) collective-permute-start(bf16[6,352,128]{2,1,0:T(8,128)(2,1)S(1)} %bitcast.117), channel_id=1, source_target_pairs={{0,16},{4,20},{8,24},{12,28},{16,0},{20,4},{24,8},{28,12},{1,17},{... | collective-permute-start | bytes 1622024 | tf_op jit(solution)/shard_map/ppermute | solution.py:65
  257.3 37.1 %collective-permute-start.49 = (bf16[6,352,128]{2,1,0:T(8,128)(2,1)S(1)}, bf16[6,352,128]{2,1,0:T(8,128)(2,1)}, u32[]{:S(2)}, u32[]{:S(2)}) collective-permute-start(bf16[6,352,128]{2,1,0:T(8,128)(2,1)S(1)} %bitcast.118), channel_id=1, source_target_pairs={{0,8},{4,12},{8,0},{12,4},{16,24},{20,28},{24,16},{28,20},{1,9},{5... | collective-permute-start | bytes 1622024 | tf_op jit(solution)/shard_map/ppermute | solution.py:65
  258.0 39.4 %collective-permute-start.45 = (bf16[512,128]{1,0:T(8,128)(2,1)S(1)}, bf16[512,128]{1,0:T(8,128)(2,1)}, u32[]{:S(2)}, u32[]{:S(2)}) collective-permute-start(bf16[512,128]{1,0:T(8,128)(2,1)S(1)} %slice.136), channel_id=1, source_target_pairs={{0,4},{4,0},{8,12},{12,8},{16,20},{20,16},{24,28},{28,24},{1,5},{5... | collective-permute-start | bytes 393224 | tf_op jit(solution)/shard_map/ppermute | solution.py:37
  262.0 35.4 %collective-permute-start.46 = (bf16[512,128]{1,0:T(8,128)(2,1)S(1)}, bf16[512,128]{1,0:T(8,128)(2,1)}, u32[]{:S(2)}, u32[]{:S(2)}) collective-permute-start(bf16[512,128]{1,0:T(8,128)(2,1)S(1)} %slice.137), channel_id=1, source_target_pairs={{0,2},{1,3},{2,0},{3,1},{4,6},{5,7},{6,4},{7,5},{8,10},{9,11},{10,... | collective-permute-start | bytes 393224 | tf_op jit(solution)/shard_map/ppermute | solution.py:83
  308.0 9.4 %collective-permute-start.53 = (bf16[4,272,128]{2,1,0:T(8,128)(2,1)S(1)}, bf16[4,272,128]{2,1,0:T(8,128)(2,1)S(1)}, u32[]{:S(2)}, u32[]{:S(2)}) collective-permute-start(bf16[4,272,128]{2,1,0:T(8,128)(2,1)S(1)} %get-tuple-element.192), channel_id=1, source_target_pairs={{0,2},{1,3},{2,0},{3,1},{4,6},{5,7},{6,4},{7,5},{8,10},{9,11},{10,... | collective-permute-start | bytes 835592 | tf_op jit(solution)/shard_map/ppermute | solution.py:83
  (70 other events, 578.3 us)
